TPU v7x, 32 devices: a whole 2x2x4 slice. The times are simulated.
32 devices in a mesh: heads: 4 (over y, x), seq: 8 (over z, core).
Axes of the slice: x: 2, y: 2, z: 4, core: 2. Of those that a mesh axis runs over, the one named last changes fastest.
Arguments:
- query_rows: bfloat16 [4096, 8, 128], P('seq', 'heads'), may hold values from -16 to 16
- key_rows: bfloat16 [4096, 8, 128], P('seq', 'heads'), may hold values from -5 to 5
- value_rows: bfloat16 [4096, 8, 128], P('seq', 'heads'), may hold values from -40 to 40
- level_pick: int32 [4096], P('seq'), may hold values from 0 to 7
- level_table: float32 [8, 8, 13], P(None, 'heads'), may hold values from 0 to 3, as said below
- norm_gain: float32 [8, 128], P('heads'), may hold values from 0.5 to 1.5
- out_grad: bfloat16 [4096, 8, 128], P('seq', 'heads'), may hold values from -6 to 6
Outputs:
- normed: float32 [4096, 8, 128], P('seq', 'heads')
- query_grad: float32 [4096, 8, 128], P('seq', 'heads')
- key_grad: float32 [4096, 8, 128], P('seq', 'heads')
- value_grad: float32 [4096, 8, 128], P('seq', 'heads')
Inputs may be any that keep to these rules, and one draw needn't show every extreme that they name: `level_table`: positive weights.
All inputs are finite; a program needn't handle non-finite values.
Results may differ from a plain program's by a relative error of at most 0.007.
Values sent between devices are 32-bit elements; how exact they have to be, the bound alone decides.
No kernel may reach another device: no remote copies, remote signals or barrier semaphores. Data moves between devices by JAX's collectives and lax.ppermute only.
A program may use at most 64 MiB of HBM per device.

v0:
```python
import jax
import jax.numpy as jnp
from jax import lax
from jax.sharding import PartitionSpec as P

exact_mode = lax.Precision.HIGHEST
epsilon = 1e-06


def swapped(block, axis, distance):
    count = lax.axis_size(axis)
    route = []
    for low in range(count):
        high = low | 1 << distance
        if high != low and high < count:
            route += [(low, high), (high, low)]
    return lax.ppermute(block, axis, route)


def bit_length(value, bits):
    result = jnp.zeros(value.shape, jnp.int32)
    for place in range(bits):
        result = result + (value >> place > 0).astype(jnp.int32)
    return result


def level_weights(token_weights, row_position, column_position, local_bits):
    level = bit_length(row_position[:, None] ^ column_position[None, :], local_bits)
    causal = column_position[None, :] <= row_position[:, None]
    weight = jnp.zeros(
        (token_weights.shape[1], row_position.shape[0], column_position.shape[0]), jnp.float32
    )
    for level_no in range(local_bits + 1):
        chosen = jnp.logical_and(level == level_no, causal)
        weight = weight + jnp.where(
            chosen[None], jnp.transpose(token_weights[:, :, level_no])[:, :, None], 0.0
        )
    return weight


def local_forward(query_block, key_block, value_block, token_weights, local_bits, scale):
    length = query_block.shape[0]
    tile = min(512, length)
    weight = level_weights(
        token_weights,
        jnp.arange(0, tile, dtype=jnp.int32),
        jnp.arange(tile, dtype=jnp.int32),
        local_bits,
    )
    scores = jnp.einsum("thd,shd->hts", query_block, key_block, preferred_element_type=jnp.float32)
    probs = (scores * scale * weight).astype(jnp.bfloat16)
    pieces = jnp.einsum("hts,shd->thd", probs, value_block, preferred_element_type=jnp.float32)
    return pieces


def local_backward(
    query_block, key_block, value_block, grad_block, token_weights, local_bits, scale
):
    length, heads, width = query_block.shape
    tile = min(512, length)
    key_part = jnp.zeros((length, heads, width), jnp.float32)
    value_part = jnp.zeros((length, heads, width), jnp.float32)
    weight = level_weights(
        token_weights,
        jnp.arange(0, tile, dtype=jnp.int32),
        jnp.arange(tile, dtype=jnp.int32),
        local_bits,
    )
    scores = jnp.einsum("thd,shd->hts", query_block, key_block, preferred_element_type=jnp.float32)
    probs = (scores * scale * weight).astype(jnp.bfloat16)
    dprob = jnp.einsum("the,she->hts", grad_block, value_block, preferred_element_type=jnp.float32)
    weighted = (dprob * scale * weight).astype(jnp.bfloat16)
    query_pieces = jnp.einsum(
        "hts,shd->thd", weighted, key_block, preferred_element_type=jnp.float32
    )
    key_part = key_part.at[:tile].add(
        jnp.einsum("hts,thd->shd", weighted, query_block, preferred_element_type=jnp.float32)
    )
    value_part = value_part.at[:tile].add(
        jnp.einsum("hts,the->she", probs, grad_block, preferred_element_type=jnp.float32)
    )
    return (query_pieces, key_part, value_part)


def shards(query_rows, key_rows, value_rows, level_pick, level_table, norm_gain, out_grad):
    length, heads_dev, width = query_rows.shape
    local_bits = length.bit_length() - 1
    seq_bits = lax.axis_size("seq").bit_length() - 1
    scale = width ** (-0.5)
    position = lax.axis_index("seq")
    groups = level_table.shape[0]
    one_hot = (level_pick[:, None] == jnp.arange(groups, dtype=jnp.int32)[None, :]).astype(
        jnp.float32
    )
    token_weights = jnp.einsum("tg,ghl->thl", one_hot, level_table, precision=exact_mode)
    upper = jnp.moveaxis(token_weights[:, :, local_bits + 1 :], 2, 0)
    flags = (position >> jnp.arange(seq_bits, dtype=jnp.int32) & 1).astype(jnp.float32)
    inner = local_forward(query_rows, key_rows, value_rows, token_weights, local_bits, scale)
    own_state = jnp.einsum("shd,she->hde", key_rows, value_rows, preferred_element_type=jnp.float32)
    block_sum = own_state
    received = []
    for bit_place in range(seq_bits):
        partner = swapped(block_sum, "seq", bit_place)
        received.append(partner)
        block_sum = block_sum + partner
    states = jnp.stack(received) * flags[:, None, None, None]
    held = states.astype(jnp.bfloat16)
    cross = jnp.einsum("thd,jhde->jthe", query_rows, held, preferred_element_type=jnp.float32)
    attn = inner + scale * jnp.sum(upper[..., None] * cross, axis=0)
    features = heads_dev * width * lax.axis_size("heads")
    total_squares = lax.psum(jnp.sum(attn * attn, axis=(1, 2)), "heads")
    inverse_rms = lax.rsqrt(total_squares / features + epsilon)
    normed = attn * inverse_rms[:, None, None] * norm_gain[None]
    gain_grad = out_grad.astype(jnp.float32) * norm_gain[None]
    projection = lax.psum(jnp.sum(gain_grad * attn, axis=(1, 2)), "heads") / features
    attn_grad = (
        inverse_rms[:, None, None] * gain_grad
        - attn * (inverse_rms**3)[:, None, None] * projection[:, None, None]
    ).astype(jnp.bfloat16)
    query_part, key_part, value_part = local_backward(
        query_rows, key_rows, value_rows, attn_grad, token_weights, local_bits, scale
    )
    cross_back = jnp.einsum("the,jhde->jthd", attn_grad, held, preferred_element_type=jnp.float32)
    query_grad = query_part + scale * jnp.sum(upper[..., None] * cross_back, axis=0)
    scaled = (scale * upper[..., None] * attn_grad.astype(jnp.float32)[None]).astype(jnp.bfloat16)
    grads = (
        jnp.einsum("thd,jthe->jhde", query_rows, scaled, preferred_element_type=jnp.float32)
        * flags[:, None, None, None]
    )
    back = jnp.zeros((heads_dev, width, width), jnp.float32)
    pending = grads
    for bit_place in range(seq_bits):
        partner = swapped(pending[bit_place:], "seq", bit_place)
        back = back + (1.0 - flags[bit_place]) * partner[0]
        pending = pending.at[bit_place + 1 :].add(partner[1:])
    back_held = back.astype(jnp.bfloat16)
    key_grad = key_part + jnp.einsum(
        "she,hde->shd", value_rows, back_held, preferred_element_type=jnp.float32
    )
    value_grad = value_part + jnp.einsum(
        "shd,hde->she", key_rows, back_held, preferred_element_type=jnp.float32
    )
    return (normed, query_grad, key_grad, value_grad)


def solution(mesh):
    in_specs = (
        P("seq", "heads", None),
        P("seq", "heads", None),
        P("seq", "heads", None),
        P("seq"),
        P(None, "heads", None),
        P("heads", None),
        P("seq", "heads", None),
    )
    out_specs = (
        P("seq", "heads", None),
        P("seq", "heads", None),
        P("seq", "heads", None),
        P("seq", "heads", None),
    )
    return jax.shard_map(shards, mesh=mesh, in_specs=in_specs, out_specs=out_specs, check_vma=False)
```

profile of v0, /device:TPU:0, one launch (start us, length us, event | category | flops | bytes accessed | tf_op | source)
XLA Modules:
  0.0 72.5 jit_solution(4098529114067647856)
XLA Ops:
  0.6 1.3 %fusion.30 = f32[2,128,128]{2,1,0:T(8,128)S(1)} fusion(bf16[512,2,128]{2,1,0:T(2,128)(2,1)} %param.21, bf16[512,2,128]{2,1,0:T(2,128)(2,1)} %param.20), kind=kOutput, calls=%fused_computation.61 | convolution fusion | flops 33554432 | bytes 655360 | tf_op jit(solution)/shard_map/shd,she->hde/dot_general | solution.py:99
  2.0 0.5 collective-permute-start
  2.5 1.0 %fusion.7 = (pred[512,512]{1,0:T(8,128)(4,1)S(1)}, pred[512,512]{1,0:T(8,128)(4,1)S(1)}) fusion(), kind=kLoop, calls=%fused_computation.20 | loop fusion | flops 10747904 | bytes 524288 | tf_op jit(solution)/shard_map/and | solution.py:34
  3.5 1.0 %fusion.9 = (pred[512,512]{1,0:T(8,128)(4,1)S(1)}, pred[512,512]{1,0:T(8,128)(4,1)S(1)}) fusion(), kind=kLoop, calls=%fused_computation.22 | loop fusion | flops 10747904 | bytes 524288 | tf_op jit(solution)/shard_map/and | solution.py:34
  4.6 1.8 %fusion.11 = (pred[512,512]{1,0:T(8,128)(4,1)}, pred[512,512]{1,0:T(8,128)(4,1)}) fusion(), kind=kLoop, calls=%fused_computation.24 | loop fusion | flops 10747904 | bytes 524288 | tf_op jit(solution)/shard_map/and | solution.py:34
  6.4 1.8 %fusion.13 = (pred[512,512]{1,0:T(8,128)(4,1)}, pred[512,512]{1,0:T(8,128)(4,1)}) fusion(), kind=kLoop, calls=%fused_computation.26 | loop fusion | flops 10747904 | bytes 524288 | tf_op jit(solution)/shard_map/and | solution.py:34
  8.2 1.8 %fusion.15 = (pred[512,512]{1,0:T(8,128)(4,1)}, pred[512,512]{1,0:T(8,128)(4,1)}) fusion(), kind=kLoop, calls=%fused_computation.28 | loop fusion | flops 10747904 | bytes 524288 | tf_op jit(solution)/shard_map/and | solution.py:34
  10.0 0.2 fusion.41
  10.4 4.9 %multiply_convert_fusion.1 = bf16[2,512,512]{2,1,0:T(8,128)(2,1)S(1)} fusion(bf16[512,2,128]{2,1,0:T(2,128)(2,1)S(1)} %copy-done.4, bf16[512,2,128]{2,1,0:T(2,128)(2,1)S(1)} %copy-done.1, f32[2,512]{1,0:T(2,128)S(1)} %get-tuple-element.95, pred[512,512]{1,0:T(8,128)(4,1)S(1)} %get-tuple-element.105, f32[2,512]{1,0:T(2,128)S(1)} %get-tuple-element.96, ...), kind=kOutput, calls=%fused_computation.1 | convolution fusion | flops 145752064 | bytes 4235264 | tf_op jit(solution)/shard_map/thd,shd->hts/dot_general | solution.py:50
  15.3 0.2 copy.19
  15.5 0.7 fusion.47
  18.2 2.7 %collective-permute-start.1 = (f32[2,128,128]{2,1,0:T(8,128)S(1)}, f32[2,128,128]{2,1,0:T(8,128)S(1)}, u32[]{:S(2)}, u32[]{:S(2)}) collective-permute-start(f32[2,128,128]{2,1,0:T(8,128)S(1)} %add.544), channel_id=1, source_target_pairs={{0,2},{2,0},{1,3},{3,1},{4,6},{6,4},{5,7},{7,5},{8,10},{10,8},{9,1... | collective-permute-start | bytes 393224 | tf_op jit(solution)/shard_map/ppermute | solution.py:17
  20.9 4.1 %collective-permute-done.1 = f32[2,128,128]{2,1,0:T(8,128)S(1)} collective-permute-done((f32[2,128,128]{2,1,0:T(8,128)S(1)}, f32[2,128,128]{2,1,0:T(8,128)S(1)}, u32[]{:S(2)}, u32[]{:S(2)}) %collective-permute-start.1) | collective-permute-done | bytes 131104 | tf_op jit(solution)/shard_map/ppermute | solution.py:17
  25.0 2.8 %collective-permute-start.2 = (f32[2,128,128]{2,1,0:T(8,128)S(1)}, f32[2,128,128]{2,1,0:T(8,128)S(1)}, u32[]{:S(2)}, u32[]{:S(2)}) collective-permute-start(f32[2,128,128]{2,1,0:T(8,128)S(1)} %add.545), channel_id=1, source_target_pairs={{0,4},{4,0},{1,5},{5,1},{2,6},{6,2},{3,7},{7,3},{8,12},{12,8},{9,1... | collective-permute-start | bytes 393224 | tf_op jit(solution)/shard_map/ppermute | solution.py:17
  27.9 6.3 %collective-permute-done.2 = f32[2,128,128]{2,1,0:T(8,128)S(1)} collective-permute-done((f32[2,128,128]{2,1,0:T(8,128)S(1)}, f32[2,128,128]{2,1,0:T(8,128)S(1)}, u32[]{:S(2)}, u32[]{:S(2)}) %collective-permute-start.2) | collective-permute-done | bytes 131104 | tf_op jit(solution)/shard_map/ppermute | solution.py:17
  34.1 0.1 fusion.19
  34.3 0.7 copy-done.21
  34.9 0.4 fusion.1
  35.4 0.5 multiply_reduce_fusion
  35.9 10.0 %all-reduce = (f32[512]{0:T(512)S(1)}, f32[512]{0:T(512)S(1)}) all-reduce(f32[512]{0:T(512)S(1)} %get-tuple-element.73, f32[512]{0:T(512)S(1)} %get-tuple-element.72), channel_id=1, replica_groups=mesh['heads'=4,'seq'=8] {'heads'}, use_global_device_ids=true, to_apply=%region_2.3 | all-reduce | flops 1024 | bytes 8192 | tf_op jit(solution)/shard_map/psum | solution.py:111
  46.0 0.2 fusion.45
  46.3 0.4 fusion.6
  46.7 0.2 copy-done.15
  46.9 0.1 copy-done.16
  47.0 0.1 copy-done.17
  47.1 0.1 copy-done.18
  47.2 0.1 copy-done.8
  47.3 0.1 copy-done.10
  47.4 0.1 copy-done.12
  47.5 0.1 copy-done.13
  47.5 0.1 copy-done.14
  47.6 3.6 %multiply_convert_fusion = bf16[2,512,512]{2,1,0:T(8,128)(2,1)S(1)} fusion(bf16[512,2,128]{0,2,1:T(8,128)(2,1)S(1)} %get-tuple-element.77, bf16[512,2,128]{2,1,0:T(2,128)(2,1)S(1)} %copy-done.2, f32[2,512]{1,0:T(2,128)S(1)} %get-tuple-element.95, pred[512,512]{1,0:T(8,128)(4,1)S(1)} %get-tuple-element.105, f32[2,512]{1,0:T(2,128)S(1)} %get-tuple-element.96, ...), kind=kOutput, calls=%fused_computation | convolution fusion | flops 145752064 | bytes 4235264 | tf_op jit(solution)/shard_map/the,she->hts/dot_general | solution.py:71
  51.3 0.4 fusion
  51.6 0.5 fusion.2
  52.2 0.7 %collective-permute-start.4 = (f32[2,2,128,128]{2,3,0,1:T(8,128)S(1)}, f32[2,2,128,128]{2,3,0,1:T(8,128)S(1)}, u32[]{:S(2)}, u32[]{:S(2)}) collective-permute-start(f32[2,2,128,128]{2,3,0,1:T(8,128)S(1)} %slice_add_fusion), channel_id=1, source_target_pairs={{0,2},{2,0},{1,3},{3,1},{4,6},{6,4},{5,7},{7,5},{8,10},{10,8},{9,1... | collective-permute-start | bytes 786440 | tf_op jit(solution)/shard_map/ppermute | solution.py:17
  53.0 0.3 fusion.48
  53.3 6.9 %collective-permute-done.4 = f32[2,2,128,128]{2,3,0,1:T(8,128)S(1)} collective-permute-done((f32[2,2,128,128]{2,3,0,1:T(8,128)S(1)}, f32[2,2,128,128]{2,3,0,1:T(8,128)S(1)}, u32[]{:S(2)}, u32[]{:S(2)}) %collective-permute-start.4) | collective-permute-done | bytes 262176 | tf_op jit(solution)/shard_map/ppermute | solution.py:17
  60.2 0.7 copy-done.19
  60.9 2.3 %collective-permute-start.5 = (f32[1,2,128,128]{2,3,0,1:T(8,128)S(1)}, f32[1,2,128,128]{2,3,0,1:T(8,128)S(1)}, u32[]{:S(2)}, u32[]{:S(2)}) collective-permute-start(f32[1,2,128,128]{2,3,0,1:T(8,128)S(1)} %slice_add_fusion.1), channel_id=1, source_target_pairs={{0,4},{4,0},{1,5},{5,1},{2,6},{6,2},{3,7},{7,3},{8,12},{12,8},{9,1... | collective-permute-start | bytes 393224 | tf_op jit(solution)/shard_map/ppermute | solution.py:17
  63.3 0.5 convolution_bitcast_fusion.1
  63.8 1.0 %copy.34 = f32[512,2,128]{2,1,0:T(2,128)} copy(f32[512,2,128]{0,2,1:T(8,128)S(1)} %fusion.2) | data formatting | bytes 1048576
  64.8 1.0 %copy.33 = f32[512,2,128]{2,1,0:T(2,128)} copy(f32[512,2,128]{0,2,1:T(8,128)S(1)} %get-tuple-element.78) | data formatting | bytes 1048576
  65.8 3.1 %collective-permute-done.5 = f32[1,2,128,128]{2,3,0,1:T(8,128)S(1)} collective-permute-done((f32[1,2,128,128]{2,3,0,1:T(8,128)S(1)}, f32[1,2,128,128]{2,3,0,1:T(8,128)S(1)}, u32[]{:S(2)}, u32[]{:S(2)}) %collective-permute-start.5) | collective-permute-done | bytes 131104 | tf_op jit(solution)/shard_map/ppermute | solution.py:17
  68.9 0.9 %fusion.39 = bf16[2,128,128]{1,2,0:T(8,128)(2,1)S(1)} fusion(f32[1,2,128,128]{2,3,0,1:T(8,128)S(1)} %collective-permute-done.5, f32[2,2,128,128]{2,3,0,1:T(8,128)S(1)} %copy-done.20, f32[3,2,128,128]{2,3,0,1:T(8,128)} %copy-done.3, f32[]{:T(128)} %bitcast.26, f32[]{:T(128)} %bitcast.25, f32[]{:T(128)} %bitcast.22), kind=kLoop, calls=%fused_computation.73 | loop fusion | flops 196608 | bytes 458764 | tf_op jit(solution)/shard_map/convert_element_type | solution.py:136
  69.8 0.2 fusion.5
  70.1 1.0 %copy.36 = f32[512,2,128]{2,1,0:T(2,128)} copy(f32[512,2,128]{0,2,1:T(8,128)S(1)} %fusion.5) | data formatting | bytes 1048576
  71.1 0.2 fusion.4
  71.3 1.2 %copy.35 = f32[512,2,128]{2,1,0:T(2,128)} copy(f32[512,2,128]{2,0,1:T(8,128)S(1)} %fusion.4) | data formatting | bytes 1048576
  (57 shorter events, 0.4 us)
Async XLA Ops:
  0.6 9.4 %copy-start = (f32[8,2,13]{2,1,0:T(2,128)S(1)}, f32[8,2,13]{2,1,0:T(2,128)}, u32[]{:S(2)}) copy-start(f32[8,2,13]{2,1,0:T(2,128)} %param.23) | copy-start | bytes 2500
  2.0 16.2 %collective-permute-start = (f32[2,128,128]{2,1,0:T(8,128)S(1)}, f32[2,128,128]{2,1,0:T(8,128)S(1)}, u32[]{:S(2)}, u32[]{:S(2)}) collective-permute-start(f32[2,128,128]{2,1,0:T(8,128)S(1)} %fusion.30), channel_id=1, source_target_pairs={{0,1},{1,0},{2,3},{3,2},{4,5},{5,4},{6,7},{7,6},{8,9},{9,8},{10,11... | collective-permute-start | bytes 393224 | tf_op jit(solution)/shard_map/ppermute | solution.py:17
  3.5 6.9 %copy-start.7 = (pred[512,512]{1,0:T(8,128)(4,1)}, pred[512,512]{1,0:T(8,128)(4,1)S(1)}, u32[]{:S(2)}) copy-start(pred[512,512]{1,0:T(8,128)(4,1)S(1)} %get-tuple-element.106) | copy-start | bytes 786436
  3.5 6.5 %copy-start.24 = (s32[512]{0:T(512)S(1)}, s32[512]{0:T(512)}, u32[]{:S(2)}) copy-start(s32[512]{0:T(512)} %param.22) | copy-start | bytes 6148
  4.5 10.8 %copy-start.9 = (pred[512,512]{1,0:T(8,128)(4,1)}, pred[512,512]{1,0:T(8,128)(4,1)S(1)}, u32[]{:S(2)}) copy-start(pred[512,512]{1,0:T(8,128)(4,1)S(1)} %get-tuple-element.107) | copy-start | bytes 786436
  4.5 10.8 %copy-start.11 = (pred[512,512]{1,0:T(8,128)(4,1)}, pred[512,512]{1,0:T(8,128)(4,1)S(1)}, u32[]{:S(2)}) copy-start(pred[512,512]{1,0:T(8,128)(4,1)S(1)} %get-tuple-element.108) | copy-start | bytes 786436
  4.6 5.8 %copy-start.1 = (bf16[512,2,128]{2,1,0:T(2,128)(2,1)S(1)}, bf16[512,2,128]{2,1,0:T(2,128)(2,1)}, u32[]{:S(2)}) copy-start(bf16[512,2,128]{2,1,0:T(2,128)(2,1)} %param.20) | copy-start | bytes 786436
  4.6 5.8 %copy-start.4 = (bf16[512,2,128]{2,1,0:T(2,128)(2,1)S(1)}, bf16[512,2,128]{2,1,0:T(2,128)(2,1)}, u32[]{:S(2)}) copy-start(bf16[512,2,128]{2,1,0:T(2,128)(2,1)} %param.19) | copy-start | bytes 786436
  10.4 4.9 %copy-start.6 = (bf16[512,2,128]{2,1,0:T(2,128)(2,1)S(1)}, bf16[512,2,128]{2,1,0:T(2,128)(2,1)}, u32[]{:S(2)}) copy-start(bf16[512,2,128]{2,1,0:T(2,128)(2,1)} %param.25) | copy-start | bytes 786436
  18.2 6.8 %collective-permute-start.1 = (f32[2,128,128]{2,1,0:T(8,128)S(1)}, f32[2,128,128]{2,1,0:T(8,128)S(1)}, u32[]{:S(2)}, u32[]{:S(2)}) collective-permute-start(f32[2,128,128]{2,1,0:T(8,128)S(1)} %add.544), channel_id=1, source_target_pairs={{0,2},{2,0},{1,3},{3,1},{4,6},{6,4},{5,7},{7,5},{8,10},{10,8},{9,1... | collective-permute-start | bytes 393224 | tf_op jit(solution)/shard_map/ppermute | solution.py:17
  20.9 14.5 %copy-start.2 = (bf16[512,2,128]{2,1,0:T(2,128)(2,1)S(1)}, bf16[512,2,128]{2,1,0:T(2,128)(2,1)}, u32[]{:S(2)}) copy-start(bf16[512,2,128]{2,1,0:T(2,128)(2,1)} %param.21) | copy-start | bytes 786436
  20.9 14.5 %copy-start.23 = (f32[2,128]{1,0:T(2,128)S(1)}, f32[2,128]{1,0:T(2,128)}, u32[]{:S(2)}) copy-start(f32[2,128]{1,0:T(2,128)} %param.24) | copy-start | bytes 3076
  25.0 9.1 %collective-permute-start.2 = (f32[2,128,128]{2,1,0:T(8,128)S(1)}, f32[2,128,128]{2,1,0:T(8,128)S(1)}, u32[]{:S(2)}, u32[]{:S(2)}) collective-permute-start(f32[2,128,128]{2,1,0:T(8,128)S(1)} %add.545), channel_id=1, source_target_pairs={{0,4},{4,0},{1,5},{5,1},{2,6},{6,2},{3,7},{7,3},{8,12},{12,8},{9,1... | collective-permute-start | bytes 393224 | tf_op jit(solution)/shard_map/ppermute | solution.py:17
  34.2 0.7 copy-start.21
  46.0 1.0 %copy-start.15 = (pred[512,512]{1,0:T(8,128)(4,1)S(1)}, pred[512,512]{1,0:T(8,128)(4,1)}, u32[]{:S(2)}) copy-start(pred[512,512]{1,0:T(8,128)(4,1)} %get-tuple-element.111) | copy-start | bytes 786436
  46.0 1.0 %copy-start.16 = (pred[512,512]{1,0:T(8,128)(4,1)S(1)}, pred[512,512]{1,0:T(8,128)(4,1)}, u32[]{:S(2)}) copy-start(pred[512,512]{1,0:T(8,128)(4,1)} %get-tuple-element.112) | copy-start | bytes 786436
  46.0 1.1 %copy-start.17 = (pred[512,512]{1,0:T(8,128)(4,1)S(1)}, pred[512,512]{1,0:T(8,128)(4,1)}, u32[]{:S(2)}) copy-start(pred[512,512]{1,0:T(8,128)(4,1)} %get-tuple-element.113) | copy-start | bytes 786436
  46.0 1.2 %copy-start.18 = (pred[512,512]{1,0:T(8,128)(4,1)S(1)}, pred[512,512]{1,0:T(8,128)(4,1)}, u32[]{:S(2)}) copy-start(pred[512,512]{1,0:T(8,128)(4,1)} %get-tuple-element.114) | copy-start | bytes 786436
  46.2 1.1 %copy-start.8 = (pred[512,512]{1,0:T(8,128)(4,1)S(1)}, pred[512,512]{1,0:T(8,128)(4,1)}, u32[]{:S(2)}) copy-start(pred[512,512]{1,0:T(8,128)(4,1)} %copy-done.7) | copy-start | bytes 786436
  46.2 1.2 %copy-start.10 = (pred[512,512]{1,0:T(8,128)(4,1)S(1)}, pred[512,512]{1,0:T(8,128)(4,1)}, u32[]{:S(2)}) copy-start(pred[512,512]{1,0:T(8,128)(4,1)} %copy-done.9) | copy-start | bytes 786436
  46.2 1.2 %copy-start.12 = (pred[512,512]{1,0:T(8,128)(4,1)S(1)}, pred[512,512]{1,0:T(8,128)(4,1)}, u32[]{:S(2)}) copy-start(pred[512,512]{1,0:T(8,128)(4,1)} %copy-done.11) | copy-start | bytes 786436
  46.2 1.3 %copy-start.13 = (pred[512,512]{1,0:T(8,128)(4,1)S(1)}, pred[512,512]{1,0:T(8,128)(4,1)}, u32[]{:S(2)}) copy-start(pred[512,512]{1,0:T(8,128)(4,1)} %get-tuple-element.109) | copy-start | bytes 786436
  46.3 1.4 %copy-start.14 = (pred[512,512]{1,0:T(8,128)(4,1)S(1)}, pred[512,512]{1,0:T(8,128)(4,1)}, u32[]{:S(2)}) copy-start(pred[512,512]{1,0:T(8,128)(4,1)} %get-tuple-element.110) | copy-start | bytes 786436
  46.7 5.5 %collective-permute-start.3 = (f32[3,2,128,128]{2,3,0,1:T(8,128)S(1)}, f32[3,2,128,128]{2,3,0,1:T(8,128)S(1)}, u32[]{:S(2)}, u32[]{:S(2)}) collective-permute-start(f32[3,2,128,128]{2,3,0,1:T(8,128)S(1)} %fusion.6), channel_id=1, source_target_pairs={{0,1},{1,0},{2,3},{3,2},{4,5},{5,4},{6,7},{7,6},{8,9},{9,8},{10,11... | collective-permute-start | bytes 1179656 | tf_op jit(solution)/shard_map/ppermute | solution.py:17
  47.6 3.6 %copy-start.22 = (bf16[3,2,128,128]{3,2,1,0:T(8,128)(2,1)S(1)}, bf16[3,2,128,128]{3,2,1,0:T(8,128)(2,1)}, u32[]{:S(2)}) copy-start(bf16[3,2,128,128]{3,2,1,0:T(8,128)(2,1)} %copy-done.21) | copy-start | bytes 589828
  52.2 1.1 %copy-start.3 = (f32[3,2,128,128]{2,3,0,1:T(8,128)}, f32[3,2,128,128]{2,3,0,1:T(8,128)S(1)}, u32[]{:S(2)}) copy-start(f32[3,2,128,128]{2,3,0,1:T(8,128)S(1)} %collective-permute-done.3) | copy-start | bytes 1179652
  52.2 11.0 %copy-start.5 = (bf16[512,2,128]{2,1,0:T(2,128)(2,1)S(1)}, bf16[512,2,128]{2,1,0:T(2,128)(2,1)}, u32[]{:S(2)}) copy-start(bf16[512,2,128]{2,1,0:T(2,128)(2,1)} %param.19) | copy-start | bytes 786436
  52.2 8.0 %collective-permute-start.4 = (f32[2,2,128,128]{2,3,0,1:T(8,128)S(1)}, f32[2,2,128,128]{2,3,0,1:T(8,128)S(1)}, u32[]{:S(2)}, u32[]{:S(2)}) collective-permute-start(f32[2,2,128,128]{2,3,0,1:T(8,128)S(1)} %slice_add_fusion), channel_id=1, source_target_pairs={{0,2},{2,0},{1,3},{3,1},{4,6},{6,4},{5,7},{7,5},{8,10},{10,8},{9,1... | collective-permute-start | bytes 786440 | tf_op jit(solution)/shard_map/ppermute | solution.py:17
  60.2 0.7 copy-start.19
  60.9 7.9 %collective-permute-start.5 = (f32[1,2,128,128]{2,3,0,1:T(8,128)S(1)}, f32[1,2,128,128]{2,3,0,1:T(8,128)S(1)}, u32[]{:S(2)}, u32[]{:S(2)}) collective-permute-start(f32[1,2,128,128]{2,3,0,1:T(8,128)S(1)} %slice_add_fusion.1), channel_id=1, source_target_pairs={{0,4},{4,0},{1,5},{5,1},{2,6},{6,2},{3,7},{7,3},{8,12},{12,8},{9,1... | collective-permute-start | bytes 393224 | tf_op jit(solution)/shard_map/ppermute | solution.py:17
  63.8 5.1 %copy-start.20 = (f32[2,2,128,128]{2,3,0,1:T(8,128)S(1)}, f32[2,2,128,128]{2,3,0,1:T(8,128)}, u32[]{:S(2)}) copy-start(f32[2,2,128,128]{2,3,0,1:T(8,128)} %copy-done.19) | copy-start | bytes 786436
where the time goes:
time: 72.8 us; the launch traced here: 72.5 us
  waiting for transfers between devices  20.4 us (28%)
  matrix products  13.5 us (19%)
  blocking collectives  10 us (14%)
  starting transfers between devices  9.12 us (13%)
  other arithmetic  8.84 us (12%)
  local copies, waits for them, and re-layouts  7.44 us (10%)
  between operations  3.11 us (4%)
    ppermute x6, waiting for transfers between devices, swapped(): return lax.ppermute(block, axis, route)  20.4 us
    psum x1, blocking collectives, shards(): total_squares = lax.psum(jnp.sum(attn * attn, axis=(1, 2)), 'heads')  10 us
    ppermute x6, starting transfers between devices, swapped(): return lax.ppermute(block, axis, route)  9.12 us
    and x5, other arithmetic, level_weights(): chosen = jnp.logical_and(level == level_no, causal)  7.5 us
    unnamed x55, local copies, waits for them, and re-layouts  6.71 us
    dot_general x1, matrix products, local_forward(): jnp.einsum('thd,shd->hts', query_block, key_block, preferred_element_type...  4.87 us
    dot_general x1, matrix products, local_backward(): jnp.einsum('the,she->hts', grad_block, value_block, preferred_element_typ...  3.63 us
  transfers between devices with their start and end apart: 6, of which 4 were waited for; matrix products, arithmetic and copies ran while one was open for 29% of the time, Pallas kernels for 0%

commit v1 on v0

v1 whole, which is shorter than its diff:
```python
import functools

import jax
import jax.numpy as jnp
from jax import lax
from jax.experimental import pallas as pl
from jax.experimental.pallas import tpu as pltpu
from jax.sharding import PartitionSpec as P

exact_mode = lax.Precision.HIGHEST
epsilon = 1e-06
F32 = jnp.float32
BF16 = jnp.bfloat16
VMEM = pl.BlockSpec(memory_space=pltpu.VMEM)
SMEM = pl.BlockSpec(memory_space=pltpu.SMEM)
NT = (((1,), (1,)), ((), ()))
TN = (((0,), (0,)), ((), ()))
NN = (((1,), (0,)), ((), ()))


def dot(left, right, dims):
    return lax.dot_general(left, right, dims, preferred_element_type=F32)


def swapped(block, axis, distance):
    count = lax.axis_size(axis)
    route = []
    for low in range(count):
        high = low | 1 << distance
        if high != low and high < count:
            route += [(low, high), (high, low)]
    return lax.ppermute(block, axis, route)


def summands(block, axis):
    count = lax.axis_size(axis)
    result = [block]
    for step in range(1, count):
        if count & (count - 1) == 0:
            route = [(i, i ^ step) for i in range(count)]
        else:
            route = [(i, (i + step) % count) for i in range(count)]
        result.append(lax.ppermute(block, axis, route))
    return result


def call(kernel, out_shape, args, specs, scratch=(), flops=0, name=None):
    return pl.pallas_call(
        kernel,
        out_shape=out_shape,
        in_specs=specs,
        out_specs=jax.tree.map(lambda _: VMEM, out_shape),
        scratch_shapes=list(scratch),
        compiler_params=pltpu.CompilerParams(vmem_limit_bytes=24 << 20),
        cost_estimate=pl.CostEstimate(
            flops=flops,
            transcendentals=0,
            bytes_accessed=sum(a.size * a.dtype.itemsize for a in args),
        ),
        name=name,
    )(*args)


def split_heads(source, wide, heads, length, store):
    wide[...] = source[...].astype(F32)
    for head in range(heads):
        store(head, wide[pl.ds(head, length, stride=heads), :])


def local_forward(sizes, q_ref, k_ref, v_ref, g_ref, tw_ref, gain_ref,
                  inner_ref, p_ref, w_ref, qd_ref, kd_ref, vd_ref, gg_ref, wide):
    heads, length, levels, block = sizes
    base = block.bit_length() - 1
    for source, target in ((q_ref, qd_ref), (k_ref, kd_ref), (v_ref, vd_ref)):
        def store(head, value, target=target):
            target[head] = value.astype(BF16)
        split_heads(source, wide, heads, length, store)

    def store_gain(head, value):
        gg_ref[head] = value * gain_ref[head:head + 1, :]
    split_heads(g_ref, wide, heads, length, store_gain)
    row = lax.broadcasted_iota(jnp.int32, (block, block), 0)
    column = lax.broadcasted_iota(jnp.int32, (block, block), 1)
    differs = row ^ column
    below = column <= row
    for head in range(heads):
        for i in range(length // block):
            rows = slice(i * block, (i + 1) * block)
            reach = slice(0, (i + 1) * block)
            def weight(level):
                at = head * levels + level
                return tw_ref[rows, at:at + 1]
            diagonal = jnp.broadcast_to(weight(0), (block, block))
            for level in range(1, base + 1):
                diagonal = jnp.where(differs >= 1 << (level - 1), weight(level), diagonal)
            diagonal = jnp.where(below, diagonal, 0.0)
            w_ref[head * (length // block) + i] = diagonal
            scores = dot(qd_ref[head, rows, :], kd_ref[head, reach, :], NT)
            parts = []
            for j in range(i):
                parts.append(scores[:, j * block:(j + 1) * block] * weight(base + (i ^ j).bit_length()))
            parts.append(scores[:, rows] * diagonal)
            for j, part in enumerate(parts):
                p_ref[head, rows, j * block:(j + 1) * block] = part.astype(BF16)
            inner_ref[head, rows, :] = dot(p_ref[head, rows, reach], vd_ref[head, reach, :], NN)


def join(core_ref, mine_ref, other_ref, target_ref, first, lead=None):
    half = mine_ref.shape[-3]
    core = core_ref[0]
    for h in range(half):
        for source, start in ((mine_ref, core * half), (other_ref, (1 - core) * half)):
            if lead is None:
                target_ref[start + h] = source[h].astype(target_ref.dtype)
            else:
                target_ref[first, start + h] = source[h].astype(target_ref.dtype)


def cross_kernel(sizes, *refs):
    heads, length, levels, block, bits = sizes
    core_ref, inner_ref, qd_ref, gg_ref, tw_ref, near_ref = refs[:6]
    halves = refs[6:6 + 2 * (bits - 1)]
    attn_ref, sums_ref, held_ref = refs[6 + 2 * (bits - 1):]
    held_ref[0] = near_ref[...].astype(BF16)
    for j in range(1, bits):
        join(core_ref, halves[2 * j - 2], halves[2 * j - 1], held_ref, j, lead=True)
    for i in range(length // block):
        rows = slice(i * block, (i + 1) * block)
        squares = 0.0
        products = 0.0
        for head in range(heads):
            total = inner_ref[head, rows, :]
            query = qd_ref[head, rows, :]
            for j in range(bits):
                at = head * levels + levels - bits + j
                total = total + tw_ref[rows, at:at + 1] * dot(query, held_ref[j, head], NN)
            attn_ref[head, rows, :] = total
            squares = squares + total * total
            products = products + total * gg_ref[head, rows, :]
        sums_ref[0:1, rows] = jnp.sum(squares.T, axis=0, keepdims=True)
        sums_ref[1:2, rows] = jnp.sum(products.T, axis=0, keepdims=True)


def spread(row, width):
    return jnp.broadcast_to(row, (width, row.shape[1])).T


def grad_kernel(sizes, features, *refs):
    heads, length, levels, block, bits = sizes
    attn_ref, gg_ref, qd_ref, tw_ref = refs[:4]
    sums = refs[4:-4]
    ag_ref, inverse_ref, state_ref, scaled_ref = refs[-4:]
    width = attn_ref.shape[-1]
    total = sums[0][...]
    for part in sums[1:]:
        total = total + part[...]
    inverse = lax.rsqrt(total[0:1] / features + epsilon)
    beta = inverse * inverse * inverse * (total[1:2] / features)
    inverse_ref[...] = inverse
    for i in range(length // block):
        rows = slice(i * block, (i + 1) * block)
        left = spread(inverse[:, rows], width)
        right = spread(beta[:, rows], width)
        for head in range(heads):
            grad = (left * gg_ref[head, rows, :] - attn_ref[head, rows, :] * right).astype(BF16)
            ag_ref[head, rows, :] = grad
            wide = grad.astype(F32)
            for j in range(bits):
                at = head * levels + levels - bits + j
                scaled_ref[head, rows, j * width:(j + 1) * width] = (tw_ref[rows, at:at + 1] * wide).astype(BF16)
    for head in range(heads):
        product = dot(qd_ref[head], scaled_ref[head], TN)
        for j in range(bits):
            state_ref[j, head] = product[:, j * width:(j + 1) * width]


def local_backward(sizes, ag_ref, qd_ref, kd_ref, vd_ref, p_ref, w_ref, tw_ref, held_ref, attn_ref,
                   inverse_ref, gain_ref, normed_ref, dq_ref, dk_ref, dv_ref, weighted_ref):
    heads, length, levels, block, bits = sizes
    base = block.bit_length() - 1
    width = ag_ref.shape[-1]
    blocks = length // block
    for i in range(blocks):
        rows = slice(i * block, (i + 1) * block)
        reach = slice(0, (i + 1) * block)
        left = spread(inverse_ref[:, rows], width)
        for head in range(heads):
            put = pl.ds(i * block * heads + head, block, stride=heads)
            normed_ref[put, :] = attn_ref[head, rows, :] * left * gain_ref[head:head + 1, :]
            def weight(level):
                at = head * levels + level
                return tw_ref[rows, at:at + 1]
            grad = ag_ref[head, rows, :]
            scores = dot(grad, vd_ref[head, reach, :], NT)
            for j in range(i + 1):
                part = scores[:, j * block:(j + 1) * block]
                if j == i:
                    part = part * w_ref[head * blocks + i]
                else:
                    part = part * weight(base + (i ^ j).bit_length())
                weighted_ref[head, rows, j * block:(j + 1) * block] = part.astype(BF16)
            total = dot(weighted_ref[head, rows, reach], kd_ref[head, reach, :], NN)
            for j in range(bits):
                total = total + weight(levels - bits + j) * dot(grad, held_ref[j, head], NT)
            dq_ref[put, :] = total
    for head in range(heads):
        for j in range(blocks):
            cols = slice(j * block, (j + 1) * block)
            rest = slice(j * block, length)
            dk_ref[head, cols, :] = dot(weighted_ref[head, rest, cols], qd_ref[head, rest, :], TN)
            dv_ref[head, cols, :] = dot(p_ref[head, rest, cols], ag_ref[head, rest, :], TN)


def final_kernel(sizes, core_ref, near_ref, mine_ref, other_ref, kd_ref, vd_ref, dk_ref, dv_ref,
                 key_ref, value_ref, back_ref):
    heads, length, block = sizes
    join(core_ref, mine_ref, other_ref, back_ref, 0)
    keep = (1 - core_ref[0]).astype(F32)
    for head in range(heads):
        back = (back_ref[head] + keep * near_ref[head]).astype(BF16)
        for i in range(length // block):
            rows = slice(i * block, (i + 1) * block)
            put = pl.ds(i * block * heads + head, block, stride=heads)
            key_ref[put, :] = dk_ref[head, rows, :] + dot(vd_ref[head, rows, :], back, NT)
            value_ref[put, :] = dv_ref[head, rows, :] + dot(kd_ref[head, rows, :], back, NN)


def shards(query_rows, key_rows, value_rows, level_pick, level_table, norm_gain, out_grad):
    length, heads, width = query_rows.shape
    groups, _, levels = level_table.shape
    local_bits = length.bit_length() - 1
    bits = lax.axis_size("seq").bit_length() - 1
    block = min(128, length)
    half = heads // 2
    scale = width ** (-0.5)
    position = lax.axis_index("seq")
    core = position & 1
    core_arg = core.reshape(1).astype(jnp.int32)
    shape = jax.ShapeDtypeStruct

    flags = (position >> jnp.arange(bits, dtype=jnp.int32) & 1).astype(F32)
    factor = scale * jnp.concatenate([jnp.ones((local_bits + 1,), F32), flags])
    table = (level_table * factor[None, None, :]).reshape(groups, heads * levels)
    one_hot = (level_pick[:, None] == jnp.arange(groups, dtype=jnp.int32)[None, :]).astype(F32)
    weights = jnp.dot(one_hot, table, precision=exact_mode)

    own = jnp.einsum("shd,she->hde", key_rows, value_rows, preferred_element_type=F32)
    near = swapped(own, "seq", 0)
    pair = own + near

    def pick(array, which):
        return lax.dynamic_slice_in_dim(array, which * half, half, array.ndim - 3)

    block_sum = pick(pair, core)
    halves = []
    for place in range(1, bits):
        partner = swapped(block_sum, "seq", place)
        halves += [partner, swapped(partner, "seq", 0)]
        block_sum = block_sum + partner

    rows = length * heads
    flat = lambda a: a.reshape(rows, width)
    local_flops = heads * length * length * width
    inner, probs, diag, qd, kd, vd, gg = call(
        functools.partial(local_forward, (heads, length, levels, block)),
        (
            shape((heads, length, width), F32),
            shape((heads, length, length), BF16),
            shape((heads * (length // block), block, block), F32),
            shape((heads, length, width), BF16),
            shape((heads, length, width), BF16),
            shape((heads, length, width), BF16),
            shape((heads, length, width), F32),
        ),
        (flat(query_rows), flat(key_rows), flat(value_rows), flat(out_grad), weights, norm_gain),
        [VMEM] * 6,
        [pltpu.VMEM((rows, width), F32)],
        flops=4 * local_flops,
        name="local_forward",
    )
    sizes = (heads, length, levels, block, bits)
    attn, sums, held = call(
        functools.partial(cross_kernel, sizes),
        (
            shape((heads, length, width), F32),
            shape((2, length), F32),
            shape((bits, heads, width, width), BF16),
        ),
        (core_arg, inner, qd, gg, weights, near, *halves),
        [SMEM] + [VMEM] * (5 + len(halves)),
        flops=2 * bits * heads * length * width * width,
        name="cross",
    )
    features = heads * width * lax.axis_size("heads")
    parts = summands(sums, "heads")
    attn_grad, inverse, grads = call(
        functools.partial(grad_kernel, sizes, features),
        (
            shape((heads, length, width), BF16),
            shape((1, length), F32),
            shape((bits, heads, width, width), F32),
        ),
        (attn, gg, qd, weights, *parts),
        [VMEM] * (4 + len(parts)),
        [pltpu.VMEM((heads, length, bits * width), BF16)],
        flops=2 * bits * heads * length * width * width,
        name="state_grads",
    )
    upper = grads[1:]
    gathered = pick(upper, core) + swapped(pick(upper, 1 - core), "seq", 0)
    back_near = swapped(grads[0], "seq", 0)
    total = jnp.zeros((half, width, width), F32)
    for place in reversed(range(1, bits)):
        total = total + swapped(total + gathered[place - 1], "seq", place)
    other = swapped(total, "seq", 0)

    normed, query_grad, key_part, value_part = call(
        functools.partial(local_backward, sizes),
        (
            shape((rows, width), F32),
            shape((rows, width), F32),
            shape((heads, length, width), F32),
            shape((heads, length, width), F32),
        ),
        (attn_grad, qd, kd, vd, probs, diag, weights, held, attn, inverse, norm_gain),
        [VMEM] * 11,
        [pltpu.VMEM((heads, length, length), BF16)],
        flops=8 * local_flops,
        name="local_backward",
    )
    key_grad, value_grad = call(
        functools.partial(final_kernel, (heads, length, block)),
        (shape((rows, width), F32), shape((rows, width), F32)),
        (core_arg, back_near, total, other, kd, vd, key_part, value_part),
        [SMEM] + [VMEM] * 7,
        [pltpu.VMEM((heads, width, width), F32)],
        flops=4 * heads * length * width * width,
        name="key_value_grads",
    )
    return tuple(a.reshape(length, heads, width) for a in (normed, query_grad, key_grad, value_grad))


def solution(mesh):
    in_specs = (
        P("seq", "heads", None),
        P("seq", "heads", None),
        P("seq", "heads", None),
        P("seq"),
        P(None, "heads", None),
        P("heads", None),
        P("seq", "heads", None),
    )
    out_specs = (
        P("seq", "heads", None),
        P("seq", "heads", None),
        P("seq", "heads", None),
        P("seq", "heads", None),
    )
    return jax.shard_map(shards, mesh=mesh, in_specs=in_specs, out_specs=out_specs, check_vma=False)
```

time: 72.8 us -> 45.5 us (0.62)
  matrix products: 13.5 us -> 1.63 us
  blocking collectives: 10 us -> 0 us
  other arithmetic: 8.84 us -> 0.14 us
  Pallas kernels: 0 us -> 7.62 us
  starting transfers between devices: 9.12 us -> 15 us
  waiting for transfers between devices: 20.4 us -> 15.8 us
  local copies, waits for them, and re-layouts: 7.44 us -> 3.83 us
  between operations: 3.11 us -> 0.77 us
    dot_general x13 -> x2, matrix products: 13.5 us -> 1.63 us  [the longest x1 1.31 us: shards(): jnp.einsum('shd,she->hde', key_rows, value_rows, preferred_element_type=F32)]
    psum x1 -> x0, blocking collectives: 10 us -> none  [shards(): total_squares = lax.psum(jnp.sum(attn * attn, axis=(1, 2)), 'heads')]
    ppermute x6 -> x10, waiting for transfers between devices: 20.4 us -> 11.6 us  [swapped(): return lax.ppermute(block, axis, route)]
    pallas_call x0 -> x5, Pallas kernels: none -> 7.62 us  [call(): pl.pallas_call(kernel, out_shape=out_shape, in_specs=specs, out_specs=jax...]
    and x5 -> x0, other arithmetic: 7.5 us -> none  [level_weights(): chosen = jnp.logical_and(level == level_no, causal)]
    ppermute x0 -> x3, waiting for transfers between devices: none -> 4.24 us  [summands(): result.append(lax.ppermute(block, axis, route))]
    ppermute x0 -> x3, starting transfers between devices: none -> 3.55 us  [summands(): result.append(lax.ppermute(block, axis, route))]
    unnamed x55 -> x22, local copies, waits for them, and re-layouts: 6.71 us -> 3.7 us
  transfers between devices with their start and end apart: 6 -> 13, of which waited for: 4 -> 9; matrix products, arithmetic and copies ran while one was open for 29% -> 1% of each run, Pallas kernels for 0% -> 10%
where the time goes in v1:
time: 45.5 us; the launch traced here: 44.8 us
  waiting for transfers between devices  15.8 us (35%)
  starting transfers between devices  15 us (33%)
  Pallas kernels  7.62 us (17%)
  local copies, waits for them, and re-layouts  3.83 us (8%)
  matrix products  1.63 us (4%)
  between operations  0.77 us (2%)
    ppermute x10, waiting for transfers between devices, swapped(): return lax.ppermute(block, axis, route)  11.6 us
    ppermute x10, starting transfers between devices, swapped(): return lax.ppermute(block, axis, route)  11.5 us
    pallas_call x5, Pallas kernels, call(): pl.pallas_call(kernel, out_shape=out_shape, in_specs=specs, out_specs=jax...  7.62 us
    ppermute x3, waiting for transfers between devices, summands(): result.append(lax.ppermute(block, axis, route))  4.24 us
    unnamed x22, local copies, waits for them, and re-layouts  3.7 us
    ppermute x3, starting transfers between devices, summands(): result.append(lax.ppermute(block, axis, route))  3.55 us
    dot_general x1, matrix products, shards(): jnp.einsum('shd,she->hde', key_rows, value_rows, preferred_element_type=F32)  1.31 us
  transfers between devices with their start and end apart: 13, of which 9 were waited for; matrix products, arithmetic and copies ran while one was open for 1% of the time, Pallas kernels for 10%

profile of v1, /device:TPU:0, one launch (start us, length us, event | category | flops | bytes accessed | tf_op | source)
XLA Modules:
  0.0 44.8 jit_solution(16977239403057127793)
XLA Ops:
  0.6 1.3 %fusion = f32[2,128,128]{2,1,0:T(8,128)S(1)} fusion(bf16[512,2,128]{2,1,0:T(2,128)(2,1)} %param.9, bf16[512,2,128]{2,1,0:T(2,128)(2,1)} %param.8), kind=kOutput, calls=%fused_computation | convolution fusion | flops 33554432 | bytes 655360 | tf_op jit(solution)/shard_map/shd,she->hde/dot_general | solution.py:247
  1.9 0.5 %collective-permute-start = (f32[2,128,128]{2,1,0:T(8,128)S(1)}, f32[2,128,128]{2,1,0:T(8,128)S(1)}, u32[]{:S(2)}, u32[]{:S(2)}) collective-permute-start(f32[2,128,128]{2,1,0:T(8,128)S(1)} %fusion), channel_id=1, source_target_pairs={{0,1},{1,0},{2,3},{3,2},{4,5},{5,4},{6,7},{7,6},{8,9},{9,8},{10,11... | collective-permute-start | bytes 393224 | tf_op jit(solution)/shard_map/ppermute | solution.py:32
  2.5 1.0 %collective-permute-done.refs_5_ = f32[2,128,128]{2,1,0:T(8,128)S(1)} collective-permute-done((f32[2,128,128]{2,1,0:T(8,128)S(1)}, f32[2,128,128]{2,1,0:T(8,128)S(1)}, u32[]{:S(2)}, u32[]{:S(2)}) %collective-permute-start) | collective-permute-done | bytes 131104 | tf_op jit(solution)/shard_map/ppermute | solution.py:32
  3.5 0.0 copy-start
  3.5 3.0 %collective-permute-start.1 = (f32[1,128,128]{2,1,0:T(8,128)S(1)}, f32[1,128,128]{2,1,0:T(8,128)S(1)}, u32[]{:S(2)}, u32[]{:S(2)}) collective-permute-start(f32[1,128,128]{2,1,0:T(8,128)S(1)} %dynamic-slice_add_fusion.1), channel_id=1, source_target_pairs={{0,2},{2,0},{1,3},{3,1},{4,6},{6,4},{5,7},{7,5},{8,10},{10,8},{9,1... | collective-permute-start | bytes 196616 | tf_op jit(solution)/shard_map/ppermute | solution.py:32
  6.5 0.1 pad_multiply_fusion
  6.5 2.3 %collective-permute-done.1.refs_6_ = f32[1,128,128]{2,1,0:T(8,128)S(1)} collective-permute-done((f32[1,128,128]{2,1,0:T(8,128)S(1)}, f32[1,128,128]{2,1,0:T(8,128)S(1)}, u32[]{:S(2)}, u32[]{:S(2)}) %collective-permute-start.1) | collective-permute-done | bytes 65568 | tf_op jit(solution)/shard_map/ppermute | solution.py:32
  8.9 2.9 %collective-permute-start.3 = (f32[1,128,128]{2,1,0:T(8,128)S(1)}, f32[1,128,128]{2,1,0:T(8,128)S(1)}, u32[]{:S(2)}, u32[]{:S(2)}) collective-permute-start(f32[1,128,128]{2,1,0:T(8,128)S(1)} %add.27), channel_id=1, source_target_pairs={{0,4},{4,0},{1,5},{5,1},{2,6},{6,2},{3,7},{7,3},{8,12},{12,8},{9,1... | collective-permute-start | bytes 196616 | tf_op jit(solution)/shard_map/ppermute | solution.py:32
  11.8 0.0 copy-done.9
  11.8 0.1 reshape.45
  11.9 0.0 collective-permute-start.2
  11.9 2.3 %collective-permute-done.3.refs_8_ = f32[1,128,128]{2,1,0:T(8,128)S(1)} collective-permute-done((f32[1,128,128]{2,1,0:T(8,128)S(1)}, f32[1,128,128]{2,1,0:T(8,128)S(1)}, u32[]{:S(2)}, u32[]{:S(2)}) %collective-permute-start.3) | collective-permute-done | bytes 65568 | tf_op jit(solution)/shard_map/ppermute | solution.py:32
  14.2 0.0 collective-permute-start.4
  14.2 0.0 copy-done.10
  14.2 0.3 fusion.3.tw_ref.refs_4_.refs_3_
  14.5 0.3 copy-done.6
  14.8 0.0 copy-done.1
  14.8 0.0 copy-done
  14.8 0.7 %copy-done.8 = f32[2,128]{1,0:T(2,128)S(1)} copy-done((f32[2,128]{1,0:T(2,128)S(1)}, f32[2,128]{1,0:T(2,128)}, u32[]{:S(2)}) %copy-start.8) | copy-done | bytes 1048
  15.5 0.9 %copy-done.4 = bf16[512,2,128]{2,1,0:T(2,128)(2,1)S(1)} copy-done((bf16[512,2,128]{2,1,0:T(2,128)(2,1)S(1)}, bf16[512,2,128]{2,1,0:T(2,128)(2,1)}, u32[]{:S(2)}) %copy-start.4) | copy-done | bytes 262168
  16.5 0.9 %copy-done.5 = bf16[512,2,128]{2,1,0:T(2,128)(2,1)S(1)} copy-done((bf16[512,2,128]{2,1,0:T(2,128)(2,1)S(1)}, bf16[512,2,128]{2,1,0:T(2,128)(2,1)}, u32[]{:S(2)}) %copy-start.5) | copy-done | bytes 262168
  17.4 1.9 %local_forward.1 = (f32[2,512,128]{2,1,0:T(8,128)S(1)}, bf16[2,512,512]{2,1,0:T(8,128)(2,1)S(1)}, f32[8,128,128]{2,1,0:T(8,128)S(1)}, bf16[2,512,128]{2,1,0:T(8,...) custom-call(bf16[1024,128]{1,0:T(8,128)(2,1)S(1)} %bitcast.20, ...), custom_call_target="tpu_custom_call" | custom-call | flops 268435456 | bytes 1102848 | tf_op jit(solution)/shard_map/local_forward/pallas_call | solution.py:48
  19.3 0.8 %copy-done.2 = f32[8,128,128]{2,1,0:T(8,128)} copy-done((f32[8,128,128]{2,1,0:T(8,128)}, f32[8,128,128]{2,1,0:T(8,128)S(1)}, u32[]{:S(2)}) %copy-start.2) | copy-done | bytes 524312
  20.1 0.0 collective-permute-done.2.refs_7_
  20.1 0.0 collective-permute-done.4.refs_9_
  20.1 0.0 copy-done.7
  20.1 0.7 %cross.1 = (f32[2,512,128]{2,1,0:T(8,128)S(1)}, f32[2,512]{1,0:T(2,128)S(1)}, bf16[3,2,128,128]{3,2,1,0:T(8,128)(2,1)S(1)}) custom-call(s32[1]{0:T(128)} %bitcast.refs_0_.core_ref, f32[2,512,128]{2,1,0:T(8,128)S(1)} %get-tuple-element.23.refs_1_, bf16[2,512,128]{2,1,0:T(8,128)(2,1)S(1)} %get-tuple-element.24.refs_2_.qd_ref, ...), custom_call_target="tpu_custom_call" | custom-call | flops 100663296 | bytes 1757188 | tf_op jit(solution)/shard_map/cross/pallas_call | solution.py:48
  20.8 1.8 %collective-permute-start.5 = (f32[2,512]{1,0:T(2,128)S(1)}, f32[2,512]{1,0:T(2,128)S(1)}, u32[]{:S(2)}, u32[]{:S(2)}) collective-permute-start(f32[2,512]{1,0:T(2,128)S(1)} %get-tuple-element.27.refs_4_), channel_id=1, source_target_pairs={{0,8},{8,0},{16,24},{24,16},{1,9},{9,1},{17,25},{25,17},{2,10},{10... | collective-permute-start | bytes 12296 | tf_op jit(solution)/shard_map/ppermute | solution.py:43
  22.6 1.5 %collective-permute-start.6 = (f32[2,512]{1,0:T(2,128)S(1)}, f32[2,512]{1,0:T(2,128)S(1)}, u32[]{:S(2)}, u32[]{:S(2)}) collective-permute-start(f32[2,512]{1,0:T(2,128)S(1)} %get-tuple-element.27.refs_4_), channel_id=1, source_target_pairs={{0,16},{8,24},{16,0},{24,8},{1,17},{9,25},{17,1},{25,9},{2,18},{10... | collective-permute-start | bytes 12296 | tf_op jit(solution)/shard_map/ppermute | solution.py:43
  24.1 0.3 collective-permute-start.7
  24.4 0.1 collective-permute-done.5.refs_5_
  24.5 1.7 %collective-permute-done.6.refs_6_ = f32[2,512]{1,0:T(2,128)S(1)} collective-permute-done((f32[2,512]{1,0:T(2,128)S(1)}, f32[2,512]{1,0:T(2,128)S(1)}, u32[]{:S(2)}, u32[]{:S(2)}) %collective-permute-start.6) | collective-permute-done | bytes 4128 | tf_op jit(solution)/shard_map/ppermute | solution.py:43
  26.2 2.4 %collective-permute-done.7.refs_7_ = f32[2,512]{1,0:T(2,128)S(1)} collective-permute-done((f32[2,512]{1,0:T(2,128)S(1)}, f32[2,512]{1,0:T(2,128)S(1)}, u32[]{:S(2)}, u32[]{:S(2)}) %collective-permute-start.7) | collective-permute-done | bytes 4128 | tf_op jit(solution)/shard_map/ppermute | solution.py:43
  28.6 1.0 %state_grads.1 = (bf16[2,512,128]{2,1,0:T(8,128)(2,1)S(1)}, f32[1,512]{1,0:T(1,128)S(1)}, f32[3,2,128,128]{3,2,1,0:T(8,128)S(1)}) custom-call(f32[2,512,128]{2,1,0:T(8,128)S(1)} %get-tuple-element.26.refs_0_.attn_ref, f32[2,512,128]{2,1,0:T(8,128)S(1)} %get-tuple-element.25.refs_3_.refs_1_, bf16[2,512,128]{2,1,0:T(8,128)(2,1)S(1)} %get-tuple-element.24.refs_2_.qd_ref, ...), custom_call_target="tpu_custom_call" | custom-call | flops 100663296 | bytes 1380352 | tf_op jit(solution)/shard_map/state_grads/pallas_call | solution.py:48
  29.7 0.0 copy-start.3
  29.7 0.1 collective-permute-start.9
  29.8 1.3 %collective-permute-done.9 = f32[2,1,128,128]{3,2,1,0:T(8,128)S(1)} collective-permute-done((f32[2,1,128,128]{3,2,1,0:T(8,128)S(1)}, f32[2,1,128,128]{3,2,1,0:T(8,128)S(1)}, u32[]{:S(2)}, u32[]{:S(2)}) %collective-permute-start.9) | collective-permute-done | bytes 131104 | tf_op jit(solution)/shard_map/ppermute | solution.py:32
  31.1 2.7 %collective-permute-start.10 = (f32[1,128,128]{2,1,0:T(8,128)S(1)}, f32[1,128,128]{2,1,0:T(8,128)S(1)}, u32[]{:S(2)}, u32[]{:S(2)}) collective-permute-start(f32[1,128,128]{2,1,0:T(8,128)S(1)} %slice_bitcast_fusion.2), channel_id=1, source_target_pairs={{0,4},{4,0},{1,5},{5,1},{2,6},{6,2},{3,7},{7,3},{8,12},{12,8},{9,1... | collective-permute-start | bytes 196616 | tf_op jit(solution)/shard_map/ppermute | solution.py:32
  33.8 2.5 %collective-permute-done.10 = f32[1,128,128]{2,1,0:T(8,128)S(1)} collective-permute-done((f32[1,128,128]{2,1,0:T(8,128)S(1)}, f32[1,128,128]{2,1,0:T(8,128)S(1)}, u32[]{:S(2)}, u32[]{:S(2)}) %collective-permute-start.10) | collective-permute-done | bytes 65568 | tf_op jit(solution)/shard_map/ppermute | solution.py:32
  36.4 2.1 %collective-permute-start.11 = (f32[1,128,128]{2,1,0:T(8,128)S(1)}, f32[1,128,128]{2,1,0:T(8,128)S(1)}, u32[]{:S(2)}, u32[]{:S(2)}) collective-permute-start(f32[1,128,128]{2,1,0:T(8,128)S(1)} %fusion.5), channel_id=1, source_target_pairs={{0,2},{2,0},{1,3},{3,1},{4,6},{6,4},{5,7},{7,5},{8,10},{10,8},{9,1... | collective-permute-start | bytes 196616 | tf_op jit(solution)/shard_map/ppermute | solution.py:32
  38.5 0.1 collective-permute-start.8
  38.5 2.2 %collective-permute-done.11 = f32[1,128,128]{2,1,0:T(8,128)S(1)} collective-permute-done((f32[1,128,128]{2,1,0:T(8,128)S(1)}, f32[1,128,128]{2,1,0:T(8,128)S(1)}, u32[]{:S(2)}, u32[]{:S(2)}) %collective-permute-start.11) | collective-permute-done | bytes 65568 | tf_op jit(solution)/shard_map/ppermute | solution.py:32
  40.7 0.1 collective-permute-start.12
  40.8 0.0 copy-done.3
  40.8 2.7 %local_backward.1 = (f32[1024,128]{1,0:T(8,128)}, f32[1024,128]{1,0:T(8,128)}, f32[2,512,128]{2,1,0:T(8,128)S(1)}, f32[2,512,128]{2,1,0:T(8,128)S(1)}) custom-call(bf16[2,512,128]{2,1,0:T(8,128)(2,1)S(1)} %get-tuple-element.28.ag_ref, bf16[2,512,128]{2,1,0:T(8,128)(2,1)S(1)} %get-tuple-element.24.refs_2_.qd_ref, ...), custom_call_target="tpu_custom_call" | custom-call | flops 536870912 | bytes 3398656 | tf_op jit(solution)/shard_map/local_backward/pallas_call | solution.py:48
  43.5 0.0 collective-permute-done.8.near_ref
  43.5 0.0 collective-permute-done.12.other_ref
  43.5 1.3 %key_value_grads.1 = (f32[1024,128]{1,0:T(8,128)}, f32[1024,128]{1,0:T(8,128)}) custom-call(s32[1]{0:T(128)} %bitcast.refs_0_.core_ref, f32[2,128,128]{2,1,0:T(8,128)S(1)} %collective-permute-done.8.near_ref, f32[1,128,128]{2,1,0:T(8,128)S(1)} %add.31.mine_ref, f32[1,128,128]{2,1,0:T(8,128)S(1)} %collective-permute-done.12.other_ref, ...), custom_call_target="tpu_custom_call" | custom-call | flops 67108864 | bytes 1835012 | tf_op jit(solution)/shard_map/key_value_grads/pallas_call | solution.py:48
  (20 shorter events, 0.1 us)
Async XLA Ops:
  1.9 1.5 %collective-permute-start = (f32[2,128,128]{2,1,0:T(8,128)S(1)}, f32[2,128,128]{2,1,0:T(8,128)S(1)}, u32[]{:S(2)}, u32[]{:S(2)}) collective-permute-start(f32[2,128,128]{2,1,0:T(8,128)S(1)} %fusion), channel_id=1, source_target_pairs={{0,1},{1,0},{2,3},{3,2},{4,5},{5,4},{6,7},{7,6},{8,9},{9,8},{10,11... | collective-permute-start | bytes 393224 | tf_op jit(solution)/shard_map/ppermute | solution.py:32
  3.4 8.4 %copy-start.9 = (f32[8,2,13]{2,1,0:T(2,128)S(1)}, f32[8,2,13]{2,1,0:T(2,128)}, u32[]{:S(2)}) copy-start(f32[8,2,13]{2,1,0:T(2,128)} %param.11) | copy-start | bytes 2500
  3.4 10.8 %copy-start.10 = (s32[512]{0:T(512)S(1)}, s32[512]{0:T(512)}, u32[]{:S(2)}) copy-start(s32[512]{0:T(512)} %param.10) | copy-start | bytes 6148
  3.4 11.4 %copy-start.1 = (bf16[512,2,128]{2,1,0:T(2,128)(2,1)S(1)}, bf16[512,2,128]{2,1,0:T(2,128)(2,1)}, u32[]{:S(2)}) copy-start(bf16[512,2,128]{2,1,0:T(2,128)(2,1)} %param.9) | copy-start | bytes 786436
  3.5 11.4 %copy-start = (bf16[512,2,128]{2,1,0:T(2,128)(2,1)S(1)}, bf16[512,2,128]{2,1,0:T(2,128)(2,1)}, u32[]{:S(2)}) copy-start(bf16[512,2,128]{2,1,0:T(2,128)(2,1)} %param.8) | copy-start | bytes 786436
  3.5 5.4 %collective-permute-start.1 = (f32[1,128,128]{2,1,0:T(8,128)S(1)}, f32[1,128,128]{2,1,0:T(8,128)S(1)}, u32[]{:S(2)}, u32[]{:S(2)}) collective-permute-start(f32[1,128,128]{2,1,0:T(8,128)S(1)} %dynamic-slice_add_fusion.1), channel_id=1, source_target_pairs={{0,2},{2,0},{1,3},{3,1},{4,6},{6,4},{5,7},{7,5},{8,10},{10,8},{9,1... | collective-permute-start | bytes 196616 | tf_op jit(solution)/shard_map/ppermute | solution.py:32
  8.9 5.3 %collective-permute-start.3 = (f32[1,128,128]{2,1,0:T(8,128)S(1)}, f32[1,128,128]{2,1,0:T(8,128)S(1)}, u32[]{:S(2)}, u32[]{:S(2)}) collective-permute-start(f32[1,128,128]{2,1,0:T(8,128)S(1)} %add.27), channel_id=1, source_target_pairs={{0,4},{4,0},{1,5},{5,1},{2,6},{6,2},{3,7},{7,3},{8,12},{12,8},{9,1... | collective-permute-start | bytes 196616 | tf_op jit(solution)/shard_map/ppermute | solution.py:32
  11.9 8.2 %collective-permute-start.2 = (f32[1,128,128]{2,1,0:T(8,128)S(1)}, f32[1,128,128]{2,1,0:T(8,128)S(1)}, u32[]{:S(2)}, u32[]{:S(2)}) collective-permute-start(f32[1,128,128]{2,1,0:T(8,128)S(1)} %collective-permute-done.1.refs_6_), channel_id=1, source_target_pairs={{0,1},{1,0},{2,3},{3,2},{4,5},{5,4},{6,7},{7,6},{8,9},{9,8},{10,11... | collective-permute-start | bytes 196616 | tf_op jit(solution)/shard_map/ppermute | solution.py:32
  14.2 0.6 %copy-start.6 = (f32[1,128,128]{2,1,0:T(8,128)}, f32[1,128,128]{2,1,0:T(8,128)S(1)}, u32[]{:S(2)}) copy-start(f32[1,128,128]{2,1,0:T(8,128)S(1)} %collective-permute-done.3.refs_8_) | copy-start | bytes 196612
  14.2 5.9 %collective-permute-start.4 = (f32[1,128,128]{2,1,0:T(8,128)S(1)}, f32[1,128,128]{2,1,0:T(8,128)S(1)}, u32[]{:S(2)}, u32[]{:S(2)}) collective-permute-start(f32[1,128,128]{2,1,0:T(8,128)S(1)} %collective-permute-done.3.refs_8_), channel_id=1, source_target_pairs={{0,1},{1,0},{2,3},{3,2},{4,5},{5,4},{6,7},{7,6},{8,9},{9,8},{10,11... | collective-permute-start | bytes 196616 | tf_op jit(solution)/shard_map/ppermute | solution.py:32
  14.8 0.7 %copy-start.8 = (f32[2,128]{1,0:T(2,128)S(1)}, f32[2,128]{1,0:T(2,128)}, u32[]{:S(2)}) copy-start(f32[2,128]{1,0:T(2,128)} %gain_ref.3) | copy-start | bytes 3076
  15.5 0.9 %copy-start.4 = (bf16[512,2,128]{2,1,0:T(2,128)(2,1)S(1)}, bf16[512,2,128]{2,1,0:T(2,128)(2,1)}, u32[]{:S(2)}) copy-start(bf16[512,2,128]{2,1,0:T(2,128)(2,1)} %param.7) | copy-start | bytes 786436
  16.5 0.9 %copy-start.5 = (bf16[512,2,128]{2,1,0:T(2,128)(2,1)S(1)}, bf16[512,2,128]{2,1,0:T(2,128)(2,1)}, u32[]{:S(2)}) copy-start(bf16[512,2,128]{2,1,0:T(2,128)(2,1)} %param.13) | copy-start | bytes 786436
  17.4 2.7 %copy-start.7 = (f32[1,128,128]{2,1,0:T(8,128)S(1)}, f32[1,128,128]{2,1,0:T(8,128)}, u32[]{:S(2)}) copy-start(f32[1,128,128]{2,1,0:T(8,128)} %copy-done.6) | copy-start | bytes 196612
  19.3 0.8 %copy-start.2 = (f32[8,128,128]{2,1,0:T(8,128)}, f32[8,128,128]{2,1,0:T(8,128)S(1)}, u32[]{:S(2)}) copy-start(f32[8,128,128]{2,1,0:T(8,128)S(1)} %get-tuple-element.32.w_ref) | copy-start | bytes 1572868
  20.8 3.7 %collective-permute-start.5 = (f32[2,512]{1,0:T(2,128)S(1)}, f32[2,512]{1,0:T(2,128)S(1)}, u32[]{:S(2)}, u32[]{:S(2)}) collective-permute-start(f32[2,512]{1,0:T(2,128)S(1)} %get-tuple-element.27.refs_4_), channel_id=1, source_target_pairs={{0,8},{8,0},{16,24},{24,16},{1,9},{9,1},{17,25},{25,17},{2,10},{10... | collective-permute-start | bytes 12296 | tf_op jit(solution)/shard_map/ppermute | solution.py:43
  22.6 3.6 %collective-permute-start.6 = (f32[2,512]{1,0:T(2,128)S(1)}, f32[2,512]{1,0:T(2,128)S(1)}, u32[]{:S(2)}, u32[]{:S(2)}) collective-permute-start(f32[2,512]{1,0:T(2,128)S(1)} %get-tuple-element.27.refs_4_), channel_id=1, source_target_pairs={{0,16},{8,24},{16,0},{24,8},{1,17},{9,25},{17,1},{25,9},{2,18},{10... | collective-permute-start | bytes 12296 | tf_op jit(solution)/shard_map/ppermute | solution.py:43
  24.1 4.5 %collective-permute-start.7 = (f32[2,512]{1,0:T(2,128)S(1)}, f32[2,512]{1,0:T(2,128)S(1)}, u32[]{:S(2)}, u32[]{:S(2)}) collective-permute-start(f32[2,512]{1,0:T(2,128)S(1)} %get-tuple-element.27.refs_4_), channel_id=1, source_target_pairs={{0,24},{8,16},{16,8},{24,0},{1,25},{9,17},{17,9},{25,1},{2,26},{10... | collective-permute-start | bytes 12296 | tf_op jit(solution)/shard_map/ppermute | solution.py:43
  29.7 11.1 %copy-start.3 = (f32[8,128,128]{2,1,0:T(8,128)S(1)}, f32[8,128,128]{2,1,0:T(8,128)}, u32[]{:S(2)}) copy-start(f32[8,128,128]{2,1,0:T(8,128)} %copy-done.2) | copy-start | bytes 1572868
  29.7 1.4 %collective-permute-start.9 = (f32[2,1,128,128]{3,2,1,0:T(8,128)S(1)}, f32[2,1,128,128]{3,2,1,0:T(8,128)S(1)}, u32[]{:S(2)}, u32[]{:S(2)}) collective-permute-start(f32[2,1,128,128]{3,2,1,0:T(8,128)S(1)} %constant_dynamic-slice_fusion), channel_id=1, source_target_pairs={{0,1},{1,0},{2,3},{3,2},{4,5},{5,4},{6,7},{7,6},{8,9},{9,8},{10,11... | collective-permute-start | bytes 393224 | tf_op jit(solution)/shard_map/ppermute | solution.py:32
  31.1 5.2 %collective-permute-start.10 = (f32[1,128,128]{2,1,0:T(8,128)S(1)}, f32[1,128,128]{2,1,0:T(8,128)S(1)}, u32[]{:S(2)}, u32[]{:S(2)}) collective-permute-start(f32[1,128,128]{2,1,0:T(8,128)S(1)} %slice_bitcast_fusion.2), channel_id=1, source_target_pairs={{0,4},{4,0},{1,5},{5,1},{2,6},{6,2},{3,7},{7,3},{8,12},{12,8},{9,1... | collective-permute-start | bytes 196616 | tf_op jit(solution)/shard_map/ppermute | solution.py:32
  36.4 4.3 %collective-permute-start.11 = (f32[1,128,128]{2,1,0:T(8,128)S(1)}, f32[1,128,128]{2,1,0:T(8,128)S(1)}, u32[]{:S(2)}, u32[]{:S(2)}) collective-permute-start(f32[1,128,128]{2,1,0:T(8,128)S(1)} %fusion.5), channel_id=1, source_target_pairs={{0,2},{2,0},{1,3},{3,1},{4,6},{6,4},{5,7},{7,5},{8,10},{10,8},{9,1... | collective-permute-start | bytes 196616 | tf_op jit(solution)/shard_map/ppermute | solution.py:32
  38.5 5.0 %collective-permute-start.8 = (f32[2,128,128]{2,1,0:T(8,128)S(1)}, f32[2,128,128]{2,1,0:T(8,128)S(1)}, u32[]{:S(2)}, u32[]{:S(2)}) collective-permute-start(f32[2,128,128]{2,1,0:T(8,128)S(1)} %slice_bitcast_fusion), channel_id=1, source_target_pairs={{0,1},{1,0},{2,3},{3,2},{4,5},{5,4},{6,7},{7,6},{8,9},{9,8},{10,11... | collective-permute-start | bytes 393224 | tf_op jit(solution)/shard_map/ppermute | solution.py:32
  40.7 2.8 %collective-permute-start.12 = (f32[1,128,128]{2,1,0:T(8,128)S(1)}, f32[1,128,128]{2,1,0:T(8,128)S(1)}, u32[]{:S(2)}, u32[]{:S(2)}) collective-permute-start(f32[1,128,128]{2,1,0:T(8,128)S(1)} %add.31.mine_ref), channel_id=1, source_target_pairs={{0,1},{1,0},{2,3},{3,2},{4,5},{5,4},{6,7},{7,6},{8,9},{9,8},{10,11... | collective-permute-start | bytes 196616 | tf_op jit(solution)/shard_map/ppermute | solution.py:32

commit v2 on v1

--- a/solution.py
+++ b/solution.py
@@ -12,6 +12,7 @@
 F32 = jnp.float32
 BF16 = jnp.bfloat16
 VMEM = pl.BlockSpec(memory_space=pltpu.VMEM)
+HBM = pl.BlockSpec(memory_space=pltpu.HBM)
 SMEM = pl.BlockSpec(memory_space=pltpu.SMEM)
 NT = (((1,), (1,)), ((), ()))
 TN = (((0,), (0,)), ((), ()))
@@ -30,6 +31,19 @@
         if high != low and high < count:
             route += [(low, high), (high, low)]
     return lax.ppermute(block, axis, route)
+
+
+def exchanged(block, axis, distance):
+    count = lax.axis_size(axis)
+    needed, rest = [], []
+    for low in range(count):
+        high = low | 1 << distance
+        if high == low:
+            continue
+        last = low >> (distance + 1) == (count - 1) >> (distance + 1)
+        route = rest if last else needed
+        route += [(low, high), (high, low)]
+    return [lax.ppermute(block, axis, route) for route in (needed, rest) if route]
 
 
 def summands(block, axis):
@@ -51,7 +65,7 @@
         in_specs=specs,
         out_specs=jax.tree.map(lambda _: VMEM, out_shape),
         scratch_shapes=list(scratch),
-        compiler_params=pltpu.CompilerParams(vmem_limit_bytes=24 << 20),
+        compiler_params=pltpu.CompilerParams(vmem_limit_bytes=16 << 20),
         cost_estimate=pl.CostEstimate(
             flops=flops,
             transcendentals=0,
@@ -67,18 +81,42 @@
         store(head, wide[pl.ds(head, length, stride=heads), :])
 
 
-def local_forward(sizes, q_ref, k_ref, v_ref, g_ref, tw_ref, gain_ref,
-                  inner_ref, p_ref, w_ref, qd_ref, kd_ref, vd_ref, gg_ref, wide):
-    heads, length, levels, block = sizes
+def level_rows(sizes, scale, position_ref, pick_ref, table_ref, tw_ref):
+    heads, length, levels, block, bits = sizes
+    groups = table_ref.shape[0]
+    lane = lax.broadcasted_iota(jnp.int32, (groups, levels), 1)
+    factor = jnp.full((groups, levels), scale, F32)
+    for j in range(bits):
+        flag = (position_ref[0] >> j & 1).astype(F32) * scale
+        factor = jnp.where(lane == levels - bits + j, flag, factor)
+    group = lax.broadcasted_iota(jnp.int32, (groups, length), 0)
+    one_hot = (group == pick_ref[...]).astype(F32)
+    for head in range(heads):
+        table = table_ref[:, head, :] * factor
+        tw_ref[head] = lax.dot_general(one_hot, table, TN, precision=exact_mode, preferred_element_type=F32)
+
+
+def local_forward(sizes, scale, position_ref, q_ref, k_ref, v_ref, g_ref, gain_hbm, pick_ref, table_ref,
+                  inner_ref, p_ref, w_ref, qd_ref, kd_ref, vd_ref, gg_ref, tw_ref, wide, raw, gain_ref, sems):
+    heads, length, levels, block, bits = sizes
     base = block.bit_length() - 1
-    for source, target in ((q_ref, qd_ref), (k_ref, kd_ref), (v_ref, vd_ref)):
+    copies = [pltpu.make_async_copy(gain_hbm, gain_ref, sems.at[4])]
+    for n, source in enumerate((k_ref, v_ref, q_ref, g_ref)):
+        copies.append(pltpu.make_async_copy(source, raw.at[n], sems.at[n]))
+    for copy in copies:
+        copy.start()
+    level_rows(sizes, scale, position_ref, pick_ref, table_ref, tw_ref)
+    for n, target in enumerate((kd_ref, vd_ref, qd_ref)):
         def store(head, value, target=target):
             target[head] = value.astype(BF16)
-        split_heads(source, wide, heads, length, store)
+        copies[n + 1].wait()
+        split_heads(raw.at[n], wide, heads, length, store)
+    copies[4].wait()
+    copies[0].wait()
 
     def store_gain(head, value):
         gg_ref[head] = value * gain_ref[head:head + 1, :]
-    split_heads(g_ref, wide, heads, length, store_gain)
+    split_heads(raw.at[3], wide, heads, length, store_gain)
     row = lax.broadcasted_iota(jnp.int32, (block, block), 0)
     column = lax.broadcasted_iota(jnp.int32, (block, block), 1)
     differs = row ^ column
@@ -88,8 +126,7 @@
             rows = slice(i * block, (i + 1) * block)
             reach = slice(0, (i + 1) * block)
             def weight(level):
-                at = head * levels + level
-                return tw_ref[rows, at:at + 1]
+                return tw_ref[head, rows, level:level + 1]
             diagonal = jnp.broadcast_to(weight(0), (block, block))
             for level in range(1, base + 1):
                 diagonal = jnp.where(differs >= 1 << (level - 1), weight(level), diagonal)
@@ -107,7 +144,7 @@
 
 def join(core_ref, mine_ref, other_ref, target_ref, first, lead=None):
     half = mine_ref.shape[-3]
-    core = core_ref[0]
+    core = (core_ref[0] & 1)
     for h in range(half):
         for source, start in ((mine_ref, core * half), (other_ref, (1 - core) * half)):
             if lead is None:
@@ -120,7 +157,7 @@
     heads, length, levels, block, bits = sizes
     core_ref, inner_ref, qd_ref, gg_ref, tw_ref, near_ref = refs[:6]
     halves = refs[6:6 + 2 * (bits - 1)]
-    attn_ref, sums_ref, held_ref = refs[6 + 2 * (bits - 1):]
+    attn_ref, sums_ref, held_ref = refs[-3:]
     held_ref[0] = near_ref[...].astype(BF16)
     for j in range(1, bits):
         join(core_ref, halves[2 * j - 2], halves[2 * j - 1], held_ref, j, lead=True)
@@ -132,8 +169,8 @@
             total = inner_ref[head, rows, :]
             query = qd_ref[head, rows, :]
             for j in range(bits):
-                at = head * levels + levels - bits + j
-                total = total + tw_ref[rows, at:at + 1] * dot(query, held_ref[j, head], NN)
+                at = levels - bits + j
+                total = total + tw_ref[head, rows, at:at + 1] * dot(query, held_ref[j, head], NN)
             attn_ref[head, rows, :] = total
             squares = squares + total * total
             products = products + total * gg_ref[head, rows, :]
@@ -147,9 +184,9 @@
 
 def grad_kernel(sizes, features, *refs):
     heads, length, levels, block, bits = sizes
-    attn_ref, gg_ref, qd_ref, tw_ref = refs[:4]
-    sums = refs[4:-4]
-    ag_ref, inverse_ref, state_ref, scaled_ref = refs[-4:]
+    position_ref, attn_ref, gg_ref, qd_ref, tw_ref = refs[:5]
+    sums = refs[5:-7]
+    ag_ref, inverse_ref, first_ref, keep_ref, send_ref, scaled_ref, state_ref = refs[-7:]
     width = attn_ref.shape[-1]
     total = sums[0][...]
     for part in sums[1:]:
@@ -166,12 +203,19 @@
             ag_ref[head, rows, :] = grad
             wide = grad.astype(F32)
             for j in range(bits):
-                at = head * levels + levels - bits + j
-                scaled_ref[head, rows, j * width:(j + 1) * width] = (tw_ref[rows, at:at + 1] * wide).astype(BF16)
+                at = levels - bits + j
+                scaled_ref[head, rows, j * width:(j + 1) * width] = (tw_ref[head, rows, at:at + 1] * wide).astype(BF16)
     for head in range(heads):
         product = dot(qd_ref[head], scaled_ref[head], TN)
-        for j in range(bits):
-            state_ref[j, head] = product[:, j * width:(j + 1) * width]
+        first_ref[head] = product[:, :width]
+        for j in range(1, bits):
+            state_ref[j - 1, head] = product[:, j * width:(j + 1) * width]
+    half = heads // 2
+    core = position_ref[0] & 1
+    for j in range(bits - 1):
+        for h in range(half):
+            keep_ref[j, h] = state_ref[j, core * half + h]
+            send_ref[j, h] = state_ref[j, (1 - core) * half + h]
 
 
 def local_backward(sizes, ag_ref, qd_ref, kd_ref, vd_ref, p_ref, w_ref, tw_ref, held_ref, attn_ref,
@@ -188,8 +232,7 @@
             put = pl.ds(i * block * heads + head, block, stride=heads)
             normed_ref[put, :] = attn_ref[head, rows, :] * left * gain_ref[head:head + 1, :]
             def weight(level):
-                at = head * levels + level
-                return tw_ref[rows, at:at + 1]
+                return tw_ref[head, rows, level:level + 1]
             grad = ag_ref[head, rows, :]
             scores = dot(grad, vd_ref[head, reach, :], NT)
             for j in range(i + 1):
@@ -215,7 +258,7 @@
                  key_ref, value_ref, back_ref):
     heads, length, block = sizes
     join(core_ref, mine_ref, other_ref, back_ref, 0)
-    keep = (1 - core_ref[0]).astype(F32)
+    keep = (1 - (core_ref[0] & 1)).astype(F32)
     for head in range(heads):
         back = (back_ref[head] + keep * near_ref[head]).astype(BF16)
         for i in range(length // block):
@@ -233,36 +276,29 @@
     block = min(128, length)
     half = heads // 2
     scale = width ** (-0.5)
-    position = lax.axis_index("seq")
-    core = position & 1
-    core_arg = core.reshape(1).astype(jnp.int32)
+    position = lax.axis_index("seq").astype(jnp.int32)
+    place_arg = position.reshape(1)
     shape = jax.ShapeDtypeStruct
-
-    flags = (position >> jnp.arange(bits, dtype=jnp.int32) & 1).astype(F32)
-    factor = scale * jnp.concatenate([jnp.ones((local_bits + 1,), F32), flags])
-    table = (level_table * factor[None, None, :]).reshape(groups, heads * levels)
-    one_hot = (level_pick[:, None] == jnp.arange(groups, dtype=jnp.int32)[None, :]).astype(F32)
-    weights = jnp.dot(one_hot, table, precision=exact_mode)
 
     own = jnp.einsum("shd,she->hde", key_rows, value_rows, preferred_element_type=F32)
     near = swapped(own, "seq", 0)
     pair = own + near
 
-    def pick(array, which):
-        return lax.dynamic_slice_in_dim(array, which * half, half, array.ndim - 3)
-
-    block_sum = pick(pair, core)
-    halves = []
+    block_sum = lax.dynamic_slice(
+        pair, ((position & 1) * half, 0, 0), (half, width, width), allow_negative_indices=False
+    )
+    partners = []
     for place in range(1, bits):
-        partner = swapped(block_sum, "seq", place)
-        halves += [partner, swapped(partner, "seq", 0)]
-        block_sum = block_sum + partner
+        arrived = exchanged(block_sum, "seq", place)
+        partners.append(arrived)
+        block_sum = block_sum + arrived[0]
 
     rows = length * heads
     flat = lambda a: a.reshape(rows, width)
     local_flops = heads * length * length * width
-    inner, probs, diag, qd, kd, vd, gg = call(
-        functools.partial(local_forward, (heads, length, levels, block)),
+    sizes = (heads, length, levels, block, bits)
+    inner, probs, diag, qd, kd, vd, gg, weights = call(
+        functools.partial(local_forward, sizes, scale),
         (
             shape((heads, length, width), F32),
             shape((heads, length, length), BF16),
@@ -271,14 +307,33 @@
             shape((heads, length, width), BF16),
             shape((heads, length, width), BF16),
             shape((heads, length, width), F32),
-        ),
-        (flat(query_rows), flat(key_rows), flat(value_rows), flat(out_grad), weights, norm_gain),
-        [VMEM] * 6,
-        [pltpu.VMEM((rows, width), F32)],
+            shape((heads, length, levels), F32),
+        ),
+        (
+            place_arg,
+            flat(query_rows),
+            flat(key_rows),
+            flat(value_rows),
+            flat(out_grad),
+            norm_gain,
+            level_pick.reshape(1, length),
+            level_table,
+        ),
+        [SMEM, HBM, HBM, HBM, HBM, HBM, VMEM, VMEM],
+        [
+            pltpu.VMEM((rows, width), F32),
+            pltpu.VMEM((4, rows, width), BF16),
+            pltpu.VMEM((heads, width), F32),
+            pltpu.SemaphoreType.DMA((5,)),
+        ],
         flops=4 * local_flops,
         name="local_forward",
     )
-    sizes = (heads, length, levels, block, bits)
+    inner, partners = lax.optimization_barrier((inner, partners))
+    halves = []
+    for arrived in partners:
+        partner = functools.reduce(jnp.add, arrived)
+        halves += [partner, swapped(partner, "seq", 0)]
     attn, sums, held = call(
         functools.partial(cross_kernel, sizes),
         (
@@ -286,33 +341,33 @@
             shape((2, length), F32),
             shape((bits, heads, width, width), BF16),
         ),
-        (core_arg, inner, qd, gg, weights, near, *halves),
-        [SMEM] + [VMEM] * (5 + len(halves)),
+        (place_arg, inner, qd, gg, weights, near, *halves, diag),
+        [SMEM] + [VMEM] * (6 + len(halves)),
         flops=2 * bits * heads * length * width * width,
         name="cross",
     )
     features = heads * width * lax.axis_size("heads")
     parts = summands(sums, "heads")
-    attn_grad, inverse, grads = call(
+    attn_grad, inverse, first, keep, send = call(
         functools.partial(grad_kernel, sizes, features),
         (
             shape((heads, length, width), BF16),
             shape((1, length), F32),
-            shape((bits, heads, width, width), F32),
-        ),
-        (attn, gg, qd, weights, *parts),
-        [VMEM] * (4 + len(parts)),
-        [pltpu.VMEM((heads, length, bits * width), BF16)],
+            shape((heads, width, width), F32),
+            shape((bits - 1, half, width, width), F32),
+            shape((bits - 1, half, width, width), F32),
+        ),
+        (place_arg, attn, gg, qd, weights, *parts),
+        [SMEM] + [VMEM] * (4 + len(parts)),
+        [
+            pltpu.VMEM((heads, length, bits * width), BF16),
+            pltpu.VMEM((bits - 1, heads, width, width), F32),
+        ],
         flops=2 * bits * heads * length * width * width,
         name="state_grads",
     )
-    upper = grads[1:]
-    gathered = pick(upper, core) + swapped(pick(upper, 1 - core), "seq", 0)
-    back_near = swapped(grads[0], "seq", 0)
-    total = jnp.zeros((half, width, width), F32)
-    for place in reversed(range(1, bits)):
-        total = total + swapped(total + gathered[place - 1], "seq", place)
-    other = swapped(total, "seq", 0)
+    gathered = keep + swapped(send, "seq", 0)
+    back_near = swapped(first, "seq", 0)
 
     normed, query_grad, key_part, value_part = call(
         functools.partial(local_backward, sizes),
@@ -328,10 +383,17 @@
         flops=8 * local_flops,
         name="local_backward",
     )
+    total = jnp.zeros((half, width, width), F32)
+    for place in reversed(range(1, bits)):
+        total = total + swapped(total + gathered[place - 1], "seq", place)
+        if place == bits - 1:
+            total, key_part = lax.optimization_barrier((total, key_part))
+    other = swapped(total, "seq", 0)
+
     key_grad, value_grad = call(
         functools.partial(final_kernel, (heads, length, block)),
         (shape((rows, width), F32), shape((rows, width), F32)),
-        (core_arg, back_near, total, other, kd, vd, key_part, value_part),
+        (place_arg, back_near, total, other, kd, vd, key_part, value_part),
         [SMEM] + [VMEM] * 7,
         [pltpu.VMEM((heads, width, width), F32)],
         flops=4 * heads * length * width * width,

time: 45.5 us -> 42.6 us (0.936)
  local copies, waits for them, and re-layouts: 3.83 us -> 0.69 us
  starting transfers between devices: 15 us -> 12.8 us
  waiting for transfers between devices: 15.8 us -> 17.9 us
  Pallas kernels: 7.62 us -> 8.73 us
    ppermute x10 -> x8, starting transfers between devices: 11.5 us -> 2.8 us  [swapped(): return lax.ppermute(block, axis, route)]
    ppermute x0 -> x3, starting transfers between devices: none -> 6.46 us  [exchanged(): lax.ppermute(block, axis, route)]
    unnamed x22 -> x14, local copies, waits for them, and re-layouts: 3.7 us -> 0.68 us
    ppermute x0 -> x3, waiting for transfers between devices: none -> 2.59 us  [exchanged(): lax.ppermute(block, axis, route)]
    pallas_call x5, Pallas kernels: 7.62 us -> 8.73 us  [call(): pl.pallas_call(kernel, out_shape=out_shape, in_specs=specs, out_specs=jax...]
    ppermute x10 -> x8, waiting for transfers between devices: 11.6 us -> 11.1 us  [swapped(): return lax.ppermute(block, axis, route)]
  transfers between devices with their start and end apart: 13 -> 14, of which waited for: 9 -> 12; matrix products, arithmetic and copies ran while one was open for 1% -> 0% of each run, Pallas kernels for 10% -> 13%
where the time goes in v2:
time: 42.6 us; the launch traced here: 42.4 us
  waiting for transfers between devices  17.9 us (42%)
  starting transfers between devices  12.8 us (30%)
  Pallas kernels  8.73 us (20%)
  matrix products  1.37 us (3%)
  between operations  0.8 us (2%)
  local copies, waits for them, and re-layouts  0.69 us (2%)
    ppermute x8, waiting for transfers between devices, swapped(): return lax.ppermute(block, axis, route)  11.1 us
    pallas_call x5, Pallas kernels, call(): pl.pallas_call(kernel, out_shape=out_shape, in_specs=specs, out_specs=jax...  8.73 us
    ppermute x3, starting transfers between devices, exchanged(): lax.ppermute(block, axis, route)  6.46 us
    ppermute x3, waiting for transfers between devices, summands(): result.append(lax.ppermute(block, axis, route))  4.23 us
    ppermute x3, starting transfers between devices, summands(): result.append(lax.ppermute(block, axis, route))  3.55 us
    ppermute x8, starting transfers between devices, swapped(): return lax.ppermute(block, axis, route)  2.8 us
    ppermute x3, waiting for transfers between devices, exchanged(): lax.ppermute(block, axis, route)  2.59 us
    dot_general x1, matrix products, shards(): jnp.einsum('shd,she->hde', key_rows, value_rows, preferred_element_type=F32)  1.37 us
  transfers between devices with their start and end apart: 14, of which 12 were waited for; matrix products, arithmetic and copies ran while one was open for 0% of the time, Pallas kernels for 13%

profile of v2, /device:TPU:0, one launch (start us, length us, event | category | flops | bytes accessed | tf_op | source)
XLA Modules:
  0.0 42.4 jit_solution(18099439096272593381)
XLA Ops:
  0.6 0.0 copy-start.1
  0.6 0.0 copy-start.2
  0.7 0.0 copy-start.3
  0.7 1.4 %fusion = f32[2,128,128]{2,1,0:T(8,128)S(1)} fusion(bf16[512,2,128]{2,1,0:T(2,128)(2,1)} %param.9, bf16[512,2,128]{2,1,0:T(2,128)(2,1)} %param.8), kind=kOutput, calls=%fused_computation | convolution fusion | flops 33554432 | bytes 655360 | tf_op jit(solution)/shard_map/shd,she->hde/dot_general | solution.py:283
  2.0 0.0 copy-start
  2.0 0.5 %collective-permute-start = (f32[2,128,128]{2,1,0:T(8,128)S(1)}, f32[2,128,128]{2,1,0:T(8,128)S(1)}, u32[]{:S(2)}, u32[]{:S(2)}) collective-permute-start(f32[2,128,128]{2,1,0:T(8,128)S(1)} %fusion), channel_id=1, source_target_pairs={{0,1},{1,0},{2,3},{3,2},{4,5},{5,4},{6,7},{7,6},{8,9},{9,8},{10,11... | collective-permute-start | bytes 393224 | tf_op jit(solution)/shard_map/ppermute | solution.py:33
  2.6 1.0 %collective-permute-done.refs_5_ = f32[2,128,128]{2,1,0:T(8,128)S(1)} collective-permute-done((f32[2,128,128]{2,1,0:T(8,128)S(1)}, f32[2,128,128]{2,1,0:T(8,128)S(1)}, u32[]{:S(2)}, u32[]{:S(2)}) %collective-permute-start) | collective-permute-done | bytes 131104 | tf_op jit(solution)/shard_map/ppermute | solution.py:33
  3.6 4.8 %collective-permute-start.1 = (f32[1,128,128]{2,1,0:T(8,128)S(1)}, f32[1,128,128]{2,1,0:T(8,128)S(1)}, u32[]{:S(2)}, u32[]{:S(2)}) collective-permute-start(f32[1,128,128]{2,1,0:T(8,128)S(1)} %dynamic-slice_add_fusion), channel_id=1, source_target_pairs={{0,2},{2,0},{1,3},{3,1},{8,10},{10,8},{9,11},{11,9},{16,18},{18,16... | collective-permute-start | bytes 196616 | tf_op jit(solution)/shard_map/ppermute | solution.py:46
  8.4 0.7 %collective-permute-start.2 = (f32[1,128,128]{2,1,0:T(8,128)S(1)}, f32[1,128,128]{2,1,0:T(8,128)S(1)}, u32[]{:S(2)}, u32[]{:S(2)}) collective-permute-start(f32[1,128,128]{2,1,0:T(8,128)S(1)} %dynamic-slice_add_fusion), channel_id=1, source_target_pairs={{4,6},{6,4},{5,7},{7,5},{12,14},{14,12},{13,15},{15,13},{20,22},{2... | collective-permute-start | bytes 196616 | tf_op jit(solution)/shard_map/ppermute | solution.py:46
  9.1 1.7 %collective-permute-done.1 = f32[1,128,128]{2,1,0:T(8,128)S(1)} collective-permute-done((f32[1,128,128]{2,1,0:T(8,128)S(1)}, f32[1,128,128]{2,1,0:T(8,128)S(1)}, u32[]{:S(2)}, u32[]{:S(2)}) %collective-permute-start.1) | collective-permute-done | bytes 65568 | tf_op jit(solution)/shard_map/ppermute | solution.py:46
  10.8 0.0 copy-start.4
  10.8 1.0 %collective-permute-start.3 = (f32[1,128,128]{2,1,0:T(8,128)S(1)}, f32[1,128,128]{2,1,0:T(8,128)S(1)}, u32[]{:S(2)}, u32[]{:S(2)}) collective-permute-start(f32[1,128,128]{2,1,0:T(8,128)S(1)} %add.19), channel_id=1, source_target_pairs={{0,4},{4,0},{1,5},{5,1},{2,6},{6,2},{3,7},{7,3},{8,12},{12,8},{9,1... | collective-permute-start | bytes 196616 | tf_op jit(solution)/shard_map/ppermute | solution.py:46
  11.8 0.0 copy-start.6
  11.8 0.0 copy-start.5
  11.8 0.0 copy-done.1
  11.8 0.0 copy-done.2
  11.8 0.0 copy-done.3
  11.8 0.0 copy-done
  11.8 0.0 copy-done.4
  11.8 0.6 %copy-done.6 = s32[512]{0:T(512)S(1)} copy-done((s32[512]{0:T(512)S(1)}, s32[512]{0:T(512)}, u32[]{:S(2)}) %copy-start.6) | copy-done | bytes 2072
  12.5 0.0 copy-done.5
  12.5 2.8 %local_forward.1 = (f32[2,512,128]{2,1,0:T(8,128)S(1)}, bf16[2,512,512]{2,1,0:T(8,128)(2,1)S(1)}, f32[8,128,128]{2,1,0:T(8,128)S(1)}, bf16[2,512,128]{2,1,0:T(8,...) custom-call(s32[1]{0:T(128)} %bitcast.position_ref.refs_0_.core_ref,, ...), custom_call_target="tpu_custom_call" | custom-call | flops 268435456 | bytes 1052484 | tf_op jit(solution)/shard_map/local_forward/pallas_call | solution.py:62
  15.2 0.0 collective-permute-done.2
  15.3 0.9 %collective-permute-done.3.refs_8_ = f32[1,128,128]{2,1,0:T(8,128)S(1)} collective-permute-done((f32[1,128,128]{2,1,0:T(8,128)S(1)}, f32[1,128,128]{2,1,0:T(8,128)S(1)}, u32[]{:S(2)}, u32[]{:S(2)}) %collective-permute-start.3) | collective-permute-done | bytes 65568 | tf_op jit(solution)/shard_map/ppermute | solution.py:46
  16.1 0.1 collective-permute-start.4
  16.2 0.5 %collective-permute-start.5 = (f32[1,128,128]{2,1,0:T(8,128)S(1)}, f32[1,128,128]{2,1,0:T(8,128)S(1)}, u32[]{:S(2)}, u32[]{:S(2)}) collective-permute-start(f32[1,128,128]{2,1,0:T(8,128)S(1)} %collective-permute-done.3.refs_8_), channel_id=1, source_target_pairs={{0,1},{1,0},{2,3},{3,2},{4,5},{5,4},{6,7},{7,6},{8,9},{9,8},{10,11... | collective-permute-start | bytes 196616 | tf_op jit(solution)/shard_map/ppermute | solution.py:33
  16.7 0.7 %collective-permute-done.4.refs_7_ = f32[1,128,128]{2,1,0:T(8,128)S(1)} collective-permute-done((f32[1,128,128]{2,1,0:T(8,128)S(1)}, f32[1,128,128]{2,1,0:T(8,128)S(1)}, u32[]{:S(2)}, u32[]{:S(2)}) %collective-permute-start.4) | collective-permute-done | bytes 65568 | tf_op jit(solution)/shard_map/ppermute | solution.py:33
  17.5 0.2 collective-permute-done.5.refs_9_
  17.6 0.8 %cross.1 = (f32[2,512,128]{2,1,0:T(8,128)S(1)}, f32[2,512]{1,0:T(2,128)S(1)}, bf16[3,2,128,128]{3,2,1,0:T(8,128)(2,1)S(1)}) custom-call(s32[1]{0:T(128)} %bitcast.position_ref.refs_0_.core_ref, f32[2,512,128]{2,1,0:T(8,128)S(1)} %get-tuple-element.33.refs_1_, bf16[2,512,128]{2,1,0:T(8,128)(2,1)S(1)} %get-tuple-element.34.refs_2_.refs_3_.qd_ref, ...), custom_call_target="tpu_custom_call" | custom-call | flops 100663296 | bytes 2281476 | tf_op jit(solution)/shard_map/cross/pallas_call | solution.py:62
  18.4 1.8 %collective-permute-start.6 = (f32[2,512]{1,0:T(2,128)S(1)}, f32[2,512]{1,0:T(2,128)S(1)}, u32[]{:S(2)}, u32[]{:S(2)}) collective-permute-start(f32[2,512]{1,0:T(2,128)S(1)} %get-tuple-element.42.refs_5_), channel_id=1, source_target_pairs={{0,8},{8,0},{16,24},{24,16},{1,9},{9,1},{17,25},{25,17},{2,10},{10... | collective-permute-start | bytes 12296 | tf_op jit(solution)/shard_map/ppermute | solution.py:57
  20.2 1.5 %collective-permute-start.7 = (f32[2,512]{1,0:T(2,128)S(1)}, f32[2,512]{1,0:T(2,128)S(1)}, u32[]{:S(2)}, u32[]{:S(2)}) collective-permute-start(f32[2,512]{1,0:T(2,128)S(1)} %get-tuple-element.42.refs_5_), channel_id=1, source_target_pairs={{0,16},{8,24},{16,0},{24,8},{1,17},{9,25},{17,1},{25,9},{2,18},{10... | collective-permute-start | bytes 12296 | tf_op jit(solution)/shard_map/ppermute | solution.py:57
  21.7 0.3 collective-permute-start.8
  22.0 0.1 collective-permute-done.6.refs_6_
  22.1 1.7 %collective-permute-done.7.refs_7_ = f32[2,512]{1,0:T(2,128)S(1)} collective-permute-done((f32[2,512]{1,0:T(2,128)S(1)}, f32[2,512]{1,0:T(2,128)S(1)}, u32[]{:S(2)}, u32[]{:S(2)}) %collective-permute-start.7) | collective-permute-done | bytes 4128 | tf_op jit(solution)/shard_map/ppermute | solution.py:57
  23.8 2.4 %collective-permute-done.8.refs_8_ = f32[2,512]{1,0:T(2,128)S(1)} collective-permute-done((f32[2,512]{1,0:T(2,128)S(1)}, f32[2,512]{1,0:T(2,128)S(1)}, u32[]{:S(2)}, u32[]{:S(2)}) %collective-permute-start.8) | collective-permute-done | bytes 4128 | tf_op jit(solution)/shard_map/ppermute | solution.py:57
  26.2 1.0 %state_grads.1 = (bf16[2,512,128]{2,1,0:T(8,128)(2,1)S(1)}, f32[1,512]{1,0:T(1,128)S(1)}, f32[2,128,128]{2,1,0:T(8,128)S(1)}, f32[2,1,128,128]{3,2,1,0:T(8,128)S(1)}, f32[2,1,128,128]{3,2,1,0:T(8,128)S(1)}) custom-call(s32[1]{0:T(128)} %bitcast.position_ref.refs_0_.core_ref, f32[2,512,128]{2,1,0:T(8,128)S(1)} %get-tuple-element.41.refs_1_.attn_ref, ...), custom_call_target="tpu_custom_call" | custom-call | flops 100663296 | bytes 1380356 | tf_op jit(solution)/shard_map/state_grads/pallas_call | solution.py:62
  27.3 0.1 collective-permute-start.10
  27.3 1.3 %collective-permute-done.10 = f32[2,1,128,128]{3,2,1,0:T(8,128)S(1)} collective-permute-done((f32[2,1,128,128]{3,2,1,0:T(8,128)S(1)}, f32[2,1,128,128]{3,2,1,0:T(8,128)S(1)}, u32[]{:S(2)}, u32[]{:S(2)}) %collective-permute-start.10) | collective-permute-done | bytes 131104 | tf_op jit(solution)/shard_map/ppermute | solution.py:33
  28.7 1.3 %collective-permute-start.11 = (f32[1,128,128]{2,1,0:T(8,128)S(1)}, f32[1,128,128]{2,1,0:T(8,128)S(1)}, u32[]{:S(2)}, u32[]{:S(2)}) collective-permute-start(f32[1,128,128]{2,1,0:T(8,128)S(1)} %slice_bitcast_fusion.1), channel_id=1, source_target_pairs={{0,4},{4,0},{1,5},{5,1},{2,6},{6,2},{3,7},{7,3},{8,12},{12,8},{9,1... | collective-permute-start | bytes 196616 | tf_op jit(solution)/shard_map/ppermute | solution.py:33
  30.0 2.8 %local_backward.1 = (f32[1024,128]{1,0:T(8,128)}, f32[1024,128]{1,0:T(8,128)}, f32[2,512,128]{2,1,0:T(8,128)S(1)}, f32[2,512,128]{2,1,0:T(8,128)S(1)}) custom-call(bf16[2,512,128]{2,1,0:T(8,128)(2,1)S(1)} %get-tuple-element.43.ag_ref, bf16[2,512,128]{2,1,0:T(8,128)(2,1)S(1)} %get-tuple-element.34.refs_2_.refs_3_.qd_ref, ...), custom_call_target="tpu_custom_call" | custom-call | flops 536870912 | bytes 3398656 | tf_op jit(solution)/shard_map/local_backward/pallas_call | solution.py:62
  32.8 2.6 %collective-permute-done.11 = f32[1,128,128]{2,1,0:T(8,128)S(1)} collective-permute-done((f32[1,128,128]{2,1,0:T(8,128)S(1)}, f32[1,128,128]{2,1,0:T(8,128)S(1)}, u32[]{:S(2)}, u32[]{:S(2)}) %collective-permute-start.11) | collective-permute-done | bytes 65568 | tf_op jit(solution)/shard_map/ppermute | solution.py:33
  35.4 0.3 collective-permute-start.12
  35.6 0.0 collective-permute-start.9
  35.6 4.1 %collective-permute-done.12 = f32[1,128,128]{2,1,0:T(8,128)S(1)} collective-permute-done((f32[1,128,128]{2,1,0:T(8,128)S(1)}, f32[1,128,128]{2,1,0:T(8,128)S(1)}, u32[]{:S(2)}, u32[]{:S(2)}) %collective-permute-start.12) | collective-permute-done | bytes 65568 | tf_op jit(solution)/shard_map/ppermute | solution.py:33
  39.7 0.1 collective-permute-start.13
  39.8 0.0 collective-permute-done.9.near_ref
  39.8 1.2 %collective-permute-done.13.other_ref = f32[1,128,128]{2,1,0:T(8,128)S(1)} collective-permute-done((f32[1,128,128]{2,1,0:T(8,128)S(1)}, f32[1,128,128]{2,1,0:T(8,128)S(1)}, u32[]{:S(2)}, u32[]{:S(2)}) %collective-permute-start.13) | collective-permute-done | bytes 65568 | tf_op jit(solution)/shard_map/ppermute | solution.py:33
  41.0 1.4 %key_value_grads.1 = (f32[1024,128]{1,0:T(8,128)}, f32[1024,128]{1,0:T(8,128)}) custom-call(s32[1]{0:T(128)} %bitcast.position_ref.refs_0_.core_ref, f32[2,128,128]{2,1,0:T(8,128)S(1)} %collective-permute-done.9.near_ref, f32[1,128,128]{2,1,0:T(8,128)S(1)} %add.23.mine_ref, f32[1,128,128]{2,1,0:T(8,128)S(1)} %collective-permute-done.13.other_ref, ...), custom_call_target="tpu_custom_call" | custom-call | flops 67108864 | bytes 1835012 | tf_op jit(solution)/shard_map/key_value_grads/pallas_call | solution.py:62
  (7 shorter events, 0.1 us)
Async XLA Ops:
  0.6 11.2 %copy-start.1 = (bf16[512,2,128]{2,1,0:T(2,128)(2,1)S(1)}, bf16[512,2,128]{2,1,0:T(2,128)(2,1)}, u32[]{:S(2)}) copy-start(bf16[512,2,128]{2,1,0:T(2,128)(2,1)} %param.9) | copy-start | bytes 786436
  0.6 11.2 %copy-start.2 = (bf16[512,2,128]{2,1,0:T(2,128)(2,1)S(1)}, bf16[512,2,128]{2,1,0:T(2,128)(2,1)}, u32[]{:S(2)}) copy-start(bf16[512,2,128]{2,1,0:T(2,128)(2,1)} %param.7) | copy-start | bytes 786436
  0.7 11.1 %copy-start.3 = (bf16[512,2,128]{2,1,0:T(2,128)(2,1)S(1)}, bf16[512,2,128]{2,1,0:T(2,128)(2,1)}, u32[]{:S(2)}) copy-start(bf16[512,2,128]{2,1,0:T(2,128)(2,1)} %param.13) | copy-start | bytes 786436
  2.0 9.8 %copy-start = (bf16[512,2,128]{2,1,0:T(2,128)(2,1)S(1)}, bf16[512,2,128]{2,1,0:T(2,128)(2,1)}, u32[]{:S(2)}) copy-start(bf16[512,2,128]{2,1,0:T(2,128)(2,1)} %param.8) | copy-start | bytes 786436
  2.0 1.5 %collective-permute-start = (f32[2,128,128]{2,1,0:T(8,128)S(1)}, f32[2,128,128]{2,1,0:T(8,128)S(1)}, u32[]{:S(2)}, u32[]{:S(2)}) collective-permute-start(f32[2,128,128]{2,1,0:T(8,128)S(1)} %fusion), channel_id=1, source_target_pairs={{0,1},{1,0},{2,3},{3,2},{4,5},{5,4},{6,7},{7,6},{8,9},{9,8},{10,11... | collective-permute-start | bytes 393224 | tf_op jit(solution)/shard_map/ppermute | solution.py:33
  3.6 7.2 %collective-permute-start.1 = (f32[1,128,128]{2,1,0:T(8,128)S(1)}, f32[1,128,128]{2,1,0:T(8,128)S(1)}, u32[]{:S(2)}, u32[]{:S(2)}) collective-permute-start(f32[1,128,128]{2,1,0:T(8,128)S(1)} %dynamic-slice_add_fusion), channel_id=1, source_target_pairs={{0,2},{2,0},{1,3},{3,1},{8,10},{10,8},{9,11},{11,9},{16,18},{18,16... | collective-permute-start | bytes 196616 | tf_op jit(solution)/shard_map/ppermute | solution.py:46
  8.4 6.8 %collective-permute-start.2 = (f32[1,128,128]{2,1,0:T(8,128)S(1)}, f32[1,128,128]{2,1,0:T(8,128)S(1)}, u32[]{:S(2)}, u32[]{:S(2)}) collective-permute-start(f32[1,128,128]{2,1,0:T(8,128)S(1)} %dynamic-slice_add_fusion), channel_id=1, source_target_pairs={{4,6},{6,4},{5,7},{7,5},{12,14},{14,12},{13,15},{15,13},{20,22},{2... | collective-permute-start | bytes 196616 | tf_op jit(solution)/shard_map/ppermute | solution.py:46
  10.8 1.0 %copy-start.4 = (f32[8,2,13]{2,1,0:T(2,128)S(1)}, f32[8,2,13]{2,1,0:T(2,128)}, u32[]{:S(2)}) copy-start(f32[8,2,13]{2,1,0:T(2,128)} %table_ref.1) | copy-start | bytes 2500
  10.8 5.3 %collective-permute-start.3 = (f32[1,128,128]{2,1,0:T(8,128)S(1)}, f32[1,128,128]{2,1,0:T(8,128)S(1)}, u32[]{:S(2)}, u32[]{:S(2)}) collective-permute-start(f32[1,128,128]{2,1,0:T(8,128)S(1)} %add.19), channel_id=1, source_target_pairs={{0,4},{4,0},{1,5},{5,1},{2,6},{6,2},{3,7},{7,3},{8,12},{12,8},{9,1... | collective-permute-start | bytes 196616 | tf_op jit(solution)/shard_map/ppermute | solution.py:46
  11.8 0.7 %copy-start.6 = (s32[512]{0:T(512)S(1)}, s32[512]{0:T(512)}, u32[]{:S(2)}) copy-start(s32[512]{0:T(512)} %param.10) | copy-start | bytes 6148
  11.8 0.7 %copy-start.5 = (f32[2,128]{1,0:T(2,128)S(1)}, f32[2,128]{1,0:T(2,128)}, u32[]{:S(2)}) copy-start(f32[2,128]{1,0:T(2,128)} %gain_ref.1) | copy-start | bytes 3076
  16.1 1.3 %collective-permute-start.4 = (f32[1,128,128]{2,1,0:T(8,128)S(1)}, f32[1,128,128]{2,1,0:T(8,128)S(1)}, u32[]{:S(2)}, u32[]{:S(2)}) collective-permute-start(f32[1,128,128]{2,1,0:T(8,128)S(1)} %add.20.refs_6_), channel_id=1, source_target_pairs={{0,1},{1,0},{2,3},{3,2},{4,5},{5,4},{6,7},{7,6},{8,9},{9,8},{10,11... | collective-permute-start | bytes 196616 | tf_op jit(solution)/shard_map/ppermute | solution.py:33
  16.2 1.4 %collective-permute-start.5 = (f32[1,128,128]{2,1,0:T(8,128)S(1)}, f32[1,128,128]{2,1,0:T(8,128)S(1)}, u32[]{:S(2)}, u32[]{:S(2)}) collective-permute-start(f32[1,128,128]{2,1,0:T(8,128)S(1)} %collective-permute-done.3.refs_8_), channel_id=1, source_target_pairs={{0,1},{1,0},{2,3},{3,2},{4,5},{5,4},{6,7},{7,6},{8,9},{9,8},{10,11... | collective-permute-start | bytes 196616 | tf_op jit(solution)/shard_map/ppermute | solution.py:33
  18.4 3.7 %collective-permute-start.6 = (f32[2,512]{1,0:T(2,128)S(1)}, f32[2,512]{1,0:T(2,128)S(1)}, u32[]{:S(2)}, u32[]{:S(2)}) collective-permute-start(f32[2,512]{1,0:T(2,128)S(1)} %get-tuple-element.42.refs_5_), channel_id=1, source_target_pairs={{0,8},{8,0},{16,24},{24,16},{1,9},{9,1},{17,25},{25,17},{2,10},{10... | collective-permute-start | bytes 12296 | tf_op jit(solution)/shard_map/ppermute | solution.py:57
  20.2 3.6 %collective-permute-start.7 = (f32[2,512]{1,0:T(2,128)S(1)}, f32[2,512]{1,0:T(2,128)S(1)}, u32[]{:S(2)}, u32[]{:S(2)}) collective-permute-start(f32[2,512]{1,0:T(2,128)S(1)} %get-tuple-element.42.refs_5_), channel_id=1, source_target_pairs={{0,16},{8,24},{16,0},{24,8},{1,17},{9,25},{17,1},{25,9},{2,18},{10... | collective-permute-start | bytes 12296 | tf_op jit(solution)/shard_map/ppermute | solution.py:57
  21.7 4.5 %collective-permute-start.8 = (f32[2,512]{1,0:T(2,128)S(1)}, f32[2,512]{1,0:T(2,128)S(1)}, u32[]{:S(2)}, u32[]{:S(2)}) collective-permute-start(f32[2,512]{1,0:T(2,128)S(1)} %get-tuple-element.42.refs_5_), channel_id=1, source_target_pairs={{0,24},{8,16},{16,8},{24,0},{1,25},{9,17},{17,9},{25,1},{2,26},{10... | collective-permute-start | bytes 12296 | tf_op jit(solution)/shard_map/ppermute | solution.py:57
  27.3 1.4 %collective-permute-start.10 = (f32[2,1,128,128]{3,2,1,0:T(8,128)S(1)}, f32[2,1,128,128]{3,2,1,0:T(8,128)S(1)}, u32[]{:S(2)}, u32[]{:S(2)}) collective-permute-start(f32[2,1,128,128]{3,2,1,0:T(8,128)S(1)} %get-tuple-element.53), channel_id=1, source_target_pairs={{0,1},{1,0},{2,3},{3,2},{4,5},{5,4},{6,7},{7,6},{8,9},{9,8},{10,11... | collective-permute-start | bytes 393224 | tf_op jit(solution)/shard_map/ppermute | solution.py:33
  28.7 6.6 %collective-permute-start.11 = (f32[1,128,128]{2,1,0:T(8,128)S(1)}, f32[1,128,128]{2,1,0:T(8,128)S(1)}, u32[]{:S(2)}, u32[]{:S(2)}) collective-permute-start(f32[1,128,128]{2,1,0:T(8,128)S(1)} %slice_bitcast_fusion.1), channel_id=1, source_target_pairs={{0,4},{4,0},{1,5},{5,1},{2,6},{6,2},{3,7},{7,3},{8,12},{12,8},{9,1... | collective-permute-start | bytes 196616 | tf_op jit(solution)/shard_map/ppermute | solution.py:33
  35.4 4.3 %collective-permute-start.12 = (f32[1,128,128]{2,1,0:T(8,128)S(1)}, f32[1,128,128]{2,1,0:T(8,128)S(1)}, u32[]{:S(2)}, u32[]{:S(2)}) collective-permute-start(f32[1,128,128]{2,1,0:T(8,128)S(1)} %fusion.3), channel_id=1, source_target_pairs={{0,2},{2,0},{1,3},{3,1},{4,6},{6,4},{5,7},{7,5},{8,10},{10,8},{9,1... | collective-permute-start | bytes 196616 | tf_op jit(solution)/shard_map/ppermute | solution.py:33
  35.6 4.2 %collective-permute-start.9 = (f32[2,128,128]{2,1,0:T(8,128)S(1)}, f32[2,128,128]{2,1,0:T(8,128)S(1)}, u32[]{:S(2)}, u32[]{:S(2)}) collective-permute-start(f32[2,128,128]{2,1,0:T(8,128)S(1)} %get-tuple-element.51), channel_id=1, source_target_pairs={{0,1},{1,0},{2,3},{3,2},{4,5},{5,4},{6,7},{7,6},{8,9},{9,8},{10,11... | collective-permute-start | bytes 393224 | tf_op jit(solution)/shard_map/ppermute | solution.py:33
  39.7 1.3 %collective-permute-start.13 = (f32[1,128,128]{2,1,0:T(8,128)S(1)}, f32[1,128,128]{2,1,0:T(8,128)S(1)}, u32[]{:S(2)}, u32[]{:S(2)}) collective-permute-start(f32[1,128,128]{2,1,0:T(8,128)S(1)} %add.23.mine_ref), channel_id=1, source_target_pairs={{0,1},{1,0},{2,3},{3,2},{4,5},{5,4},{6,7},{7,6},{8,9},{9,8},{10,11... | collective-permute-start | bytes 196616 | tf_op jit(solution)/shard_map/ppermute | solution.py:33

commit v3 on v2

--- a/solution.py
+++ b/solution.py
@@ -58,12 +58,12 @@
     return result
 
 
-def call(kernel, out_shape, args, specs, scratch=(), flops=0, name=None):
+def call(kernel, out_shape, args, specs, scratch=(), flops=0, name=None, outs=VMEM):
     return pl.pallas_call(
         kernel,
         out_shape=out_shape,
         in_specs=specs,
-        out_specs=jax.tree.map(lambda _: VMEM, out_shape),
+        out_specs=jax.tree.map(lambda _: outs, out_shape),
         scratch_shapes=list(scratch),
         compiler_params=pltpu.CompilerParams(vmem_limit_bytes=16 << 20),
         cost_estimate=pl.CostEstimate(
@@ -142,80 +142,140 @@
             inner_ref[head, rows, :] = dot(p_ref[head, rows, reach], vd_ref[head, reach, :], NN)
 
 
-def join(core_ref, mine_ref, other_ref, target_ref, first, lead=None):
-    half = mine_ref.shape[-3]
-    core = (core_ref[0] & 1)
-    for h in range(half):
-        for source, start in ((mine_ref, core * half), (other_ref, (1 - core) * half)):
-            if lead is None:
-                target_ref[start + h] = source[h].astype(target_ref.dtype)
-            else:
-                target_ref[first, start + h] = source[h].astype(target_ref.dtype)
-
-
-def cross_kernel(sizes, *refs):
-    heads, length, levels, block, bits = sizes
-    core_ref, inner_ref, qd_ref, gg_ref, tw_ref, near_ref = refs[:6]
-    halves = refs[6:6 + 2 * (bits - 1)]
-    attn_ref, sums_ref, held_ref = refs[-3:]
-    held_ref[0] = near_ref[...].astype(BF16)
-    for j in range(1, bits):
-        join(core_ref, halves[2 * j - 2], halves[2 * j - 1], held_ref, j, lead=True)
+def cross_heads(sizes, heads_at, held_at, inner_ref, qd_ref, gg_ref, tw_ref, attn_ref, sums_ref, add=None):
+    _, length, levels, block, bits = sizes
     for i in range(length // block):
         rows = slice(i * block, (i + 1) * block)
         squares = 0.0
         products = 0.0
-        for head in range(heads):
+        for h, head in enumerate(heads_at):
             total = inner_ref[head, rows, :]
             query = qd_ref[head, rows, :]
             for j in range(bits):
                 at = levels - bits + j
-                total = total + tw_ref[head, rows, at:at + 1] * dot(query, held_ref[j, head], NN)
-            attn_ref[head, rows, :] = total
+                total = total + tw_ref[head, rows, at:at + 1] * dot(query, held_at(j, h), NN)
+            attn_ref[h, rows, :] = total
             squares = squares + total * total
             products = products + total * gg_ref[head, rows, :]
-        sums_ref[0:1, rows] = jnp.sum(squares.T, axis=0, keepdims=True)
-        sums_ref[1:2, rows] = jnp.sum(products.T, axis=0, keepdims=True)
+        both = (squares, products)
+        for n in range(2):
+            row = jnp.sum(both[n].T, axis=0, keepdims=True)
+            if add is not None:
+                row = row + add[n:n + 1, rows]
+            sums_ref[n:n + 1, rows] = row
+
+
+def cross_mine(sizes, *refs):
+    heads, length, levels, block, bits = sizes
+    position_ref, inner_ref, qd_ref, gg_ref, tw_ref, near_ref = refs[:6]
+    mine = refs[6:6 + bits - 1]
+    attn_ref, sums_ref, held_ref = refs[-3:]
+    half = heads // 2
+    start = (position_ref[0] & 1) * half
+    for h in range(half):
+        held_ref[0, h] = near_ref[start + h].astype(BF16)
+        for j in range(1, bits):
+            held_ref[j, h] = mine[j - 1][h].astype(BF16)
+    cross_heads(sizes, [start + h for h in range(half)], lambda j, h: held_ref[j, h],
+                inner_ref, qd_ref, gg_ref, tw_ref, attn_ref, sums_ref)
+
+
+def cross_other(sizes, *refs):
+    heads, length, levels, block, bits = sizes
+    position_ref, inner_ref, qd_ref, gg_ref, tw_ref, near_ref, add_ref = refs[:7]
+    other = refs[7:7 + bits - 1]
+    attn_ref, sums_ref, held_ref = refs[-3:]
+    half = heads // 2
+    start = (1 - (position_ref[0] & 1)) * half
+    for h in range(half):
+        held_ref[0, h] = near_ref[start + h].astype(BF16)
+        for j in range(1, bits):
+            held_ref[j, h] = other[j - 1][h].astype(BF16)
+    cross_heads(sizes, [start + h for h in range(half)], lambda j, h: held_ref[j, h],
+                inner_ref, qd_ref, gg_ref, tw_ref, attn_ref, sums_ref, add_ref)
 
 
 def spread(row, width):
     return jnp.broadcast_to(row, (width, row.shape[1])).T
 
 
-def grad_kernel(sizes, features, *refs):
-    heads, length, levels, block, bits = sizes
-    position_ref, attn_ref, gg_ref, qd_ref, tw_ref = refs[:5]
-    sums = refs[5:-7]
-    ag_ref, inverse_ref, first_ref, keep_ref, send_ref, scaled_ref, state_ref = refs[-7:]
-    width = attn_ref.shape[-1]
+def token_scales(features, sums):
     total = sums[0][...]
     for part in sums[1:]:
         total = total + part[...]
     inverse = lax.rsqrt(total[0:1] / features + epsilon)
-    beta = inverse * inverse * inverse * (total[1:2] / features)
+    return inverse, inverse * inverse * inverse * (total[1:2] / features)
+
+
+def grad_heads(sizes, heads_at, left_at, right_at, attn_ref, gg_ref, qd_ref, tw_ref, put_grad, scaled_ref, put_state):
+    _, length, levels, block, bits = sizes
+    width = attn_ref.shape[-1]
+    for h, head in enumerate(heads_at):
+        for i in range(length // block):
+            rows = slice(i * block, (i + 1) * block)
+            grad = (left_at(rows) * gg_ref[head, rows, :] - attn_ref[h, rows, :] * right_at(rows)).astype(BF16)
+            put_grad(h, rows, grad)
+            wide = grad.astype(F32)
+            for j in range(bits):
+                at = levels - bits + j
+                scaled_ref[rows, j * width:(j + 1) * width] = (tw_ref[head, rows, at:at + 1] * wide).astype(BF16)
+        product = dot(qd_ref[head], scaled_ref[...], TN)
+        for j in range(bits):
+            put_state(j, h, product[:, j * width:(j + 1) * width])
+
+
+def grad_other(sizes, features, *refs):
+    heads, length, levels, block, bits = sizes
+    position_ref, attn_ref, gg_ref, qd_ref, tw_ref = refs[:5]
+    sums = refs[5:-7]
+    ag_ref, inverse_ref, left_ref, right_ref, first_ref, send_ref, scaled_ref = refs[-7:]
+    half = heads // 2
+    start = (1 - (position_ref[0] & 1)) * half
+    width = attn_ref.shape[-1]
+    inverse, beta = token_scales(features, sums)
     inverse_ref[...] = inverse
     for i in range(length // block):
         rows = slice(i * block, (i + 1) * block)
-        left = spread(inverse[:, rows], width)
-        right = spread(beta[:, rows], width)
-        for head in range(heads):
-            grad = (left * gg_ref[head, rows, :] - attn_ref[head, rows, :] * right).astype(BF16)
-            ag_ref[head, rows, :] = grad
-            wide = grad.astype(F32)
-            for j in range(bits):
-                at = levels - bits + j
-                scaled_ref[head, rows, j * width:(j + 1) * width] = (tw_ref[head, rows, at:at + 1] * wide).astype(BF16)
-    for head in range(heads):
-        product = dot(qd_ref[head], scaled_ref[head], TN)
-        first_ref[head] = product[:, :width]
-        for j in range(1, bits):
-            state_ref[j - 1, head] = product[:, j * width:(j + 1) * width]
+        left_ref[rows, :] = spread(inverse[:, rows], width)
+        right_ref[rows, :] = spread(beta[:, rows], width)
+
+    def put_grad(h, rows, grad):
+        ag_ref[h, rows, :] = grad
+
+    def put_state(j, h, value):
+        if j == 0:
+            first_ref[h] = value
+        else:
+            send_ref[j - 1, h] = value
+    grad_heads(sizes, [start + h for h in range(half)], lambda rows: left_ref[rows, :], lambda rows: right_ref[rows, :],
+               attn_ref, gg_ref, qd_ref, tw_ref, put_grad, scaled_ref, put_state)
+
+
+def grad_mine(sizes, position_ref, attn_ref, far_ref, gg_ref, qd_ref, tw_ref, other_ref, left_ref, right_ref,
+              held_mine_ref, held_other_ref, ag_ref, first_ref, keep_ref, attn_full_ref, held_ref, scaled_ref):
+    heads, length, levels, block, bits = sizes
     half = heads // 2
     core = position_ref[0] & 1
-    for j in range(bits - 1):
-        for h in range(half):
-            keep_ref[j, h] = state_ref[j, core * half + h]
-            send_ref[j, h] = state_ref[j, (1 - core) * half + h]
+    start = core * half
+    away = (1 - core) * half
+
+    def put_grad(h, rows, grad):
+        ag_ref[start + h, rows, :] = grad
+
+    def put_state(j, h, value):
+        if j == 0:
+            first_ref[h] = value
+        else:
+            keep_ref[j - 1, h] = value
+    grad_heads(sizes, [start + h for h in range(half)], lambda rows: left_ref[rows, :], lambda rows: right_ref[rows, :],
+               attn_ref, gg_ref, qd_ref, tw_ref, put_grad, scaled_ref, put_state)
+    for h in range(half):
+        ag_ref[away + h] = other_ref[h]
+        attn_full_ref[start + h] = attn_ref[h]
+        attn_full_ref[away + h] = far_ref[h]
+        for j in range(bits):
+            held_ref[j, start + h] = held_mine_ref[j, h]
+            held_ref[j, away + h] = held_other_ref[j, h]
 
 
 def local_backward(sizes, ag_ref, qd_ref, kd_ref, vd_ref, p_ref, w_ref, tw_ref, held_ref, attn_ref,
@@ -254,18 +314,50 @@
             dv_ref[head, cols, :] = dot(p_ref[head, rest, cols], ag_ref[head, rest, :], TN)
 
 
-def final_kernel(sizes, core_ref, near_ref, mine_ref, other_ref, kd_ref, vd_ref, dk_ref, dv_ref,
-                 key_ref, value_ref, back_ref):
+def final_mine(sizes, position_ref, near_ref, total_ref, kd_ref, vd_ref, dk_ref, dv_ref, key_ref, value_ref):
     heads, length, block = sizes
-    join(core_ref, mine_ref, other_ref, back_ref, 0)
-    keep = (1 - (core_ref[0] & 1)).astype(F32)
-    for head in range(heads):
-        back = (back_ref[head] + keep * near_ref[head]).astype(BF16)
-        for i in range(length // block):
-            rows = slice(i * block, (i + 1) * block)
-            put = pl.ds(i * block * heads + head, block, stride=heads)
-            key_ref[put, :] = dk_ref[head, rows, :] + dot(vd_ref[head, rows, :], back, NT)
-            value_ref[put, :] = dv_ref[head, rows, :] + dot(kd_ref[head, rows, :], back, NN)
+    half = heads // 2
+    core = position_ref[0] & 1
+    keep = (1 - core).astype(F32)
+    for h in range(half):
+        head = core * half + h
+        back = (total_ref[h] + keep * near_ref[h]).astype(BF16)
+        key_ref[h] = dk_ref[head] + dot(vd_ref[head], back, NT)
+        value_ref[h] = dv_ref[head] + dot(kd_ref[head], back, NN)
+
+
+def final_other(sizes, position_ref, near_ref, total_ref, kd_ref, vd_ref, dk_ref, dv_ref, mine_key_ref, mine_value_ref,
+                key_hbm, value_hbm, back_ref, key_ref, value_ref, sems):
+    heads, length, block = sizes
+    half = heads // 2
+    core = position_ref[0] & 1
+    keep = (1 - core).astype(F32)
+    away = (1 - core) * half
+    for h in range(half):
+        back_ref[h] = (total_ref[h] + keep * near_ref[h]).astype(BF16)
+    copies = []
+    for i in range(length // block):
+        rows = slice(i * block, (i + 1) * block)
+        new = []
+        for h in range(half):
+            head = away + h
+            back = back_ref[h]
+            new.append((dk_ref[head, rows, :] + dot(vd_ref[head, rows, :], back, NT),
+                        dv_ref[head, rows, :] + dot(kd_ref[head, rows, :], back, NN)))
+        for h in range(half):
+            old = (mine_key_ref[h, rows, :], mine_value_ref[h, rows, :])
+            for n, target in enumerate((key_ref, value_ref)):
+                low = jnp.where(core == 0, old[n], new[h][n])
+                high = jnp.where(core == 0, new[h][n], old[n])
+                target[pl.ds(i * block * heads + h, block, stride=heads), :] = low
+                target[pl.ds(i * block * heads + half + h, block, stride=heads), :] = high
+        chunk = pl.ds(i * block * heads, block * heads)
+        for n, (source, target) in enumerate(((key_ref, key_hbm), (value_ref, value_hbm))):
+            copy = pltpu.make_async_copy(source.at[chunk], target.at[chunk], sems.at[n, i])
+            copy.start()
+            copies.append(copy)
+    for copy in copies:
+        copy.wait()
 
 
 def shards(query_rows, key_rows, value_rows, level_pick, level_table, norm_gain, out_grad):
@@ -330,44 +422,66 @@
         name="local_forward",
     )
     inner, partners = lax.optimization_barrier((inner, partners))
-    halves = []
-    for arrived in partners:
-        partner = functools.reduce(jnp.add, arrived)
-        halves += [partner, swapped(partner, "seq", 0)]
-    attn, sums, held = call(
-        functools.partial(cross_kernel, sizes),
+    mine = [functools.reduce(jnp.add, arrived) for arrived in partners]
+    others = [swapped(partner, "seq", 0) for partner in mine]
+    cross_flops = bits * heads * length * width * width
+    cross_shapes = (
+        shape((half, length, width), F32),
+        shape((2, length), F32),
+        shape((bits, half, width, width), BF16),
+    )
+    attn_mine, sums, held_mine = call(
+        functools.partial(cross_mine, sizes),
+        cross_shapes,
+        (place_arg, inner, qd, gg, weights, near, *mine),
+        [SMEM] + [VMEM] * (5 + len(mine)),
+        flops=cross_flops,
+        name="cross_mine",
+    )
+    attn_other, sums, held_other = call(
+        functools.partial(cross_other, sizes),
+        cross_shapes,
+        (place_arg, inner, qd, gg, weights, near, sums, *others),
+        [SMEM] + [VMEM] * (6 + len(others)),
+        flops=cross_flops,
+        name="cross_other",
+    )
+    features = heads * width * lax.axis_size("heads")
+    parts = summands(sums, "heads")
+    grad_far, inverse, left, right, first_other, send = call(
+        functools.partial(grad_other, sizes, features),
         (
+            shape((half, length, width), BF16),
+            shape((1, length), F32),
+            shape((length, width), F32),
+            shape((length, width), F32),
+            shape((half, width, width), F32),
+            shape((bits - 1, half, width, width), F32),
+        ),
+        (place_arg, attn_other, gg, qd, weights, *parts),
+        [SMEM] + [VMEM] * (4 + len(parts)),
+        [pltpu.VMEM((length, bits * width), BF16)],
+        flops=cross_flops,
+        name="state_grads_other",
+    )
+    attn_grad, first_mine, keep, attn, held = call(
+        functools.partial(grad_mine, sizes),
+        (
+            shape((heads, length, width), BF16),
+            shape((half, width, width), F32),
+            shape((bits - 1, half, width, width), F32),
             shape((heads, length, width), F32),
-            shape((2, length), F32),
             shape((bits, heads, width, width), BF16),
         ),
-        (place_arg, inner, qd, gg, weights, near, *halves, diag),
-        [SMEM] + [VMEM] * (6 + len(halves)),
-        flops=2 * bits * heads * length * width * width,
-        name="cross",
-    )
-    features = heads * width * lax.axis_size("heads")
-    parts = summands(sums, "heads")
-    attn_grad, inverse, first, keep, send = call(
-        functools.partial(grad_kernel, sizes, features),
-        (
-            shape((heads, length, width), BF16),
-            shape((1, length), F32),
-            shape((heads, width, width), F32),
-            shape((bits - 1, half, width, width), F32),
-            shape((bits - 1, half, width, width), F32),
-        ),
-        (place_arg, attn, gg, qd, weights, *parts),
-        [SMEM] + [VMEM] * (4 + len(parts)),
-        [
-            pltpu.VMEM((heads, length, bits * width), BF16),
-            pltpu.VMEM((bits - 1, heads, width, width), F32),
-        ],
-        flops=2 * bits * heads * length * width * width,
-        name="state_grads",
+        (place_arg, attn_mine, attn_other, gg, qd, weights, grad_far, left, right, held_mine, held_other),
+        [SMEM] + [VMEM] * 10,
+        [pltpu.VMEM((length, bits * width), BF16)],
+        flops=cross_flops,
+        name="state_grads_mine",
     )
     gathered = keep + swapped(send, "seq", 0)
-    back_near = swapped(first, "seq", 0)
+    near_other = swapped(first_mine, "seq", 0)
+    near_mine = swapped(first_other, "seq", 0)
 
     normed, query_grad, key_part, value_part = call(
         functools.partial(local_backward, sizes),
@@ -390,14 +504,30 @@
             total, key_part = lax.optimization_barrier((total, key_part))
     other = swapped(total, "seq", 0)
 
+    final_sizes = (heads, length, block)
+    final_flops = 2 * heads * length * width * width
+    key_mine, value_mine = call(
+        functools.partial(final_mine, final_sizes),
+        (shape((half, length, width), F32), shape((half, length, width), F32)),
+        (place_arg, near_mine, total, kd, vd, key_part, value_part),
+        [SMEM] + [VMEM] * 6,
+        flops=final_flops,
+        name="key_value_mine",
+    )
     key_grad, value_grad = call(
-        functools.partial(final_kernel, (heads, length, block)),
+        functools.partial(final_other, final_sizes),
         (shape((rows, width), F32), shape((rows, width), F32)),
-        (place_arg, back_near, total, other, kd, vd, key_part, value_part),
-        [SMEM] + [VMEM] * 7,
-        [pltpu.VMEM((heads, width, width), F32)],
-        flops=4 * heads * length * width * width,
-        name="key_value_grads",
+        (place_arg, near_other, other, kd, vd, key_part, value_part, key_mine, value_mine),
+        [SMEM] + [VMEM] * 8,
+        [
+            pltpu.VMEM((half, width, width), BF16),
+            pltpu.VMEM((rows, width), F32),
+            pltpu.VMEM((rows, width), F32),
+            pltpu.SemaphoreType.DMA((2, length // block)),
+        ],
+        flops=final_flops,
+        name="key_value_other",
+        outs=HBM,
     )
     return tuple(a.reshape(length, heads, width) for a in (normed, query_grad, key_grad, value_grad))
 

time: 42.6 us -> 41.8 us (0.981)
  waiting for transfers between devices: 17.9 us -> 16.1 us
  Pallas kernels: 8.73 us -> 9.3 us
  starting transfers between devices: 12.8 us -> 13.3 us
    ppermute x8 -> x9, waiting for transfers between devices: 11.1 us -> 9.26 us  [swapped(): return lax.ppermute(block, axis, route)]
    pallas_call x5 -> x8, Pallas kernels: 8.73 us -> 9.3 us  [call(): pl.pallas_call(kernel, out_shape=out_shape, in_specs=specs, out_specs=jax...]
    ppermute x8 -> x9, starting transfers between devices: 2.8 us -> 3.28 us  [swapped(): return lax.ppermute(block, axis, route)]
  transfers between devices with their start and end apart: 14 -> 15, of which waited for: 12 -> 12; matrix products, arithmetic and copies ran while one was open for 0% -> 0% of each run, Pallas kernels for 13% -> 16%
where the time goes in v3:
time: 41.8 us; the launch traced here: 41.6 us
  waiting for transfers between devices  16.1 us (39%)
  starting transfers between devices  13.3 us (32%)
  Pallas kernels  9.3 us (22%)
  matrix products  1.37 us (3%)
  between operations  0.84 us (2%)
  local copies, waits for them, and re-layouts  0.69 us (2%)
    pallas_call x8, Pallas kernels, call(): pl.pallas_call(kernel, out_shape=out_shape, in_specs=specs, out_specs=jax...  9.3 us
    ppermute x9, waiting for transfers between devices, swapped(): return lax.ppermute(block, axis, route)  9.26 us
    ppermute x3, starting transfers between devices, exchanged(): lax.ppermute(block, axis, route)  6.46 us
    ppermute x3, waiting for transfers between devices, summands(): result.append(lax.ppermute(block, axis, route))  4.23 us
    ppermute x3, starting transfers between devices, summands(): result.append(lax.ppermute(block, axis, route))  3.55 us
    ppermute x9, starting transfers between devices, swapped(): return lax.ppermute(block, axis, route)  3.28 us
    ppermute x3, waiting for transfers between devices, exchanged(): lax.ppermute(block, axis, route)  2.6 us
    dot_general x1, matrix products, shards(): jnp.einsum('shd,she->hde', key_rows, value_rows, preferred_element_type=F32)  1.37 us
  transfers between devices with their start and end apart: 15, of which 12 were waited for; matrix products, arithmetic and copies ran while one was open for 0% of the time, Pallas kernels for 16%

profile of v3, /device:TPU:0, one launch (start us, length us, event | category | flops | bytes accessed | tf_op | source)
XLA Modules:
  0.0 41.6 jit_solution(16885924455682358020)
XLA Ops:
  0.6 0.0 copy-start.1
  0.6 0.0 copy-start.2
  0.7 0.0 copy-start.3
  0.7 1.4 %fusion = f32[2,128,128]{2,1,0:T(8,128)S(1)} fusion(bf16[512,2,128]{2,1,0:T(2,128)(2,1)} %param.9, bf16[512,2,128]{2,1,0:T(2,128)(2,1)} %param.8), kind=kOutput, calls=%fused_computation | convolution fusion | flops 33554432 | bytes 655360 | tf_op jit(solution)/shard_map/shd,she->hde/dot_general | solution.py:375
  2.0 0.0 copy-start
  2.0 0.5 %collective-permute-start = (f32[2,128,128]{2,1,0:T(8,128)S(1)}, f32[2,128,128]{2,1,0:T(8,128)S(1)}, u32[]{:S(2)}, u32[]{:S(2)}) collective-permute-start(f32[2,128,128]{2,1,0:T(8,128)S(1)} %fusion), channel_id=1, source_target_pairs={{0,1},{1,0},{2,3},{3,2},{4,5},{5,4},{6,7},{7,6},{8,9},{9,8},{10,11... | collective-permute-start | bytes 393224 | tf_op jit(solution)/shard_map/ppermute | solution.py:33
  2.6 1.0 %collective-permute-done.refs_5_ = f32[2,128,128]{2,1,0:T(8,128)S(1)} collective-permute-done((f32[2,128,128]{2,1,0:T(8,128)S(1)}, f32[2,128,128]{2,1,0:T(8,128)S(1)}, u32[]{:S(2)}, u32[]{:S(2)}) %collective-permute-start) | collective-permute-done | bytes 131104 | tf_op jit(solution)/shard_map/ppermute | solution.py:33
  3.6 4.8 %collective-permute-start.1 = (f32[1,128,128]{2,1,0:T(8,128)S(1)}, f32[1,128,128]{2,1,0:T(8,128)S(1)}, u32[]{:S(2)}, u32[]{:S(2)}) collective-permute-start(f32[1,128,128]{2,1,0:T(8,128)S(1)} %dynamic-slice_add_fusion), channel_id=1, source_target_pairs={{0,2},{2,0},{1,3},{3,1},{8,10},{10,8},{9,11},{11,9},{16,18},{18,16... | collective-permute-start | bytes 196616 | tf_op jit(solution)/shard_map/ppermute | solution.py:46
  8.4 0.7 %collective-permute-start.2 = (f32[1,128,128]{2,1,0:T(8,128)S(1)}, f32[1,128,128]{2,1,0:T(8,128)S(1)}, u32[]{:S(2)}, u32[]{:S(2)}) collective-permute-start(f32[1,128,128]{2,1,0:T(8,128)S(1)} %dynamic-slice_add_fusion), channel_id=1, source_target_pairs={{4,6},{6,4},{5,7},{7,5},{12,14},{14,12},{13,15},{15,13},{20,22},{2... | collective-permute-start | bytes 196616 | tf_op jit(solution)/shard_map/ppermute | solution.py:46
  9.1 1.7 %collective-permute-done.1 = f32[1,128,128]{2,1,0:T(8,128)S(1)} collective-permute-done((f32[1,128,128]{2,1,0:T(8,128)S(1)}, f32[1,128,128]{2,1,0:T(8,128)S(1)}, u32[]{:S(2)}, u32[]{:S(2)}) %collective-permute-start.1) | collective-permute-done | bytes 65568 | tf_op jit(solution)/shard_map/ppermute | solution.py:46
  10.8 0.0 copy-start.4
  10.8 1.0 %collective-permute-start.3 = (f32[1,128,128]{2,1,0:T(8,128)S(1)}, f32[1,128,128]{2,1,0:T(8,128)S(1)}, u32[]{:S(2)}, u32[]{:S(2)}) collective-permute-start(f32[1,128,128]{2,1,0:T(8,128)S(1)} %add.19), channel_id=1, source_target_pairs={{0,4},{4,0},{1,5},{5,1},{2,6},{6,2},{3,7},{7,3},{8,12},{12,8},{9,1... | collective-permute-start | bytes 196616 | tf_op jit(solution)/shard_map/ppermute | solution.py:46
  11.8 0.0 copy-done.1
  11.8 0.0 copy-done.2
  11.8 0.6 %copy-done.6 = s32[512]{0:T(512)S(1)} copy-done((s32[512]{0:T(512)S(1)}, s32[512]{0:T(512)}, u32[]{:S(2)}) %copy-start.6) | copy-done | bytes 2072
  12.5 0.0 copy-done.5
  12.5 2.8 %local_forward.1 = (f32[2,512,128]{2,1,0:T(8,128)S(1)}, bf16[2,512,512]{2,1,0:T(8,128)(2,1)S(1)}, f32[8,128,128]{2,1,0:T(8,128)S(1)}, bf16[2,512,128]{2,1,0:T(8,...) custom-call(s32[1]{0:T(128)} %bitcast.position_ref.refs_0_, ...), custom_call_target="tpu_custom_call" | custom-call | flops 268435456 | bytes 1052484 | tf_op jit(solution)/shard_map/local_forward/pallas_call | solution.py:62
  15.2 0.0 collective-permute-done.2
  15.3 0.9 %collective-permute-done.3.refs_7_ = f32[1,128,128]{2,1,0:T(8,128)S(1)} collective-permute-done((f32[1,128,128]{2,1,0:T(8,128)S(1)}, f32[1,128,128]{2,1,0:T(8,128)S(1)}, u32[]{:S(2)}, u32[]{:S(2)}) %collective-permute-start.3) | collective-permute-done | bytes 65568 | tf_op jit(solution)/shard_map/ppermute | solution.py:46
  16.1 0.1 collective-permute-start.4
  16.2 0.5 %collective-permute-start.5 = (f32[1,128,128]{2,1,0:T(8,128)S(1)}, f32[1,128,128]{2,1,0:T(8,128)S(1)}, u32[]{:S(2)}, u32[]{:S(2)}) collective-permute-start(f32[1,128,128]{2,1,0:T(8,128)S(1)} %collective-permute-done.3.refs_7_), channel_id=1, source_target_pairs={{0,1},{1,0},{2,3},{3,2},{4,5},{5,4},{6,7},{7,6},{8,9},{9,8},{10,11... | collective-permute-start | bytes 196616 | tf_op jit(solution)/shard_map/ppermute | solution.py:33
  16.7 0.5 %cross_mine.1 = (f32[1,512,128]{2,1,0:T(8,128)S(1)}, f32[2,512]{1,0:T(2,128)S(1)}, bf16[3,1,128,128]{3,2,1,0:T(8,128)(2,1)S(1)}) custom-call(s32[1]{0:T(128)} %bitcast.position_ref.refs_0_, f32[2,512,128]{2,1,0:T(8,128)S(1)} %get-tuple-element.44.refs_1_, bf16[2,512,128]{2,1,0:T(8,128)(2,1)S(1)} %get-tuple-element.45.refs_2_.refs_3_.qd_ref, ...), custom_call_target="tpu_custom_call" | custom-call | flops 50331648 | bytes 1626116 | tf_op jit(solution)/shard_map/cross_mine/pallas_call | solution.py:62
  17.2 0.2 collective-permute-done.4.refs_7_
  17.5 0.2 collective-permute-done.5.refs_8_
  17.6 0.5 %cross_other.1 = (f32[1,512,128]{2,1,0:T(8,128)S(1)}, f32[2,512]{1,0:T(2,128)S(1)}, bf16[3,1,128,128]{3,2,1,0:T(8,128)(2,1)S(1)}) custom-call(s32[1]{0:T(128)} %bitcast.position_ref.refs_0_, f32[2,512,128]{2,1,0:T(8,128)S(1)} %get-tuple-element.44.refs_1_, bf16[2,512,128]{2,1,0:T(8,128)(2,1)S(1)} %get-tuple-element.45.refs_2_.refs_3_.qd_ref, ...), custom_call_target="tpu_custom_call" | custom-call | flops 50331648 | bytes 1630212 | tf_op jit(solution)/shard_map/cross_other/pallas_call | solution.py:62
  18.1 1.8 %collective-permute-start.6 = (f32[2,512]{1,0:T(2,128)S(1)}, f32[2,512]{1,0:T(2,128)S(1)}, u32[]{:S(2)}, u32[]{:S(2)}) collective-permute-start(f32[2,512]{1,0:T(2,128)S(1)} %get-tuple-element.54.refs_5_), channel_id=1, source_target_pairs={{0,8},{8,0},{16,24},{24,16},{1,9},{9,1},{17,25},{25,17},{2,10},{10... | collective-permute-start | bytes 12296 | tf_op jit(solution)/shard_map/ppermute | solution.py:57
  19.9 1.5 %collective-permute-start.7 = (f32[2,512]{1,0:T(2,128)S(1)}, f32[2,512]{1,0:T(2,128)S(1)}, u32[]{:S(2)}, u32[]{:S(2)}) collective-permute-start(f32[2,512]{1,0:T(2,128)S(1)} %get-tuple-element.54.refs_5_), channel_id=1, source_target_pairs={{0,16},{8,24},{16,0},{24,8},{1,17},{9,25},{17,1},{25,9},{2,18},{10... | collective-permute-start | bytes 12296 | tf_op jit(solution)/shard_map/ppermute | solution.py:57
  21.4 0.3 collective-permute-start.8
  21.7 0.1 collective-permute-done.6.refs_6_
  21.8 1.7 %collective-permute-done.7.refs_7_ = f32[2,512]{1,0:T(2,128)S(1)} collective-permute-done((f32[2,512]{1,0:T(2,128)S(1)}, f32[2,512]{1,0:T(2,128)S(1)}, u32[]{:S(2)}, u32[]{:S(2)}) %collective-permute-start.7) | collective-permute-done | bytes 4128 | tf_op jit(solution)/shard_map/ppermute | solution.py:57
  23.5 2.4 %collective-permute-done.8.refs_8_ = f32[2,512]{1,0:T(2,128)S(1)} collective-permute-done((f32[2,512]{1,0:T(2,128)S(1)}, f32[2,512]{1,0:T(2,128)S(1)}, u32[]{:S(2)}, u32[]{:S(2)}) %collective-permute-start.8) | collective-permute-done | bytes 4128 | tf_op jit(solution)/shard_map/ppermute | solution.py:57
  25.9 0.8 %state_grads_other.1 = (bf16[1,512,128]{2,1,0:T(8,128)(2,1)S(1)}, f32[1,512]{1,0:T(1,128)S(1)}, f32[512,128]{1,0:T(8,128)S(1)}, f32[512,128]{1,0:T(8,128)S(1)}, ...) custom-call(s32[1]{0:T(128)} %bitcast.position_ref.refs_0_, ...), custom_call_target="tpu_custom_call" | custom-call | flops 50331648 | bytes 1118212 | tf_op jit(solution)/shard_map/state_grads_other/pallas_call | solution.py:62
  26.7 0.1 collective-permute-start.10
  26.8 0.6 %state_grads_mine.1 = (bf16[2,512,128]{2,1,0:T(8,128)(2,1)S(1)}, f32[1,128,128]{2,1,0:T(8,128)S(1)}, f32[2,1,128,128]{3,2,1,0:T(8,128)S(1)}, f32[2,512,128]{2,1,0:T(8,128)S(1)}, bf16[3,2,128,128]{3,2,1,0:T(8,128)(2,1)S(1)}) custom-call(s32[1]{0:T(128)} %bitcast.position_ref.refs_0_, f32[1,512,128]{2,1,0:T(8,128)S(1)} %get-tuple-element.51.attn_ref, ...), custom_call_target="tpu_custom_call" | custom-call | flops 50331648 | bytes 2215940 | tf_op jit(solution)/shard_map/state_grads_mine/pallas_call | solution.py:62
  27.4 0.7 %collective-permute-done.10 = f32[2,1,128,128]{3,2,1,0:T(8,128)S(1)} collective-permute-done((f32[2,1,128,128]{3,2,1,0:T(8,128)S(1)}, f32[2,1,128,128]{3,2,1,0:T(8,128)S(1)}, u32[]{:S(2)}, u32[]{:S(2)}) %collective-permute-start.10) | collective-permute-done | bytes 131104 | tf_op jit(solution)/shard_map/ppermute | solution.py:33
  28.1 1.3 %collective-permute-start.11 = (f32[1,128,128]{2,1,0:T(8,128)S(1)}, f32[1,128,128]{2,1,0:T(8,128)S(1)}, u32[]{:S(2)}, u32[]{:S(2)}) collective-permute-start(f32[1,128,128]{2,1,0:T(8,128)S(1)} %slice_bitcast_fusion.1), channel_id=1, source_target_pairs={{0,4},{4,0},{1,5},{5,1},{2,6},{6,2},{3,7},{7,3},{8,12},{12,8},{9,1... | collective-permute-start | bytes 196616 | tf_op jit(solution)/shard_map/ppermute | solution.py:33
  29.4 2.8 %local_backward.1 = (f32[1024,128]{1,0:T(8,128)}, f32[1024,128]{1,0:T(8,128)}, f32[2,512,128]{2,1,0:T(8,128)S(1)}, f32[2,512,128]{2,1,0:T(8,128)S(1)}) custom-call(bf16[2,512,128]{2,1,0:T(8,128)(2,1)S(1)} %get-tuple-element.60.ag_ref, bf16[2,512,128]{2,1,0:T(8,128)(2,1)S(1)} %get-tuple-element.45.refs_2_.refs_3_.qd_ref, ...), custom_call_target="tpu_custom_call" | custom-call | flops 536870912 | bytes 3398656 | tf_op jit(solution)/shard_map/local_backward/pallas_call | solution.py:62
  32.2 2.6 %collective-permute-done.11 = f32[1,128,128]{2,1,0:T(8,128)S(1)} collective-permute-done((f32[1,128,128]{2,1,0:T(8,128)S(1)}, f32[1,128,128]{2,1,0:T(8,128)S(1)}, u32[]{:S(2)}, u32[]{:S(2)}) %collective-permute-start.11) | collective-permute-done | bytes 65568 | tf_op jit(solution)/shard_map/ppermute | solution.py:33
  34.8 0.2 collective-permute-start.12
  35.0 0.0 collective-permute-start.14
  35.0 0.5 %collective-permute-start.9 = (f32[1,128,128]{2,1,0:T(8,128)S(1)}, f32[1,128,128]{2,1,0:T(8,128)S(1)}, u32[]{:S(2)}, u32[]{:S(2)}) collective-permute-start(f32[1,128,128]{2,1,0:T(8,128)S(1)} %get-tuple-element.70), channel_id=1, source_target_pairs={{0,1},{1,0},{2,3},{3,2},{4,5},{5,4},{6,7},{7,6},{8,9},{9,8},{10,11... | collective-permute-start | bytes 196616 | tf_op jit(solution)/shard_map/ppermute | solution.py:33
  35.5 3.6 %collective-permute-done.12 = f32[1,128,128]{2,1,0:T(8,128)S(1)} collective-permute-done((f32[1,128,128]{2,1,0:T(8,128)S(1)}, f32[1,128,128]{2,1,0:T(8,128)S(1)}, u32[]{:S(2)}, u32[]{:S(2)}) %collective-permute-start.12) | collective-permute-done | bytes 65568 | tf_op jit(solution)/shard_map/ppermute | solution.py:33
  39.1 0.1 collective-permute-start.13
  39.2 0.0 collective-permute-done.14.near_ref
  39.2 0.2 key_value_mine.1
  39.4 0.0 collective-permute-done.9.near_ref
  39.5 1.0 %collective-permute-done.13.total_ref = f32[1,128,128]{2,1,0:T(8,128)S(1)} collective-permute-done((f32[1,128,128]{2,1,0:T(8,128)S(1)}, f32[1,128,128]{2,1,0:T(8,128)S(1)}, u32[]{:S(2)}, u32[]{:S(2)}) %collective-permute-start.13) | collective-permute-done | bytes 65568 | tf_op jit(solution)/shard_map/ppermute | solution.py:33
  40.4 1.2 %key_value_other.1 = (f32[1024,128]{1,0:T(8,128)}, f32[1024,128]{1,0:T(8,128)}) custom-call(s32[1]{0:T(128)} %bitcast.position_ref.refs_0_, f32[1,128,128]{2,1,0:T(8,128)S(1)} %collective-permute-done.9.near_ref, f32[1,128,128]{2,1,0:T(8,128)S(1)} %collective-permute-done.13.total_ref, bf16[2,512,128]{2,1,0:T(8,128)(2,1)S(1)} %get-tuple-element.61.kd_ref, ...), custom_call_target="tpu_custom_call" | custom-call | flops 33554432 | bytes 2228228 | tf_op jit(solution)/shard_map/key_value_other/pallas_call | solution.py:62
  (12 shorter events, 0.1 us)
Async XLA Ops:
  0.6 11.2 %copy-start.1 = (bf16[512,2,128]{2,1,0:T(2,128)(2,1)S(1)}, bf16[512,2,128]{2,1,0:T(2,128)(2,1)}, u32[]{:S(2)}) copy-start(bf16[512,2,128]{2,1,0:T(2,128)(2,1)} %param.9) | copy-start | bytes 786436
  0.6 11.2 %copy-start.2 = (bf16[512,2,128]{2,1,0:T(2,128)(2,1)S(1)}, bf16[512,2,128]{2,1,0:T(2,128)(2,1)}, u32[]{:S(2)}) copy-start(bf16[512,2,128]{2,1,0:T(2,128)(2,1)} %param.7) | copy-start | bytes 786436
  0.7 11.1 %copy-start.3 = (bf16[512,2,128]{2,1,0:T(2,128)(2,1)S(1)}, bf16[512,2,128]{2,1,0:T(2,128)(2,1)}, u32[]{:S(2)}) copy-start(bf16[512,2,128]{2,1,0:T(2,128)(2,1)} %param.13) | copy-start | bytes 786436
  2.0 9.8 %copy-start = (bf16[512,2,128]{2,1,0:T(2,128)(2,1)S(1)}, bf16[512,2,128]{2,1,0:T(2,128)(2,1)}, u32[]{:S(2)}) copy-start(bf16[512,2,128]{2,1,0:T(2,128)(2,1)} %param.8) | copy-start | bytes 786436
  2.0 1.5 %collective-permute-start = (f32[2,128,128]{2,1,0:T(8,128)S(1)}, f32[2,128,128]{2,1,0:T(8,128)S(1)}, u32[]{:S(2)}, u32[]{:S(2)}) collective-permute-start(f32[2,128,128]{2,1,0:T(8,128)S(1)} %fusion), channel_id=1, source_target_pairs={{0,1},{1,0},{2,3},{3,2},{4,5},{5,4},{6,7},{7,6},{8,9},{9,8},{10,11... | collective-permute-start | bytes 393224 | tf_op jit(solution)/shard_map/ppermute | solution.py:33
  3.6 7.2 %collective-permute-start.1 = (f32[1,128,128]{2,1,0:T(8,128)S(1)}, f32[1,128,128]{2,1,0:T(8,128)S(1)}, u32[]{:S(2)}, u32[]{:S(2)}) collective-permute-start(f32[1,128,128]{2,1,0:T(8,128)S(1)} %dynamic-slice_add_fusion), channel_id=1, source_target_pairs={{0,2},{2,0},{1,3},{3,1},{8,10},{10,8},{9,11},{11,9},{16,18},{18,16... | collective-permute-start | bytes 196616 | tf_op jit(solution)/shard_map/ppermute | solution.py:46
  8.4 6.8 %collective-permute-start.2 = (f32[1,128,128]{2,1,0:T(8,128)S(1)}, f32[1,128,128]{2,1,0:T(8,128)S(1)}, u32[]{:S(2)}, u32[]{:S(2)}) collective-permute-start(f32[1,128,128]{2,1,0:T(8,128)S(1)} %dynamic-slice_add_fusion), channel_id=1, source_target_pairs={{4,6},{6,4},{5,7},{7,5},{12,14},{14,12},{13,15},{15,13},{20,22},{2... | collective-permute-start | bytes 196616 | tf_op jit(solution)/shard_map/ppermute | solution.py:46
  10.8 1.0 %copy-start.4 = (f32[8,2,13]{2,1,0:T(2,128)S(1)}, f32[8,2,13]{2,1,0:T(2,128)}, u32[]{:S(2)}) copy-start(f32[8,2,13]{2,1,0:T(2,128)} %table_ref.1) | copy-start | bytes 2500
  10.8 5.3 %collective-permute-start.3 = (f32[1,128,128]{2,1,0:T(8,128)S(1)}, f32[1,128,128]{2,1,0:T(8,128)S(1)}, u32[]{:S(2)}, u32[]{:S(2)}) collective-permute-start(f32[1,128,128]{2,1,0:T(8,128)S(1)} %add.19), channel_id=1, source_target_pairs={{0,4},{4,0},{1,5},{5,1},{2,6},{6,2},{3,7},{7,3},{8,12},{12,8},{9,1... | collective-permute-start | bytes 196616 | tf_op jit(solution)/shard_map/ppermute | solution.py:46
  11.8 0.7 %copy-start.6 = (s32[512]{0:T(512)S(1)}, s32[512]{0:T(512)}, u32[]{:S(2)}) copy-start(s32[512]{0:T(512)} %param.10) | copy-start | bytes 6148
  11.8 0.7 %copy-start.5 = (f32[2,128]{1,0:T(2,128)S(1)}, f32[2,128]{1,0:T(2,128)}, u32[]{:S(2)}) copy-start(f32[2,128]{1,0:T(2,128)} %gain_ref.1) | copy-start | bytes 3076
  16.1 1.3 %collective-permute-start.4 = (f32[1,128,128]{2,1,0:T(8,128)S(1)}, f32[1,128,128]{2,1,0:T(8,128)S(1)}, u32[]{:S(2)}, u32[]{:S(2)}) collective-permute-start(f32[1,128,128]{2,1,0:T(8,128)S(1)} %add.20.refs_6_), channel_id=1, source_target_pairs={{0,1},{1,0},{2,3},{3,2},{4,5},{5,4},{6,7},{7,6},{8,9},{9,8},{10,11... | collective-permute-start | bytes 196616 | tf_op jit(solution)/shard_map/ppermute | solution.py:33
  16.2 1.4 %collective-permute-start.5 = (f32[1,128,128]{2,1,0:T(8,128)S(1)}, f32[1,128,128]{2,1,0:T(8,128)S(1)}, u32[]{:S(2)}, u32[]{:S(2)}) collective-permute-start(f32[1,128,128]{2,1,0:T(8,128)S(1)} %collective-permute-done.3.refs_7_), channel_id=1, source_target_pairs={{0,1},{1,0},{2,3},{3,2},{4,5},{5,4},{6,7},{7,6},{8,9},{9,8},{10,11... | collective-permute-start | bytes 196616 | tf_op jit(solution)/shard_map/ppermute | solution.py:33
  18.1 3.7 %collective-permute-start.6 = (f32[2,512]{1,0:T(2,128)S(1)}, f32[2,512]{1,0:T(2,128)S(1)}, u32[]{:S(2)}, u32[]{:S(2)}) collective-permute-start(f32[2,512]{1,0:T(2,128)S(1)} %get-tuple-element.54.refs_5_), channel_id=1, source_target_pairs={{0,8},{8,0},{16,24},{24,16},{1,9},{9,1},{17,25},{25,17},{2,10},{10... | collective-permute-start | bytes 12296 | tf_op jit(solution)/shard_map/ppermute | solution.py:57
  19.9 3.6 %collective-permute-start.7 = (f32[2,512]{1,0:T(2,128)S(1)}, f32[2,512]{1,0:T(2,128)S(1)}, u32[]{:S(2)}, u32[]{:S(2)}) collective-permute-start(f32[2,512]{1,0:T(2,128)S(1)} %get-tuple-element.54.refs_5_), channel_id=1, source_target_pairs={{0,16},{8,24},{16,0},{24,8},{1,17},{9,25},{17,1},{25,9},{2,18},{10... | collective-permute-start | bytes 12296 | tf_op jit(solution)/shard_map/ppermute | solution.py:57
  21.4 4.5 %collective-permute-start.8 = (f32[2,512]{1,0:T(2,128)S(1)}, f32[2,512]{1,0:T(2,128)S(1)}, u32[]{:S(2)}, u32[]{:S(2)}) collective-permute-start(f32[2,512]{1,0:T(2,128)S(1)} %get-tuple-element.54.refs_5_), channel_id=1, source_target_pairs={{0,24},{8,16},{16,8},{24,0},{1,25},{9,17},{17,9},{25,1},{2,26},{10... | collective-permute-start | bytes 12296 | tf_op jit(solution)/shard_map/ppermute | solution.py:57
  26.7 1.4 %collective-permute-start.10 = (f32[2,1,128,128]{3,2,1,0:T(8,128)S(1)}, f32[2,1,128,128]{3,2,1,0:T(8,128)S(1)}, u32[]{:S(2)}, u32[]{:S(2)}) collective-permute-start(f32[2,1,128,128]{3,2,1,0:T(8,128)S(1)} %get-tuple-element.72), channel_id=1, source_target_pairs={{0,1},{1,0},{2,3},{3,2},{4,5},{5,4},{6,7},{7,6},{8,9},{9,8},{10,11... | collective-permute-start | bytes 393224 | tf_op jit(solution)/shard_map/ppermute | solution.py:33
  28.1 6.6 %collective-permute-start.11 = (f32[1,128,128]{2,1,0:T(8,128)S(1)}, f32[1,128,128]{2,1,0:T(8,128)S(1)}, u32[]{:S(2)}, u32[]{:S(2)}) collective-permute-start(f32[1,128,128]{2,1,0:T(8,128)S(1)} %slice_bitcast_fusion.1), channel_id=1, source_target_pairs={{0,4},{4,0},{1,5},{5,1},{2,6},{6,2},{3,7},{7,3},{8,12},{12,8},{9,1... | collective-permute-start | bytes 196616 | tf_op jit(solution)/shard_map/ppermute | solution.py:33
  34.8 4.3 %collective-permute-start.12 = (f32[1,128,128]{2,1,0:T(8,128)S(1)}, f32[1,128,128]{2,1,0:T(8,128)S(1)}, u32[]{:S(2)}, u32[]{:S(2)}) collective-permute-start(f32[1,128,128]{2,1,0:T(8,128)S(1)} %fusion.3), channel_id=1, source_target_pairs={{0,2},{2,0},{1,3},{3,1},{4,6},{6,4},{5,7},{7,5},{8,10},{10,8},{9,1... | collective-permute-start | bytes 196616 | tf_op jit(solution)/shard_map/ppermute | solution.py:33
  35.0 4.2 %collective-permute-start.14 = (f32[1,128,128]{2,1,0:T(8,128)S(1)}, f32[1,128,128]{2,1,0:T(8,128)S(1)}, u32[]{:S(2)}, u32[]{:S(2)}) collective-permute-start(f32[1,128,128]{2,1,0:T(8,128)S(1)} %get-tuple-element.77), channel_id=1, source_target_pairs={{0,1},{1,0},{2,3},{3,2},{4,5},{5,4},{6,7},{7,6},{8,9},{9,8},{10,11... | collective-permute-start | bytes 196616 | tf_op jit(solution)/shard_map/ppermute | solution.py:33
  35.0 4.4 %collective-permute-start.9 = (f32[1,128,128]{2,1,0:T(8,128)S(1)}, f32[1,128,128]{2,1,0:T(8,128)S(1)}, u32[]{:S(2)}, u32[]{:S(2)}) collective-permute-start(f32[1,128,128]{2,1,0:T(8,128)S(1)} %get-tuple-element.70), channel_id=1, source_target_pairs={{0,1},{1,0},{2,3},{3,2},{4,5},{5,4},{6,7},{7,6},{8,9},{9,8},{10,11... | collective-permute-start | bytes 196616 | tf_op jit(solution)/shard_map/ppermute | solution.py:33
  39.1 1.3 %collective-permute-start.13 = (f32[1,128,128]{2,1,0:T(8,128)S(1)}, f32[1,128,128]{2,1,0:T(8,128)S(1)}, u32[]{:S(2)}, u32[]{:S(2)}) collective-permute-start(f32[1,128,128]{2,1,0:T(8,128)S(1)} %add.23.total_ref), channel_id=1, source_target_pairs={{0,1},{1,0},{2,3},{3,2},{4,5},{5,4},{6,7},{7,6},{8,9},{9,8},{10,11... | collective-permute-start | bytes 196616 | tf_op jit(solution)/shard_map/ppermute | solution.py:33

commit v4 on v3

--- a/solution.py
+++ b/solution.py
@@ -33,27 +33,30 @@
     return lax.ppermute(block, axis, route)
 
 
-def exchanged(block, axis, distance):
-    count = lax.axis_size(axis)
-    needed, rest = [], []
-    for low in range(count):
-        high = low | 1 << distance
-        if high == low:
-            continue
-        last = low >> (distance + 1) == (count - 1) >> (distance + 1)
-        route = rest if last else needed
-        route += [(low, high), (high, low)]
-    return [lax.ppermute(block, axis, route) for route in (needed, rest) if route]
+def turns(count):
+    order = []
+    for step in range(1, count // 2 + 1):
+        order += [step] if 2 * step == count else [step, count - step]
+    return order
 
 
 def summands(block, axis):
     count = lax.axis_size(axis)
     result = [block]
-    for step in range(1, count):
-        if count & (count - 1) == 0:
-            route = [(i, i ^ step) for i in range(count)]
-        else:
-            route = [(i, (i + step) % count) for i in range(count)]
+    for step in turns(count):
+        result.append(lax.ppermute(block, axis, [(i, (i + step) % count) for i in range(count)]))
+    return result
+
+
+def turned(blocks, axis, group):
+    count = lax.axis_size(axis)
+    result = []
+    for step, block in zip(turns(group), blocks):
+        route = []
+        for i in range(count):
+            chip = i >> 1
+            target = chip - chip % group + (chip + step) % group
+            route.append((i, target << 1 | i & 1))
         result.append(lax.ppermute(block, axis, route))
     return result
 
@@ -193,6 +196,33 @@
             held_ref[j, h] = other[j - 1][h].astype(BF16)
     cross_heads(sizes, [start + h for h in range(half)], lambda j, h: held_ref[j, h],
                 inner_ref, qd_ref, gg_ref, tw_ref, attn_ref, sums_ref, add_ref)
+
+
+def sibling(source, target, place):
+    return ((source >> place) == (target >> place ^ 1)).astype(F32)
+
+
+def combine_kernel(group, position_ref, *refs):
+    far = group.bit_length() - 1
+    received, targets = refs[:group - 1], refs[group - 1:]
+    chip = (position_ref[0] >> 1) & (group - 1)
+    for place in range(far):
+        total = 0.0
+        for step, block in zip(turns(group), received):
+            source = (chip + group - step) & (group - 1)
+            total = total + sibling(source, chip, place) * block[...]
+        targets[place][...] = total
+
+
+def message_kernel(group, position_ref, above_ref, keep_ref, came_ref, *targets):
+    far = group.bit_length() - 1
+    chip = (position_ref[0] >> 1) & (group - 1)
+    for step, message in zip(turns(group), targets):
+        target = (chip + step) & (group - 1)
+        total = above_ref[...]
+        for place in range(far):
+            total = total + sibling(chip, target, place) * (keep_ref[place] + came_ref[place])
+        message[...] = total
 
 
 def spread(row, width):
@@ -379,11 +409,9 @@
     block_sum = lax.dynamic_slice(
         pair, ((position & 1) * half, 0, 0), (half, width, width), allow_negative_indices=False
     )
-    partners = []
-    for place in range(1, bits):
-        arrived = exchanged(block_sum, "seq", place)
-        partners.append(arrived)
-        block_sum = block_sum + arrived[0]
+    far = min(bits - 1, 2)
+    group = 1 << far
+    received = turned([block_sum] * (group - 1), "seq", group)
 
     rows = length * heads
     flat = lambda a: a.reshape(rows, width)
@@ -421,8 +449,20 @@
         flops=4 * local_flops,
         name="local_forward",
     )
-    inner, partners = lax.optimization_barrier((inner, partners))
-    mine = [functools.reduce(jnp.add, arrived) for arrived in partners]
+    inner, received = lax.optimization_barrier((inner, received))
+    state = shape((half, width, width), F32)
+    mine = call(
+        functools.partial(combine_kernel, group),
+        (state,) * far,
+        (place_arg, *received),
+        [SMEM] + [VMEM] * (group - 1),
+        name="far_states",
+    )
+    mine = list(mine)
+    block_sum = functools.reduce(jnp.add, received, block_sum)
+    for place in range(far + 1, bits):
+        mine.append(swapped(block_sum, "seq", place))
+        block_sum = block_sum + mine[-1]
     others = [swapped(partner, "seq", 0) for partner in mine]
     cross_flops = bits * heads * length * width * width
     cross_shapes = (
@@ -479,7 +519,18 @@
         flops=cross_flops,
         name="state_grads_mine",
     )
-    gathered = keep + swapped(send, "seq", 0)
+    came = swapped(send, "seq", 0)
+    above = jnp.zeros((half, width, width), F32)
+    for place in reversed(range(far + 1, bits)):
+        above = above + swapped(above + keep[place - 1] + came[place - 1], "seq", place)
+    messages = call(
+        functools.partial(message_kernel, group),
+        (state,) * (group - 1),
+        (place_arg, above, keep, came),
+        [SMEM] + [VMEM] * 3,
+        name="far_messages",
+    )
+    landed = turned(messages, "seq", group)
     near_other = swapped(first_mine, "seq", 0)
     near_mine = swapped(first_other, "seq", 0)
 
@@ -497,11 +548,8 @@
         flops=8 * local_flops,
         name="local_backward",
     )
-    total = jnp.zeros((half, width, width), F32)
-    for place in reversed(range(1, bits)):
-        total = total + swapped(total + gathered[place - 1], "seq", place)
-        if place == bits - 1:
-            total, key_part = lax.optimization_barrier((total, key_part))
+    landed, key_part = lax.optimization_barrier((landed, key_part))
+    total = functools.reduce(jnp.add, landed, above)
     other = swapped(total, "seq", 0)
 
     final_sizes = (heads, length, block)

time: 41.8 us -> 38.4 us (0.919)
  waiting for transfers between devices: 16.1 us -> 8.8 us
  starting transfers between devices: 13.3 us -> 16.1 us
  local copies, waits for them, and re-layouts: 0.69 us -> 1.64 us
    ppermute x9 -> x7, waiting for transfers between devices: 9.26 us -> 3.1 us  [swapped(): return lax.ppermute(block, axis, route)]
    ppermute x6 -> x9, starting transfers between devices: 10 us -> 14.4 us  [the longest x6 9.9 us: turned(): result.append(lax.ppermute(block, axis, route))]
    ppermute x9 -> x7, starting transfers between devices: 3.28 us -> 1.74 us  [swapped(): return lax.ppermute(block, axis, route)]
    ppermute x6 -> x9, waiting for transfers between devices: 6.83 us -> 5.7 us  [the longest x6 3.62 us: turned(): result.append(lax.ppermute(block, axis, route))]
    unnamed x14, local copies, waits for them, and re-layouts: 0.68 us -> 1.63 us
    pallas_call x8 -> x10, Pallas kernels: 9.3 us -> 9.39 us  [call(): pl.pallas_call(kernel, out_shape=out_shape, in_specs=specs, out_specs=jax...]
  transfers between devices with their start and end apart: 15 -> 16, of which waited for: 12 -> 10; matrix products, arithmetic and copies ran while one was open for 0% -> 0% of each run, Pallas kernels for 16% -> 18%
where the time goes in v4:
time: 38.4 us; the launch traced here: 38.2 us
  starting transfers between devices  16.1 us (42%)
  Pallas kernels  9.39 us (24%)
  waiting for transfers between devices  8.8 us (23%)
  local copies, waits for them, and re-layouts  1.64 us (4%)
  matrix products  1.37 us (4%)
  between operations  0.8 us (2%)
    ppermute x6, starting transfers between devices, turned(): result.append(lax.ppermute(block, axis, route))  9.9 us
    pallas_call x10, Pallas kernels, call(): pl.pallas_call(kernel, out_shape=out_shape, in_specs=specs, out_specs=jax...  9.39 us
    ppermute x3, starting transfers between devices, summands(): lax.ppermute(block, axis, [(i, (i + step) % count) for i in range(count)])  4.49 us
    ppermute x6, waiting for transfers between devices, turned(): result.append(lax.ppermute(block, axis, route))  3.62 us
    ppermute x7, waiting for transfers between devices, swapped(): return lax.ppermute(block, axis, route)  3.1 us
    ppermute x3, waiting for transfers between devices, summands(): lax.ppermute(block, axis, [(i, (i + step) % count) for i in range(count)])  2.09 us
    ppermute x7, starting transfers between devices, swapped(): return lax.ppermute(block, axis, route)  1.74 us
    unnamed x14, local copies, waits for them, and re-layouts  1.63 us
  transfers between devices with their start and end apart: 16, of which 10 were waited for; matrix products, arithmetic and copies ran while one was open for 0% of the time, Pallas kernels for 18%

profile of v4, /device:TPU:0, one launch (start us, length us, event | category | flops | bytes accessed | tf_op | source)
XLA Modules:
  0.0 38.2 jit_solution(8621277212465147930)
XLA Ops:
  0.7 1.4 %fusion = f32[2,128,128]{2,1,0:T(8,128)S(1)} fusion(bf16[512,2,128]{2,1,0:T(2,128)(2,1)} %param.9, bf16[512,2,128]{2,1,0:T(2,128)(2,1)} %param.8), kind=kOutput, calls=%fused_computation | convolution fusion | flops 33554432 | bytes 655360 | tf_op jit(solution)/shard_map/shd,she->hde/dot_general | solution.py:405
  2.0 0.5 %collective-permute-start = (f32[2,128,128]{2,1,0:T(8,128)S(1)}, f32[2,128,128]{2,1,0:T(8,128)S(1)}, u32[]{:S(2)}, u32[]{:S(2)}) collective-permute-start(f32[2,128,128]{2,1,0:T(8,128)S(1)} %fusion), channel_id=1, source_target_pairs={{0,1},{1,0},{2,3},{3,2},{4,5},{5,4},{6,7},{7,6},{8,9},{9,8},{10,11... | collective-permute-start | bytes 393224 | tf_op jit(solution)/shard_map/ppermute | solution.py:33
  2.6 1.0 %collective-permute-done.refs_5_ = f32[2,128,128]{2,1,0:T(8,128)S(1)} collective-permute-done((f32[2,128,128]{2,1,0:T(8,128)S(1)}, f32[2,128,128]{2,1,0:T(8,128)S(1)}, u32[]{:S(2)}, u32[]{:S(2)}) %collective-permute-start) | collective-permute-done | bytes 131104 | tf_op jit(solution)/shard_map/ppermute | solution.py:33
  3.6 0.0 copy-start.4
  3.6 3.0 %collective-permute-start.1 = (f32[1,128,128]{2,1,0:T(8,128)S(1)}, f32[1,128,128]{2,1,0:T(8,128)S(1)}, u32[]{:S(2)}, u32[]{:S(2)}) collective-permute-start(f32[1,128,128]{2,1,0:T(8,128)S(1)} %dynamic-slice_add_fusion), channel_id=1, source_target_pairs={{0,2},{1,3},{2,4},{3,5},{4,6},{5,7},{6,0},{7,1},{8,10},{9,11},{10,... | collective-permute-start | bytes 196616 | tf_op jit(solution)/shard_map/ppermute | solution.py:60
  6.6 2.1 %collective-permute-start.2 = (f32[1,128,128]{2,1,0:T(8,128)S(1)}, f32[1,128,128]{2,1,0:T(8,128)S(1)}, u32[]{:S(2)}, u32[]{:S(2)}) collective-permute-start(f32[1,128,128]{2,1,0:T(8,128)S(1)} %dynamic-slice_add_fusion), channel_id=1, source_target_pairs={{0,6},{1,7},{2,0},{3,1},{4,2},{5,3},{6,4},{7,5},{8,14},{9,15},{10,... | collective-permute-start | bytes 196616 | tf_op jit(solution)/shard_map/ppermute | solution.py:60
  8.6 0.9 %collective-permute-start.3 = (f32[1,128,128]{2,1,0:T(8,128)S(1)}, f32[1,128,128]{2,1,0:T(8,128)S(1)}, u32[]{:S(2)}, u32[]{:S(2)}) collective-permute-start(f32[1,128,128]{2,1,0:T(8,128)S(1)} %dynamic-slice_add_fusion), channel_id=1, source_target_pairs={{0,4},{1,5},{2,6},{3,7},{4,0},{5,1},{6,2},{7,3},{8,12},{9,13},{10,... | collective-permute-start | bytes 196616 | tf_op jit(solution)/shard_map/ppermute | solution.py:60
  9.6 0.0 copy-done.1
  9.6 0.0 copy-done.2
  9.6 0.0 copy-done.4
  9.6 0.6 %copy-done.6 = s32[512]{0:T(512)S(1)} copy-done((s32[512]{0:T(512)S(1)}, s32[512]{0:T(512)}, u32[]{:S(2)}) %copy-start.6) | copy-done | bytes 2072
  10.3 0.0 copy-done.5
  10.3 0.9 %copy-done.3 = bf16[512,2,128]{2,1,0:T(2,128)(2,1)S(1)} copy-done((bf16[512,2,128]{2,1,0:T(2,128)(2,1)S(1)}, bf16[512,2,128]{2,1,0:T(2,128)(2,1)}, u32[]{:S(2)}) %copy-start.3) | copy-done | bytes 262168
  11.2 2.8 %local_forward.1 = (f32[2,512,128]{2,1,0:T(8,128)S(1)}, bf16[2,512,512]{2,1,0:T(8,128)(2,1)S(1)}, f32[8,128,128]{2,1,0:T(8,128)S(1)}, bf16[2,512,128]{2,1,0:T(8,...) custom-call(s32[1]{0:T(128)} %bitcast.position_ref.refs_0_, ...), custom_call_target="tpu_custom_call" | custom-call | flops 268435456 | bytes 1052484 | tf_op jit(solution)/shard_map/local_forward/pallas_call | solution.py:65
  14.0 0.0 collective-permute-done.1.refs_0_
  14.0 0.0 collective-permute-done.2.refs_1_
  14.0 1.2 %collective-permute-done.3.refs_2_ = f32[1,128,128]{2,1,0:T(8,128)S(1)} collective-permute-done((f32[1,128,128]{2,1,0:T(8,128)S(1)}, f32[1,128,128]{2,1,0:T(8,128)S(1)}, u32[]{:S(2)}, u32[]{:S(2)}) %collective-permute-start.3) | collective-permute-done | bytes 65568 | tf_op jit(solution)/shard_map/ppermute | solution.py:60
  15.2 0.1 collective-permute-start.4
  15.3 0.5 %collective-permute-start.5 = (f32[1,128,128]{2,1,0:T(8,128)S(1)}, f32[1,128,128]{2,1,0:T(8,128)S(1)}, u32[]{:S(2)}, u32[]{:S(2)}) collective-permute-start(f32[1,128,128]{2,1,0:T(8,128)S(1)} %get-tuple-element.59.refs_7_), channel_id=1, source_target_pairs={{0,1},{1,0},{2,3},{3,2},{4,5},{5,4},{6,7},{7,6},{8,9},{9,8},{10,11... | collective-permute-start | bytes 196616 | tf_op jit(solution)/shard_map/ppermute | solution.py:33
  15.8 0.5 %cross_mine.1 = (f32[1,512,128]{2,1,0:T(8,128)S(1)}, f32[2,512]{1,0:T(2,128)S(1)}, bf16[3,1,128,128]{3,2,1,0:T(8,128)(2,1)S(1)}) custom-call(s32[1]{0:T(128)} %bitcast.position_ref.refs_0_, f32[2,512,128]{2,1,0:T(8,128)S(1)} %get-tuple-element.51.refs_1_, bf16[2,512,128]{2,1,0:T(8,128)(2,1)S(1)} %get-tuple-element.52.refs_2_.refs_3_.qd_ref, ...), custom_call_target="tpu_custom_call" | custom-call | flops 50331648 | bytes 1626116 | tf_op jit(solution)/shard_map/cross_mine/pallas_call | solution.py:65
  16.3 0.2 collective-permute-done.4.refs_7_
  16.6 0.2 collective-permute-done.5.refs_8_
  16.7 0.5 %cross_other.1 = (f32[1,512,128]{2,1,0:T(8,128)S(1)}, f32[2,512]{1,0:T(2,128)S(1)}, bf16[3,1,128,128]{3,2,1,0:T(8,128)(2,1)S(1)}) custom-call(s32[1]{0:T(128)} %bitcast.position_ref.refs_0_, f32[2,512,128]{2,1,0:T(8,128)S(1)} %get-tuple-element.51.refs_1_, bf16[2,512,128]{2,1,0:T(8,128)(2,1)S(1)} %get-tuple-element.52.refs_2_.refs_3_.qd_ref, ...), custom_call_target="tpu_custom_call" | custom-call | flops 50331648 | bytes 1630212 | tf_op jit(solution)/shard_map/cross_other/pallas_call | solution.py:65
  17.2 1.5 %collective-permute-start.6 = (f32[2,512]{1,0:T(2,128)S(1)}, f32[2,512]{1,0:T(2,128)S(1)}, u32[]{:S(2)}, u32[]{:S(2)}) collective-permute-start(f32[2,512]{1,0:T(2,128)S(1)} %get-tuple-element.63.refs_5_), channel_id=1, source_target_pairs={{0,8},{8,16},{16,24},{24,0},{1,9},{9,17},{17,25},{25,1},{2,10},{10... | collective-permute-start | bytes 12296 | tf_op jit(solution)/shard_map/ppermute | solution.py:47
  18.7 1.4 %collective-permute-start.7 = (f32[2,512]{1,0:T(2,128)S(1)}, f32[2,512]{1,0:T(2,128)S(1)}, u32[]{:S(2)}, u32[]{:S(2)}) collective-permute-start(f32[2,512]{1,0:T(2,128)S(1)} %get-tuple-element.63.refs_5_), channel_id=1, source_target_pairs={{0,24},{8,0},{16,8},{24,16},{1,25},{9,1},{17,9},{25,17},{2,26},{10... | collective-permute-start | bytes 12296 | tf_op jit(solution)/shard_map/ppermute | solution.py:47
  20.2 1.5 %collective-permute-start.8 = (f32[2,512]{1,0:T(2,128)S(1)}, f32[2,512]{1,0:T(2,128)S(1)}, u32[]{:S(2)}, u32[]{:S(2)}) collective-permute-start(f32[2,512]{1,0:T(2,128)S(1)} %get-tuple-element.63.refs_5_), channel_id=1, source_target_pairs={{0,16},{8,24},{16,0},{24,8},{1,17},{9,25},{17,1},{25,9},{2,18},{10... | collective-permute-start | bytes 12296 | tf_op jit(solution)/shard_map/ppermute | solution.py:47
  21.7 0.1 collective-permute-done.6.refs_6_
  21.8 0.6 %collective-permute-done.7.refs_7_ = f32[2,512]{1,0:T(2,128)S(1)} collective-permute-done((f32[2,512]{1,0:T(2,128)S(1)}, f32[2,512]{1,0:T(2,128)S(1)}, u32[]{:S(2)}, u32[]{:S(2)}) %collective-permute-start.7) | collective-permute-done | bytes 4128 | tf_op jit(solution)/shard_map/ppermute | solution.py:47
  22.3 1.4 %collective-permute-done.8.refs_8_ = f32[2,512]{1,0:T(2,128)S(1)} collective-permute-done((f32[2,512]{1,0:T(2,128)S(1)}, f32[2,512]{1,0:T(2,128)S(1)}, u32[]{:S(2)}, u32[]{:S(2)}) %collective-permute-start.8) | collective-permute-done | bytes 4128 | tf_op jit(solution)/shard_map/ppermute | solution.py:47
  23.8 0.8 %state_grads_other.1 = (bf16[1,512,128]{2,1,0:T(8,128)(2,1)S(1)}, f32[1,512]{1,0:T(1,128)S(1)}, f32[512,128]{1,0:T(8,128)S(1)}, f32[512,128]{1,0:T(8,128)S(1)}, ...) custom-call(s32[1]{0:T(128)} %bitcast.position_ref.refs_0_, ...), custom_call_target="tpu_custom_call" | custom-call | flops 50331648 | bytes 1118212 | tf_op jit(solution)/shard_map/state_grads_other/pallas_call | solution.py:65
  24.6 0.1 collective-permute-start.10
  24.6 0.6 %state_grads_mine.1 = (bf16[2,512,128]{2,1,0:T(8,128)(2,1)S(1)}, f32[1,128,128]{2,1,0:T(8,128)S(1)}, f32[2,1,128,128]{3,2,1,0:T(8,128)S(1)}, f32[2,512,128]{2,1,0:T(8,128)S(1)}, bf16[3,2,128,128]{3,2,1,0:T(8,128)(2,1)S(1)}) custom-call(s32[1]{0:T(128)} %bitcast.position_ref.refs_0_, f32[1,512,128]{2,1,0:T(8,128)S(1)} %get-tuple-element.60.attn_ref, ...), custom_call_target="tpu_custom_call" | custom-call | flops 50331648 | bytes 2215940 | tf_op jit(solution)/shard_map/state_grads_mine/pallas_call | solution.py:65
  25.3 0.7 %collective-permute-done.10.came_ref = f32[2,1,128,128]{3,2,1,0:T(8,128)S(1)} collective-permute-done((f32[2,1,128,128]{3,2,1,0:T(8,128)S(1)}, f32[2,1,128,128]{3,2,1,0:T(8,128)S(1)}, u32[]{:S(2)}, u32[]{:S(2)}) %collective-permute-start.10) | collective-permute-done | bytes 131104 | tf_op jit(solution)/shard_map/ppermute | solution.py:33
  26.0 0.5 %collective-permute-start.11 = (f32[1,128,128]{2,1,0:T(8,128)S(1)}, f32[1,128,128]{2,1,0:T(8,128)S(1)}, u32[]{:S(2)}, u32[]{:S(2)}) collective-permute-start(f32[1,128,128]{2,1,0:T(8,128)S(1)} %get-tuple-element.82), channel_id=1, source_target_pairs={{0,2},{1,3},{2,4},{3,5},{4,6},{5,7},{6,0},{7,1},{8,10},{9,11},{10,... | collective-permute-start | bytes 196616 | tf_op jit(solution)/shard_map/ppermute | solution.py:60
  26.5 3.4 %collective-permute-start.12 = (f32[1,128,128]{2,1,0:T(8,128)S(1)}, f32[1,128,128]{2,1,0:T(8,128)S(1)}, u32[]{:S(2)}, u32[]{:S(2)}) collective-permute-start(f32[1,128,128]{2,1,0:T(8,128)S(1)} %get-tuple-element.83), channel_id=1, source_target_pairs={{0,6},{1,7},{2,0},{3,1},{4,2},{5,3},{6,4},{7,5},{8,14},{9,15},{10,... | collective-permute-start | bytes 196616 | tf_op jit(solution)/shard_map/ppermute | solution.py:60
  29.9 0.0 collective-permute-start.13
  29.9 0.0 collective-permute-start.15
  29.9 0.5 %collective-permute-start.9 = (f32[1,128,128]{2,1,0:T(8,128)S(1)}, f32[1,128,128]{2,1,0:T(8,128)S(1)}, u32[]{:S(2)}, u32[]{:S(2)}) collective-permute-start(f32[1,128,128]{2,1,0:T(8,128)S(1)} %get-tuple-element.79), channel_id=1, source_target_pairs={{0,1},{1,0},{2,3},{3,2},{4,5},{5,4},{6,7},{7,6},{8,9},{9,8},{10,11... | collective-permute-start | bytes 196616 | tf_op jit(solution)/shard_map/ppermute | solution.py:33
  30.4 2.8 %local_backward.1 = (f32[1024,128]{1,0:T(8,128)}, f32[1024,128]{1,0:T(8,128)}, f32[2,512,128]{2,1,0:T(8,128)S(1)}, f32[2,512,128]{2,1,0:T(8,128)S(1)}) custom-call(bf16[2,512,128]{2,1,0:T(8,128)(2,1)S(1)} %get-tuple-element.69.ag_ref, bf16[2,512,128]{2,1,0:T(8,128)(2,1)S(1)} %get-tuple-element.52.refs_2_.refs_3_.qd_ref, ...), custom_call_target="tpu_custom_call" | custom-call | flops 536870912 | bytes 3398656 | tf_op jit(solution)/shard_map/local_backward/pallas_call | solution.py:65
  33.2 0.0 collective-permute-done.11
  33.2 0.0 collective-permute-done.12
  33.2 2.4 %collective-permute-done.13 = f32[1,128,128]{2,1,0:T(8,128)S(1)} collective-permute-done((f32[1,128,128]{2,1,0:T(8,128)S(1)}, f32[1,128,128]{2,1,0:T(8,128)S(1)}, u32[]{:S(2)}, u32[]{:S(2)}) %collective-permute-start.13) | collective-permute-done | bytes 65568 | tf_op jit(solution)/shard_map/ppermute | solution.py:60
  35.6 0.1 collective-permute-start.14
  35.7 0.0 collective-permute-done.15.near_ref
  35.7 0.2 key_value_mine.1
  36.0 0.0 collective-permute-done.9.near_ref
  36.0 1.0 %collective-permute-done.14.total_ref = f32[1,128,128]{2,1,0:T(8,128)S(1)} collective-permute-done((f32[1,128,128]{2,1,0:T(8,128)S(1)}, f32[1,128,128]{2,1,0:T(8,128)S(1)}, u32[]{:S(2)}, u32[]{:S(2)}) %collective-permute-start.14) | collective-permute-done | bytes 65568 | tf_op jit(solution)/shard_map/ppermute | solution.py:33
  37.0 1.2 %key_value_other.1 = (f32[1024,128]{1,0:T(8,128)}, f32[1024,128]{1,0:T(8,128)}) custom-call(s32[1]{0:T(128)} %bitcast.position_ref.refs_0_, f32[1,128,128]{2,1,0:T(8,128)S(1)} %collective-permute-done.9.near_ref, f32[1,128,128]{2,1,0:T(8,128)S(1)} %collective-permute-done.14.total_ref, bf16[2,512,128]{2,1,0:T(8,128)(2,1)S(1)} %get-tuple-element.70.kd_ref, ...), custom_call_target="tpu_custom_call" | custom-call | flops 33554432 | bytes 2228228 | tf_op jit(solution)/shard_map/key_value_other/pallas_call | solution.py:65
  (12 shorter events, 0.1 us)
Async XLA Ops:
  0.6 9.0 %copy-start = (bf16[512,2,128]{2,1,0:T(2,128)(2,1)S(1)}, bf16[512,2,128]{2,1,0:T(2,128)(2,1)}, u32[]{:S(2)}) copy-start(bf16[512,2,128]{2,1,0:T(2,128)(2,1)} %param.8) | copy-start | bytes 786436
  0.6 9.0 %copy-start.1 = (bf16[512,2,128]{2,1,0:T(2,128)(2,1)S(1)}, bf16[512,2,128]{2,1,0:T(2,128)(2,1)}, u32[]{:S(2)}) copy-start(bf16[512,2,128]{2,1,0:T(2,128)(2,1)} %param.9) | copy-start | bytes 786436
  0.7 9.0 %copy-start.2 = (bf16[512,2,128]{2,1,0:T(2,128)(2,1)S(1)}, bf16[512,2,128]{2,1,0:T(2,128)(2,1)}, u32[]{:S(2)}) copy-start(bf16[512,2,128]{2,1,0:T(2,128)(2,1)} %param.7) | copy-start | bytes 786436
  2.0 1.5 %collective-permute-start = (f32[2,128,128]{2,1,0:T(8,128)S(1)}, f32[2,128,128]{2,1,0:T(8,128)S(1)}, u32[]{:S(2)}, u32[]{:S(2)}) collective-permute-start(f32[2,128,128]{2,1,0:T(8,128)S(1)} %fusion), channel_id=1, source_target_pairs={{0,1},{1,0},{2,3},{3,2},{4,5},{5,4},{6,7},{7,6},{8,9},{9,8},{10,11... | collective-permute-start | bytes 393224 | tf_op jit(solution)/shard_map/ppermute | solution.py:33
  3.6 6.1 %copy-start.4 = (f32[8,2,13]{2,1,0:T(2,128)S(1)}, f32[8,2,13]{2,1,0:T(2,128)}, u32[]{:S(2)}) copy-start(f32[8,2,13]{2,1,0:T(2,128)} %table_ref.1) | copy-start | bytes 2500
  3.6 10.4 %collective-permute-start.1 = (f32[1,128,128]{2,1,0:T(8,128)S(1)}, f32[1,128,128]{2,1,0:T(8,128)S(1)}, u32[]{:S(2)}, u32[]{:S(2)}) collective-permute-start(f32[1,128,128]{2,1,0:T(8,128)S(1)} %dynamic-slice_add_fusion), channel_id=1, source_target_pairs={{0,2},{1,3},{2,4},{3,5},{4,6},{5,7},{6,0},{7,1},{8,10},{9,11},{10,... | collective-permute-start | bytes 196616 | tf_op jit(solution)/shard_map/ppermute | solution.py:60
  6.6 7.5 %collective-permute-start.2 = (f32[1,128,128]{2,1,0:T(8,128)S(1)}, f32[1,128,128]{2,1,0:T(8,128)S(1)}, u32[]{:S(2)}, u32[]{:S(2)}) collective-permute-start(f32[1,128,128]{2,1,0:T(8,128)S(1)} %dynamic-slice_add_fusion), channel_id=1, source_target_pairs={{0,6},{1,7},{2,0},{3,1},{4,2},{5,3},{6,4},{7,5},{8,14},{9,15},{10,... | collective-permute-start | bytes 196616 | tf_op jit(solution)/shard_map/ppermute | solution.py:60
  8.6 6.6 %collective-permute-start.3 = (f32[1,128,128]{2,1,0:T(8,128)S(1)}, f32[1,128,128]{2,1,0:T(8,128)S(1)}, u32[]{:S(2)}, u32[]{:S(2)}) collective-permute-start(f32[1,128,128]{2,1,0:T(8,128)S(1)} %dynamic-slice_add_fusion), channel_id=1, source_target_pairs={{0,4},{1,5},{2,6},{3,7},{4,0},{5,1},{6,2},{7,3},{8,12},{9,13},{10,... | collective-permute-start | bytes 196616 | tf_op jit(solution)/shard_map/ppermute | solution.py:60
  9.6 0.7 %copy-start.6 = (s32[512]{0:T(512)S(1)}, s32[512]{0:T(512)}, u32[]{:S(2)}) copy-start(s32[512]{0:T(512)} %param.10) | copy-start | bytes 6148
  9.6 0.7 %copy-start.5 = (f32[2,128]{1,0:T(2,128)S(1)}, f32[2,128]{1,0:T(2,128)}, u32[]{:S(2)}) copy-start(f32[2,128]{1,0:T(2,128)} %gain_ref.1) | copy-start | bytes 3076
  10.3 0.9 %copy-start.3 = (bf16[512,2,128]{2,1,0:T(2,128)(2,1)S(1)}, bf16[512,2,128]{2,1,0:T(2,128)(2,1)}, u32[]{:S(2)}) copy-start(bf16[512,2,128]{2,1,0:T(2,128)(2,1)} %param.13) | copy-start | bytes 786436
  15.2 1.3 %collective-permute-start.4 = (f32[1,128,128]{2,1,0:T(8,128)S(1)}, f32[1,128,128]{2,1,0:T(8,128)S(1)}, u32[]{:S(2)}, u32[]{:S(2)}) collective-permute-start(f32[1,128,128]{2,1,0:T(8,128)S(1)} %get-tuple-element.58.refs_6_), channel_id=1, source_target_pairs={{0,1},{1,0},{2,3},{3,2},{4,5},{5,4},{6,7},{7,6},{8,9},{9,8},{10,11... | collective-permute-start | bytes 196616 | tf_op jit(solution)/shard_map/ppermute | solution.py:33
  15.3 1.4 %collective-permute-start.5 = (f32[1,128,128]{2,1,0:T(8,128)S(1)}, f32[1,128,128]{2,1,0:T(8,128)S(1)}, u32[]{:S(2)}, u32[]{:S(2)}) collective-permute-start(f32[1,128,128]{2,1,0:T(8,128)S(1)} %get-tuple-element.59.refs_7_), channel_id=1, source_target_pairs={{0,1},{1,0},{2,3},{3,2},{4,5},{5,4},{6,7},{7,6},{8,9},{9,8},{10,11... | collective-permute-start | bytes 196616 | tf_op jit(solution)/shard_map/ppermute | solution.py:33
  17.2 4.6 %collective-permute-start.6 = (f32[2,512]{1,0:T(2,128)S(1)}, f32[2,512]{1,0:T(2,128)S(1)}, u32[]{:S(2)}, u32[]{:S(2)}) collective-permute-start(f32[2,512]{1,0:T(2,128)S(1)} %get-tuple-element.63.refs_5_), channel_id=1, source_target_pairs={{0,8},{8,16},{16,24},{24,0},{1,9},{9,17},{17,25},{25,1},{2,10},{10... | collective-permute-start | bytes 12296 | tf_op jit(solution)/shard_map/ppermute | solution.py:47
  18.7 3.6 %collective-permute-start.7 = (f32[2,512]{1,0:T(2,128)S(1)}, f32[2,512]{1,0:T(2,128)S(1)}, u32[]{:S(2)}, u32[]{:S(2)}) collective-permute-start(f32[2,512]{1,0:T(2,128)S(1)} %get-tuple-element.63.refs_5_), channel_id=1, source_target_pairs={{0,24},{8,0},{16,8},{24,16},{1,25},{9,1},{17,9},{25,17},{2,26},{10... | collective-permute-start | bytes 12296 | tf_op jit(solution)/shard_map/ppermute | solution.py:47
  20.2 3.6 %collective-permute-start.8 = (f32[2,512]{1,0:T(2,128)S(1)}, f32[2,512]{1,0:T(2,128)S(1)}, u32[]{:S(2)}, u32[]{:S(2)}) collective-permute-start(f32[2,512]{1,0:T(2,128)S(1)} %get-tuple-element.63.refs_5_), channel_id=1, source_target_pairs={{0,16},{8,24},{16,0},{24,8},{1,17},{9,25},{17,1},{25,9},{2,18},{10... | collective-permute-start | bytes 12296 | tf_op jit(solution)/shard_map/ppermute | solution.py:47
  24.6 1.4 %collective-permute-start.10 = (f32[2,1,128,128]{3,2,1,0:T(8,128)S(1)}, f32[2,1,128,128]{3,2,1,0:T(8,128)S(1)}, u32[]{:S(2)}, u32[]{:S(2)}) collective-permute-start(f32[2,1,128,128]{3,2,1,0:T(8,128)S(1)} %get-tuple-element.81), channel_id=1, source_target_pairs={{0,1},{1,0},{2,3},{3,2},{4,5},{5,4},{6,7},{7,6},{8,9},{9,8},{10,11... | collective-permute-start | bytes 393224 | tf_op jit(solution)/shard_map/ppermute | solution.py:33
  26.0 7.2 %collective-permute-start.11 = (f32[1,128,128]{2,1,0:T(8,128)S(1)}, f32[1,128,128]{2,1,0:T(8,128)S(1)}, u32[]{:S(2)}, u32[]{:S(2)}) collective-permute-start(f32[1,128,128]{2,1,0:T(8,128)S(1)} %get-tuple-element.82), channel_id=1, source_target_pairs={{0,2},{1,3},{2,4},{3,5},{4,6},{5,7},{6,0},{7,1},{8,10},{9,11},{10,... | collective-permute-start | bytes 196616 | tf_op jit(solution)/shard_map/ppermute | solution.py:60
  26.5 6.7 %collective-permute-start.12 = (f32[1,128,128]{2,1,0:T(8,128)S(1)}, f32[1,128,128]{2,1,0:T(8,128)S(1)}, u32[]{:S(2)}, u32[]{:S(2)}) collective-permute-start(f32[1,128,128]{2,1,0:T(8,128)S(1)} %get-tuple-element.83), channel_id=1, source_target_pairs={{0,6},{1,7},{2,0},{3,1},{4,2},{5,3},{6,4},{7,5},{8,14},{9,15},{10,... | collective-permute-start | bytes 196616 | tf_op jit(solution)/shard_map/ppermute | solution.py:60
  29.9 5.7 %collective-permute-start.13 = (f32[1,128,128]{2,1,0:T(8,128)S(1)}, f32[1,128,128]{2,1,0:T(8,128)S(1)}, u32[]{:S(2)}, u32[]{:S(2)}) collective-permute-start(f32[1,128,128]{2,1,0:T(8,128)S(1)} %get-tuple-element.84), channel_id=1, source_target_pairs={{0,4},{1,5},{2,6},{3,7},{4,0},{5,1},{6,2},{7,3},{8,12},{9,13},{10,... | collective-permute-start | bytes 196616 | tf_op jit(solution)/shard_map/ppermute | solution.py:60
  29.9 5.8 %collective-permute-start.15 = (f32[1,128,128]{2,1,0:T(8,128)S(1)}, f32[1,128,128]{2,1,0:T(8,128)S(1)}, u32[]{:S(2)}, u32[]{:S(2)}) collective-permute-start(f32[1,128,128]{2,1,0:T(8,128)S(1)} %get-tuple-element.91), channel_id=1, source_target_pairs={{0,1},{1,0},{2,3},{3,2},{4,5},{5,4},{6,7},{7,6},{8,9},{9,8},{10,11... | collective-permute-start | bytes 196616 | tf_op jit(solution)/shard_map/ppermute | solution.py:33
  29.9 6.1 %collective-permute-start.9 = (f32[1,128,128]{2,1,0:T(8,128)S(1)}, f32[1,128,128]{2,1,0:T(8,128)S(1)}, u32[]{:S(2)}, u32[]{:S(2)}) collective-permute-start(f32[1,128,128]{2,1,0:T(8,128)S(1)} %get-tuple-element.79), channel_id=1, source_target_pairs={{0,1},{1,0},{2,3},{3,2},{4,5},{5,4},{6,7},{7,6},{8,9},{9,8},{10,11... | collective-permute-start | bytes 196616 | tf_op jit(solution)/shard_map/ppermute | solution.py:33
  35.6 1.3 %collective-permute-start.14 = (f32[1,128,128]{2,1,0:T(8,128)S(1)}, f32[1,128,128]{2,1,0:T(8,128)S(1)}, u32[]{:S(2)}, u32[]{:S(2)}) collective-permute-start(f32[1,128,128]{2,1,0:T(8,128)S(1)} %add_add_fusion.total_ref), channel_id=1, source_target_pairs={{0,1},{1,0},{2,3},{3,2},{4,5},{5,4},{6,7},{7,6},{8,9},{9,8},{10,11... | collective-permute-start | bytes 196616 | tf_op jit(solution)/shard_map/ppermute | solution.py:33

commit v5 on v4

--- a/solution.py
+++ b/solution.py
@@ -40,6 +40,10 @@
     return order
 
 
+def swaps(group):
+    return list(range(group - 1, 0, -1))
+
+
 def summands(block, axis):
     count = lax.axis_size(axis)
     result = [block]
@@ -51,11 +55,11 @@
 def turned(blocks, axis, group):
     count = lax.axis_size(axis)
     result = []
-    for step, block in zip(turns(group), blocks):
+    for step, block in zip(swaps(group), blocks):
         route = []
         for i in range(count):
             chip = i >> 1
-            target = chip - chip % group + (chip + step) % group
+            target = chip - chip % group + (chip % group ^ step)
             route.append((i, target << 1 | i & 1))
         result.append(lax.ppermute(block, axis, route))
     return result
@@ -208,8 +212,8 @@
     chip = (position_ref[0] >> 1) & (group - 1)
     for place in range(far):
         total = 0.0
-        for step, block in zip(turns(group), received):
-            source = (chip + group - step) & (group - 1)
+        for step, block in zip(swaps(group), received):
+            source = chip ^ step
             total = total + sibling(source, chip, place) * block[...]
         targets[place][...] = total
 
@@ -217,8 +221,8 @@
 def message_kernel(group, position_ref, above_ref, keep_ref, came_ref, *targets):
     far = group.bit_length() - 1
     chip = (position_ref[0] >> 1) & (group - 1)
-    for step, message in zip(turns(group), targets):
-        target = (chip + step) & (group - 1)
+    for step, message in zip(swaps(group), targets):
+        target = chip ^ step
         total = above_ref[...]
         for place in range(far):
             total = total + sibling(chip, target, place) * (keep_ref[place] + came_ref[place])

time: 38.4 us -> 37.1 us (0.966)
  waiting for transfers between devices: 8.8 us -> 7.38 us
    ppermute x6, waiting for transfers between devices: 3.62 us -> 2.2 us  [turned(): result.append(lax.ppermute(block, axis, route))]
  transfers between devices with their start and end apart: 16 -> 16, of which waited for: 10 -> 10; matrix products, arithmetic and copies ran while one was open for 0% -> 0% of each run, Pallas kernels for 18% -> 19%
where the time goes in v5:
time: 37.1 us; the launch traced here: 36.9 us
  starting transfers between devices  16.4 us (44%)
  Pallas kernels  9.38 us (25%)
  waiting for transfers between devices  7.38 us (20%)
  local copies, waits for them, and re-layouts  1.64 us (4%)
  matrix products  1.37 us (4%)
  between operations  0.8 us (2%)
    ppermute x6, starting transfers between devices, turned(): result.append(lax.ppermute(block, axis, route))  10.1 us
    pallas_call x10, Pallas kernels, call(): pl.pallas_call(kernel, out_shape=out_shape, in_specs=specs, out_specs=jax...  9.38 us
    ppermute x3, starting transfers between devices, summands(): lax.ppermute(block, axis, [(i, (i + step) % count) for i in range(count)])  4.49 us
    ppermute x7, waiting for transfers between devices, swapped(): return lax.ppermute(block, axis, route)  3.09 us
    ppermute x6, waiting for transfers between devices, turned(): result.append(lax.ppermute(block, axis, route))  2.2 us
    ppermute x3, waiting for transfers between devices, summands(): lax.ppermute(block, axis, [(i, (i + step) % count) for i in range(count)])  2.09 us
    ppermute x7, starting transfers between devices, swapped(): return lax.ppermute(block, axis, route)  1.74 us
    unnamed x14, local copies, waits for them, and re-layouts  1.63 us
  transfers between devices with their start and end apart: 16, of which 10 were waited for; matrix products, arithmetic and copies ran while one was open for 0% of the time, Pallas kernels for 19%

profile of v5, /device:TPU:0, one launch (start us, length us, event | category | flops | bytes accessed | tf_op | source)
XLA Modules:
  0.0 36.9 jit_solution(8822322853379463278)
XLA Ops:
  0.6 0.0 copy-start
  0.6 0.0 copy-start.1
  0.7 1.4 %fusion = f32[2,128,128]{2,1,0:T(8,128)S(1)} fusion(bf16[512,2,128]{2,1,0:T(2,128)(2,1)} %param.9, bf16[512,2,128]{2,1,0:T(2,128)(2,1)} %param.8), kind=kOutput, calls=%fused_computation | convolution fusion | flops 33554432 | bytes 655360 | tf_op jit(solution)/shard_map/shd,she->hde/dot_general | solution.py:409
  2.0 0.5 %collective-permute-start = (f32[2,128,128]{2,1,0:T(8,128)S(1)}, f32[2,128,128]{2,1,0:T(8,128)S(1)}, u32[]{:S(2)}, u32[]{:S(2)}) collective-permute-start(f32[2,128,128]{2,1,0:T(8,128)S(1)} %fusion), channel_id=1, source_target_pairs={{0,1},{1,0},{2,3},{3,2},{4,5},{5,4},{6,7},{7,6},{8,9},{9,8},{10,11... | collective-permute-start | bytes 393224 | tf_op jit(solution)/shard_map/ppermute | solution.py:33
  2.6 1.0 %collective-permute-done.refs_5_ = f32[2,128,128]{2,1,0:T(8,128)S(1)} collective-permute-done((f32[2,128,128]{2,1,0:T(8,128)S(1)}, f32[2,128,128]{2,1,0:T(8,128)S(1)}, u32[]{:S(2)}, u32[]{:S(2)}) %collective-permute-start) | collective-permute-done | bytes 131104 | tf_op jit(solution)/shard_map/ppermute | solution.py:33
  3.6 0.0 copy-start.4
  3.6 5.0 %collective-permute-start.1 = (f32[1,128,128]{2,1,0:T(8,128)S(1)}, f32[1,128,128]{2,1,0:T(8,128)S(1)}, u32[]{:S(2)}, u32[]{:S(2)}) collective-permute-start(f32[1,128,128]{2,1,0:T(8,128)S(1)} %dynamic-slice_add_fusion), channel_id=1, source_target_pairs={{0,6},{1,7},{2,4},{3,5},{4,2},{5,3},{6,0},{7,1},{8,14},{9,15},{10,... | collective-permute-start | bytes 196616 | tf_op jit(solution)/shard_map/ppermute | solution.py:64
  8.6 0.0 collective-permute-start.2
  8.6 0.6 %collective-permute-start.3 = (f32[1,128,128]{2,1,0:T(8,128)S(1)}, f32[1,128,128]{2,1,0:T(8,128)S(1)}, u32[]{:S(2)}, u32[]{:S(2)}) collective-permute-start(f32[1,128,128]{2,1,0:T(8,128)S(1)} %dynamic-slice_add_fusion), channel_id=1, source_target_pairs={{0,2},{1,3},{2,0},{3,1},{4,6},{5,7},{6,4},{7,5},{8,10},{9,11},{10,... | collective-permute-start | bytes 196616 | tf_op jit(solution)/shard_map/ppermute | solution.py:64
  9.2 0.0 copy-done
  9.3 0.6 %copy-done.6 = s32[512]{0:T(512)S(1)} copy-done((s32[512]{0:T(512)S(1)}, s32[512]{0:T(512)}, u32[]{:S(2)}) %copy-start.6) | copy-done | bytes 2072
  9.9 0.0 copy-done.5
  9.9 0.9 %copy-done.3 = bf16[512,2,128]{2,1,0:T(2,128)(2,1)S(1)} copy-done((bf16[512,2,128]{2,1,0:T(2,128)(2,1)S(1)}, bf16[512,2,128]{2,1,0:T(2,128)(2,1)}, u32[]{:S(2)}) %copy-start.3) | copy-done | bytes 262168
  10.9 2.8 %local_forward.1 = (f32[2,512,128]{2,1,0:T(8,128)S(1)}, bf16[2,512,512]{2,1,0:T(8,128)(2,1)S(1)}, f32[8,128,128]{2,1,0:T(8,128)S(1)}, bf16[2,512,128]{2,1,0:T(8,...) custom-call(s32[1]{0:T(128)} %bitcast.position_ref.refs_0_, ...), custom_call_target="tpu_custom_call" | custom-call | flops 268435456 | bytes 1052484 | tf_op jit(solution)/shard_map/local_forward/pallas_call | solution.py:69
  13.6 0.0 collective-permute-done.1.refs_0_
  13.7 0.8 %collective-permute-done.2.refs_1_ = f32[1,128,128]{2,1,0:T(8,128)S(1)} collective-permute-done((f32[1,128,128]{2,1,0:T(8,128)S(1)}, f32[1,128,128]{2,1,0:T(8,128)S(1)}, u32[]{:S(2)}, u32[]{:S(2)}) %collective-permute-start.2) | collective-permute-done | bytes 65568 | tf_op jit(solution)/shard_map/ppermute | solution.py:64
  14.5 0.0 collective-permute-done.3.refs_2_
  14.5 0.1 collective-permute-start.4
  14.6 0.5 %collective-permute-start.5 = (f32[1,128,128]{2,1,0:T(8,128)S(1)}, f32[1,128,128]{2,1,0:T(8,128)S(1)}, u32[]{:S(2)}, u32[]{:S(2)}) collective-permute-start(f32[1,128,128]{2,1,0:T(8,128)S(1)} %get-tuple-element.59.refs_7_), channel_id=1, source_target_pairs={{0,1},{1,0},{2,3},{3,2},{4,5},{5,4},{6,7},{7,6},{8,9},{9,8},{10,11... | collective-permute-start | bytes 196616 | tf_op jit(solution)/shard_map/ppermute | solution.py:33
  15.1 0.5 %cross_mine.1 = (f32[1,512,128]{2,1,0:T(8,128)S(1)}, f32[2,512]{1,0:T(2,128)S(1)}, bf16[3,1,128,128]{3,2,1,0:T(8,128)(2,1)S(1)}) custom-call(s32[1]{0:T(128)} %bitcast.position_ref.refs_0_, f32[2,512,128]{2,1,0:T(8,128)S(1)} %get-tuple-element.51.refs_1_, bf16[2,512,128]{2,1,0:T(8,128)(2,1)S(1)} %get-tuple-element.52.refs_2_.refs_3_.qd_ref, ...), custom_call_target="tpu_custom_call" | custom-call | flops 50331648 | bytes 1626116 | tf_op jit(solution)/shard_map/cross_mine/pallas_call | solution.py:69
  15.6 0.2 collective-permute-done.4.refs_7_
  15.8 0.2 collective-permute-done.5.refs_8_
  16.0 0.5 %cross_other.1 = (f32[1,512,128]{2,1,0:T(8,128)S(1)}, f32[2,512]{1,0:T(2,128)S(1)}, bf16[3,1,128,128]{3,2,1,0:T(8,128)(2,1)S(1)}) custom-call(s32[1]{0:T(128)} %bitcast.position_ref.refs_0_, f32[2,512,128]{2,1,0:T(8,128)S(1)} %get-tuple-element.51.refs_1_, bf16[2,512,128]{2,1,0:T(8,128)(2,1)S(1)} %get-tuple-element.52.refs_2_.refs_3_.qd_ref, ...), custom_call_target="tpu_custom_call" | custom-call | flops 50331648 | bytes 1630212 | tf_op jit(solution)/shard_map/cross_other/pallas_call | solution.py:69
  16.5 1.5 %collective-permute-start.6 = (f32[2,512]{1,0:T(2,128)S(1)}, f32[2,512]{1,0:T(2,128)S(1)}, u32[]{:S(2)}, u32[]{:S(2)}) collective-permute-start(f32[2,512]{1,0:T(2,128)S(1)} %get-tuple-element.63.refs_5_), channel_id=1, source_target_pairs={{0,8},{8,16},{16,24},{24,0},{1,9},{9,17},{17,25},{25,1},{2,10},{10... | collective-permute-start | bytes 12296 | tf_op jit(solution)/shard_map/ppermute | solution.py:51
  18.0 1.4 %collective-permute-start.7 = (f32[2,512]{1,0:T(2,128)S(1)}, f32[2,512]{1,0:T(2,128)S(1)}, u32[]{:S(2)}, u32[]{:S(2)}) collective-permute-start(f32[2,512]{1,0:T(2,128)S(1)} %get-tuple-element.63.refs_5_), channel_id=1, source_target_pairs={{0,24},{8,0},{16,8},{24,16},{1,25},{9,1},{17,9},{25,17},{2,26},{10... | collective-permute-start | bytes 12296 | tf_op jit(solution)/shard_map/ppermute | solution.py:51
  19.5 1.5 %collective-permute-start.8 = (f32[2,512]{1,0:T(2,128)S(1)}, f32[2,512]{1,0:T(2,128)S(1)}, u32[]{:S(2)}, u32[]{:S(2)}) collective-permute-start(f32[2,512]{1,0:T(2,128)S(1)} %get-tuple-element.63.refs_5_), channel_id=1, source_target_pairs={{0,16},{8,24},{16,0},{24,8},{1,17},{9,25},{17,1},{25,9},{2,18},{10... | collective-permute-start | bytes 12296 | tf_op jit(solution)/shard_map/ppermute | solution.py:51
  21.0 0.1 collective-permute-done.6.refs_6_
  21.0 0.6 %collective-permute-done.7.refs_7_ = f32[2,512]{1,0:T(2,128)S(1)} collective-permute-done((f32[2,512]{1,0:T(2,128)S(1)}, f32[2,512]{1,0:T(2,128)S(1)}, u32[]{:S(2)}, u32[]{:S(2)}) %collective-permute-start.7) | collective-permute-done | bytes 4128 | tf_op jit(solution)/shard_map/ppermute | solution.py:51
  21.6 1.4 %collective-permute-done.8.refs_8_ = f32[2,512]{1,0:T(2,128)S(1)} collective-permute-done((f32[2,512]{1,0:T(2,128)S(1)}, f32[2,512]{1,0:T(2,128)S(1)}, u32[]{:S(2)}, u32[]{:S(2)}) %collective-permute-start.8) | collective-permute-done | bytes 4128 | tf_op jit(solution)/shard_map/ppermute | solution.py:51
  23.1 0.8 %state_grads_other.1 = (bf16[1,512,128]{2,1,0:T(8,128)(2,1)S(1)}, f32[1,512]{1,0:T(1,128)S(1)}, f32[512,128]{1,0:T(8,128)S(1)}, f32[512,128]{1,0:T(8,128)S(1)}, ...) custom-call(s32[1]{0:T(128)} %bitcast.position_ref.refs_0_, ...), custom_call_target="tpu_custom_call" | custom-call | flops 50331648 | bytes 1118212 | tf_op jit(solution)/shard_map/state_grads_other/pallas_call | solution.py:69
  23.8 0.1 collective-permute-start.10
  23.9 0.6 %state_grads_mine.1 = (bf16[2,512,128]{2,1,0:T(8,128)(2,1)S(1)}, f32[1,128,128]{2,1,0:T(8,128)S(1)}, f32[2,1,128,128]{3,2,1,0:T(8,128)S(1)}, f32[2,512,128]{2,1,0:T(8,128)S(1)}, bf16[3,2,128,128]{3,2,1,0:T(8,128)(2,1)S(1)}) custom-call(s32[1]{0:T(128)} %bitcast.position_ref.refs_0_, f32[1,512,128]{2,1,0:T(8,128)S(1)} %get-tuple-element.60.attn_ref, ...), custom_call_target="tpu_custom_call" | custom-call | flops 50331648 | bytes 2215940 | tf_op jit(solution)/shard_map/state_grads_mine/pallas_call | solution.py:69
  24.5 0.7 %collective-permute-done.10.came_ref = f32[2,1,128,128]{3,2,1,0:T(8,128)S(1)} collective-permute-done((f32[2,1,128,128]{3,2,1,0:T(8,128)S(1)}, f32[2,1,128,128]{3,2,1,0:T(8,128)S(1)}, u32[]{:S(2)}, u32[]{:S(2)}) %collective-permute-start.10) | collective-permute-done | bytes 131104 | tf_op jit(solution)/shard_map/ppermute | solution.py:33
  25.3 3.0 %collective-permute-start.11 = (f32[1,128,128]{2,1,0:T(8,128)S(1)}, f32[1,128,128]{2,1,0:T(8,128)S(1)}, u32[]{:S(2)}, u32[]{:S(2)}) collective-permute-start(f32[1,128,128]{2,1,0:T(8,128)S(1)} %get-tuple-element.82), channel_id=1, source_target_pairs={{0,6},{1,7},{2,4},{3,5},{4,2},{5,3},{6,0},{7,1},{8,14},{9,15},{10,... | collective-permute-start | bytes 196616 | tf_op jit(solution)/shard_map/ppermute | solution.py:64
  28.3 0.0 collective-permute-start.12
  28.3 1.4 %collective-permute-start.13 = (f32[1,128,128]{2,1,0:T(8,128)S(1)}, f32[1,128,128]{2,1,0:T(8,128)S(1)}, u32[]{:S(2)}, u32[]{:S(2)}) collective-permute-start(f32[1,128,128]{2,1,0:T(8,128)S(1)} %get-tuple-element.84), channel_id=1, source_target_pairs={{0,2},{1,3},{2,0},{3,1},{4,6},{5,7},{6,4},{7,5},{8,10},{9,11},{10,... | collective-permute-start | bytes 196616 | tf_op jit(solution)/shard_map/ppermute | solution.py:64
  29.8 0.0 collective-permute-start.15
  29.8 0.5 %collective-permute-start.9 = (f32[1,128,128]{2,1,0:T(8,128)S(1)}, f32[1,128,128]{2,1,0:T(8,128)S(1)}, u32[]{:S(2)}, u32[]{:S(2)}) collective-permute-start(f32[1,128,128]{2,1,0:T(8,128)S(1)} %get-tuple-element.79), channel_id=1, source_target_pairs={{0,1},{1,0},{2,3},{3,2},{4,5},{5,4},{6,7},{7,6},{8,9},{9,8},{10,11... | collective-permute-start | bytes 196616 | tf_op jit(solution)/shard_map/ppermute | solution.py:33
  30.3 2.8 %local_backward.1 = (f32[1024,128]{1,0:T(8,128)}, f32[1024,128]{1,0:T(8,128)}, f32[2,512,128]{2,1,0:T(8,128)S(1)}, f32[2,512,128]{2,1,0:T(8,128)S(1)}) custom-call(bf16[2,512,128]{2,1,0:T(8,128)(2,1)S(1)} %get-tuple-element.69.ag_ref, bf16[2,512,128]{2,1,0:T(8,128)(2,1)S(1)} %get-tuple-element.52.refs_2_.refs_3_.qd_ref, ...), custom_call_target="tpu_custom_call" | custom-call | flops 536870912 | bytes 3398656 | tf_op jit(solution)/shard_map/local_backward/pallas_call | solution.py:69
  33.0 0.0 collective-permute-done.11
  33.0 1.4 %collective-permute-done.12 = f32[1,128,128]{2,1,0:T(8,128)S(1)} collective-permute-done((f32[1,128,128]{2,1,0:T(8,128)S(1)}, f32[1,128,128]{2,1,0:T(8,128)S(1)}, u32[]{:S(2)}, u32[]{:S(2)}) %collective-permute-start.12) | collective-permute-done | bytes 65568 | tf_op jit(solution)/shard_map/ppermute | solution.py:64
  34.4 0.0 collective-permute-done.13
  34.4 0.1 collective-permute-start.14
  34.5 0.0 collective-permute-done.15.near_ref
  34.5 0.2 key_value_mine.1
  34.7 0.0 collective-permute-done.9.near_ref
  34.8 1.0 %collective-permute-done.14.total_ref = f32[1,128,128]{2,1,0:T(8,128)S(1)} collective-permute-done((f32[1,128,128]{2,1,0:T(8,128)S(1)}, f32[1,128,128]{2,1,0:T(8,128)S(1)}, u32[]{:S(2)}, u32[]{:S(2)}) %collective-permute-start.14) | collective-permute-done | bytes 65568 | tf_op jit(solution)/shard_map/ppermute | solution.py:33
  35.7 1.2 %key_value_other.1 = (f32[1024,128]{1,0:T(8,128)}, f32[1024,128]{1,0:T(8,128)}) custom-call(s32[1]{0:T(128)} %bitcast.position_ref.refs_0_, f32[1,128,128]{2,1,0:T(8,128)S(1)} %collective-permute-done.9.near_ref, f32[1,128,128]{2,1,0:T(8,128)S(1)} %collective-permute-done.14.total_ref, bf16[2,512,128]{2,1,0:T(8,128)(2,1)S(1)} %get-tuple-element.70.kd_ref, ...), custom_call_target="tpu_custom_call" | custom-call | flops 33554432 | bytes 2228228 | tf_op jit(solution)/shard_map/key_value_other/pallas_call | solution.py:69
  (12 shorter events, 0.1 us)
Async XLA Ops:
  0.6 8.6 %copy-start = (bf16[512,2,128]{2,1,0:T(2,128)(2,1)S(1)}, bf16[512,2,128]{2,1,0:T(2,128)(2,1)}, u32[]{:S(2)}) copy-start(bf16[512,2,128]{2,1,0:T(2,128)(2,1)} %param.8) | copy-start | bytes 786436
  0.6 8.6 %copy-start.1 = (bf16[512,2,128]{2,1,0:T(2,128)(2,1)S(1)}, bf16[512,2,128]{2,1,0:T(2,128)(2,1)}, u32[]{:S(2)}) copy-start(bf16[512,2,128]{2,1,0:T(2,128)(2,1)} %param.9) | copy-start | bytes 786436
  0.7 8.6 %copy-start.2 = (bf16[512,2,128]{2,1,0:T(2,128)(2,1)S(1)}, bf16[512,2,128]{2,1,0:T(2,128)(2,1)}, u32[]{:S(2)}) copy-start(bf16[512,2,128]{2,1,0:T(2,128)(2,1)} %param.7) | copy-start | bytes 786436
  2.0 1.5 %collective-permute-start = (f32[2,128,128]{2,1,0:T(8,128)S(1)}, f32[2,128,128]{2,1,0:T(8,128)S(1)}, u32[]{:S(2)}, u32[]{:S(2)}) collective-permute-start(f32[2,128,128]{2,1,0:T(8,128)S(1)} %fusion), channel_id=1, source_target_pairs={{0,1},{1,0},{2,3},{3,2},{4,5},{5,4},{6,7},{7,6},{8,9},{9,8},{10,11... | collective-permute-start | bytes 393224 | tf_op jit(solution)/shard_map/ppermute | solution.py:33
  3.6 5.7 %copy-start.4 = (f32[8,2,13]{2,1,0:T(2,128)S(1)}, f32[8,2,13]{2,1,0:T(2,128)}, u32[]{:S(2)}) copy-start(f32[8,2,13]{2,1,0:T(2,128)} %table_ref.1) | copy-start | bytes 2500
  3.6 10.1 %collective-permute-start.1 = (f32[1,128,128]{2,1,0:T(8,128)S(1)}, f32[1,128,128]{2,1,0:T(8,128)S(1)}, u32[]{:S(2)}, u32[]{:S(2)}) collective-permute-start(f32[1,128,128]{2,1,0:T(8,128)S(1)} %dynamic-slice_add_fusion), channel_id=1, source_target_pairs={{0,6},{1,7},{2,4},{3,5},{4,2},{5,3},{6,0},{7,1},{8,14},{9,15},{10,... | collective-permute-start | bytes 196616 | tf_op jit(solution)/shard_map/ppermute | solution.py:64
  8.6 5.9 %collective-permute-start.2 = (f32[1,128,128]{2,1,0:T(8,128)S(1)}, f32[1,128,128]{2,1,0:T(8,128)S(1)}, u32[]{:S(2)}, u32[]{:S(2)}) collective-permute-start(f32[1,128,128]{2,1,0:T(8,128)S(1)} %dynamic-slice_add_fusion), channel_id=1, source_target_pairs={{0,4},{1,5},{2,6},{3,7},{4,0},{5,1},{6,2},{7,3},{8,12},{9,13},{10,... | collective-permute-start | bytes 196616 | tf_op jit(solution)/shard_map/ppermute | solution.py:64
  8.6 5.9 %collective-permute-start.3 = (f32[1,128,128]{2,1,0:T(8,128)S(1)}, f32[1,128,128]{2,1,0:T(8,128)S(1)}, u32[]{:S(2)}, u32[]{:S(2)}) collective-permute-start(f32[1,128,128]{2,1,0:T(8,128)S(1)} %dynamic-slice_add_fusion), channel_id=1, source_target_pairs={{0,2},{1,3},{2,0},{3,1},{4,6},{5,7},{6,4},{7,5},{8,10},{9,11},{10,... | collective-permute-start | bytes 196616 | tf_op jit(solution)/shard_map/ppermute | solution.py:64
  9.2 0.7 %copy-start.6 = (s32[512]{0:T(512)S(1)}, s32[512]{0:T(512)}, u32[]{:S(2)}) copy-start(s32[512]{0:T(512)} %param.10) | copy-start | bytes 6148
  9.2 0.7 %copy-start.5 = (f32[2,128]{1,0:T(2,128)S(1)}, f32[2,128]{1,0:T(2,128)}, u32[]{:S(2)}) copy-start(f32[2,128]{1,0:T(2,128)} %gain_ref.1) | copy-start | bytes 3076
  9.9 0.9 %copy-start.3 = (bf16[512,2,128]{2,1,0:T(2,128)(2,1)S(1)}, bf16[512,2,128]{2,1,0:T(2,128)(2,1)}, u32[]{:S(2)}) copy-start(bf16[512,2,128]{2,1,0:T(2,128)(2,1)} %param.13) | copy-start | bytes 786436
  14.5 1.3 %collective-permute-start.4 = (f32[1,128,128]{2,1,0:T(8,128)S(1)}, f32[1,128,128]{2,1,0:T(8,128)S(1)}, u32[]{:S(2)}, u32[]{:S(2)}) collective-permute-start(f32[1,128,128]{2,1,0:T(8,128)S(1)} %get-tuple-element.58.refs_6_), channel_id=1, source_target_pairs={{0,1},{1,0},{2,3},{3,2},{4,5},{5,4},{6,7},{7,6},{8,9},{9,8},{10,11... | collective-permute-start | bytes 196616 | tf_op jit(solution)/shard_map/ppermute | solution.py:33
  14.6 1.4 %collective-permute-start.5 = (f32[1,128,128]{2,1,0:T(8,128)S(1)}, f32[1,128,128]{2,1,0:T(8,128)S(1)}, u32[]{:S(2)}, u32[]{:S(2)}) collective-permute-start(f32[1,128,128]{2,1,0:T(8,128)S(1)} %get-tuple-element.59.refs_7_), channel_id=1, source_target_pairs={{0,1},{1,0},{2,3},{3,2},{4,5},{5,4},{6,7},{7,6},{8,9},{9,8},{10,11... | collective-permute-start | bytes 196616 | tf_op jit(solution)/shard_map/ppermute | solution.py:33
  16.5 4.6 %collective-permute-start.6 = (f32[2,512]{1,0:T(2,128)S(1)}, f32[2,512]{1,0:T(2,128)S(1)}, u32[]{:S(2)}, u32[]{:S(2)}) collective-permute-start(f32[2,512]{1,0:T(2,128)S(1)} %get-tuple-element.63.refs_5_), channel_id=1, source_target_pairs={{0,8},{8,16},{16,24},{24,0},{1,9},{9,17},{17,25},{25,1},{2,10},{10... | collective-permute-start | bytes 12296 | tf_op jit(solution)/shard_map/ppermute | solution.py:51
  18.0 3.6 %collective-permute-start.7 = (f32[2,512]{1,0:T(2,128)S(1)}, f32[2,512]{1,0:T(2,128)S(1)}, u32[]{:S(2)}, u32[]{:S(2)}) collective-permute-start(f32[2,512]{1,0:T(2,128)S(1)} %get-tuple-element.63.refs_5_), channel_id=1, source_target_pairs={{0,24},{8,0},{16,8},{24,16},{1,25},{9,1},{17,9},{25,17},{2,26},{10... | collective-permute-start | bytes 12296 | tf_op jit(solution)/shard_map/ppermute | solution.py:51
  19.5 3.6 %collective-permute-start.8 = (f32[2,512]{1,0:T(2,128)S(1)}, f32[2,512]{1,0:T(2,128)S(1)}, u32[]{:S(2)}, u32[]{:S(2)}) collective-permute-start(f32[2,512]{1,0:T(2,128)S(1)} %get-tuple-element.63.refs_5_), channel_id=1, source_target_pairs={{0,16},{8,24},{16,0},{24,8},{1,17},{9,25},{17,1},{25,9},{2,18},{10... | collective-permute-start | bytes 12296 | tf_op jit(solution)/shard_map/ppermute | solution.py:51
  23.8 1.4 %collective-permute-start.10 = (f32[2,1,128,128]{3,2,1,0:T(8,128)S(1)}, f32[2,1,128,128]{3,2,1,0:T(8,128)S(1)}, u32[]{:S(2)}, u32[]{:S(2)}) collective-permute-start(f32[2,1,128,128]{3,2,1,0:T(8,128)S(1)} %get-tuple-element.81), channel_id=1, source_target_pairs={{0,1},{1,0},{2,3},{3,2},{4,5},{5,4},{6,7},{7,6},{8,9},{9,8},{10,11... | collective-permute-start | bytes 393224 | tf_op jit(solution)/shard_map/ppermute | solution.py:33
  25.3 7.7 %collective-permute-start.11 = (f32[1,128,128]{2,1,0:T(8,128)S(1)}, f32[1,128,128]{2,1,0:T(8,128)S(1)}, u32[]{:S(2)}, u32[]{:S(2)}) collective-permute-start(f32[1,128,128]{2,1,0:T(8,128)S(1)} %get-tuple-element.82), channel_id=1, source_target_pairs={{0,6},{1,7},{2,4},{3,5},{4,2},{5,3},{6,0},{7,1},{8,14},{9,15},{10,... | collective-permute-start | bytes 196616 | tf_op jit(solution)/shard_map/ppermute | solution.py:64
  28.3 6.1 %collective-permute-start.12 = (f32[1,128,128]{2,1,0:T(8,128)S(1)}, f32[1,128,128]{2,1,0:T(8,128)S(1)}, u32[]{:S(2)}, u32[]{:S(2)}) collective-permute-start(f32[1,128,128]{2,1,0:T(8,128)S(1)} %get-tuple-element.83), channel_id=1, source_target_pairs={{0,4},{1,5},{2,6},{3,7},{4,0},{5,1},{6,2},{7,3},{8,12},{9,13},{10,... | collective-permute-start | bytes 196616 | tf_op jit(solution)/shard_map/ppermute | solution.py:64
  28.3 6.1 %collective-permute-start.13 = (f32[1,128,128]{2,1,0:T(8,128)S(1)}, f32[1,128,128]{2,1,0:T(8,128)S(1)}, u32[]{:S(2)}, u32[]{:S(2)}) collective-permute-start(f32[1,128,128]{2,1,0:T(8,128)S(1)} %get-tuple-element.84), channel_id=1, source_target_pairs={{0,2},{1,3},{2,0},{3,1},{4,6},{5,7},{6,4},{7,5},{8,10},{9,11},{10,... | collective-permute-start | bytes 196616 | tf_op jit(solution)/shard_map/ppermute | solution.py:64
  29.8 4.7 %collective-permute-start.15 = (f32[1,128,128]{2,1,0:T(8,128)S(1)}, f32[1,128,128]{2,1,0:T(8,128)S(1)}, u32[]{:S(2)}, u32[]{:S(2)}) collective-permute-start(f32[1,128,128]{2,1,0:T(8,128)S(1)} %get-tuple-element.91), channel_id=1, source_target_pairs={{0,1},{1,0},{2,3},{3,2},{4,5},{5,4},{6,7},{7,6},{8,9},{9,8},{10,11... | collective-permute-start | bytes 196616 | tf_op jit(solution)/shard_map/ppermute | solution.py:33
  29.8 5.0 %collective-permute-start.9 = (f32[1,128,128]{2,1,0:T(8,128)S(1)}, f32[1,128,128]{2,1,0:T(8,128)S(1)}, u32[]{:S(2)}, u32[]{:S(2)}) collective-permute-start(f32[1,128,128]{2,1,0:T(8,128)S(1)} %get-tuple-element.79), channel_id=1, source_target_pairs={{0,1},{1,0},{2,3},{3,2},{4,5},{5,4},{6,7},{7,6},{8,9},{9,8},{10,11... | collective-permute-start | bytes 196616 | tf_op jit(solution)/shard_map/ppermute | solution.py:33
  34.4 1.3 %collective-permute-start.14 = (f32[1,128,128]{2,1,0:T(8,128)S(1)}, f32[1,128,128]{2,1,0:T(8,128)S(1)}, u32[]{:S(2)}, u32[]{:S(2)}) collective-permute-start(f32[1,128,128]{2,1,0:T(8,128)S(1)} %add_add_fusion.total_ref), channel_id=1, source_target_pairs={{0,1},{1,0},{2,3},{3,2},{4,5},{5,4},{6,7},{7,6},{8,9},{9,8},{10,11... | collective-permute-start | bytes 196616 | tf_op jit(solution)/shard_map/ppermute | solution.py:33

commit v6 on v5

--- a/solution.py
+++ b/solution.py
@@ -65,7 +65,7 @@
     return result
 
 
-def call(kernel, out_shape, args, specs, scratch=(), flops=0, name=None, outs=VMEM):
+def call(kernel, out_shape, args, specs, scratch=(), flops=0, name=None, outs=VMEM, aliases={}):
     return pl.pallas_call(
         kernel,
         out_shape=out_shape,
@@ -79,6 +79,7 @@
             bytes_accessed=sum(a.size * a.dtype.itemsize for a in args),
         ),
         name=name,
+        input_output_aliases=aliases,
     )(*args)
 
 
@@ -103,27 +104,21 @@
         tw_ref[head] = lax.dot_general(one_hot, table, TN, precision=exact_mode, preferred_element_type=F32)
 
 
-def local_forward(sizes, scale, position_ref, q_ref, k_ref, v_ref, g_ref, gain_hbm, pick_ref, table_ref,
-                  inner_ref, p_ref, w_ref, qd_ref, kd_ref, vd_ref, gg_ref, tw_ref, wide, raw, gain_ref, sems):
+def gain_rows(sizes, g_ref, gain_ref, gg_ref, wide):
+    heads, length = sizes
+
+    def store(head, value):
+        gg_ref[head] = value * gain_ref[head:head + 1, :]
+    split_heads(g_ref, wide, heads, length, store)
+
+
+def local_forward(sizes, q_ref, k_ref, v_ref, tw_ref, inner_ref, p_ref, w_ref, qd_ref, kd_ref, vd_ref, wide):
     heads, length, levels, block, bits = sizes
     base = block.bit_length() - 1
-    copies = [pltpu.make_async_copy(gain_hbm, gain_ref, sems.at[4])]
-    for n, source in enumerate((k_ref, v_ref, q_ref, g_ref)):
-        copies.append(pltpu.make_async_copy(source, raw.at[n], sems.at[n]))
-    for copy in copies:
-        copy.start()
-    level_rows(sizes, scale, position_ref, pick_ref, table_ref, tw_ref)
-    for n, target in enumerate((kd_ref, vd_ref, qd_ref)):
+    for source, target in ((k_ref, kd_ref), (v_ref, vd_ref), (q_ref, qd_ref)):
         def store(head, value, target=target):
             target[head] = value.astype(BF16)
-        copies[n + 1].wait()
-        split_heads(raw.at[n], wide, heads, length, store)
-    copies[4].wait()
-    copies[0].wait()
-
-    def store_gain(head, value):
-        gg_ref[head] = value * gain_ref[head:head + 1, :]
-    split_heads(raw.at[3], wide, heads, length, store_gain)
+        split_heads(source, wide, heads, length, store)
     row = lax.broadcasted_iota(jnp.int32, (block, block), 0)
     column = lax.broadcasted_iota(jnp.int32, (block, block), 1)
     differs = row ^ column
@@ -348,50 +343,32 @@
             dv_ref[head, cols, :] = dot(p_ref[head, rest, cols], ag_ref[head, rest, :], TN)
 
 
-def final_mine(sizes, position_ref, near_ref, total_ref, kd_ref, vd_ref, dk_ref, dv_ref, key_ref, value_ref):
+def final_heads(sizes, start, position_ref, near_ref, total_ref, kd_ref, vd_ref, dk_ref, dv_ref,
+                key_ref, value_ref, key_hbm, value_hbm, sems):
     heads, length, block = sizes
     half = heads // 2
-    core = position_ref[0] & 1
-    keep = (1 - core).astype(F32)
+    keep = (1 - (position_ref[0] & 1)).astype(F32)
+    copies = []
     for h in range(half):
-        head = core * half + h
+        head = start + h
         back = (total_ref[h] + keep * near_ref[h]).astype(BF16)
         key_ref[h] = dk_ref[head] + dot(vd_ref[head], back, NT)
+        copies.append(pltpu.make_async_copy(key_ref.at[h], key_hbm.at[:, head, :], sems.at[0, h]))
+        copies[-1].start()
         value_ref[h] = dv_ref[head] + dot(kd_ref[head], back, NN)
-
-
-def final_other(sizes, position_ref, near_ref, total_ref, kd_ref, vd_ref, dk_ref, dv_ref, mine_key_ref, mine_value_ref,
-                key_hbm, value_hbm, back_ref, key_ref, value_ref, sems):
-    heads, length, block = sizes
-    half = heads // 2
-    core = position_ref[0] & 1
-    keep = (1 - core).astype(F32)
-    away = (1 - core) * half
-    for h in range(half):
-        back_ref[h] = (total_ref[h] + keep * near_ref[h]).astype(BF16)
-    copies = []
-    for i in range(length // block):
-        rows = slice(i * block, (i + 1) * block)
-        new = []
-        for h in range(half):
-            head = away + h
-            back = back_ref[h]
-            new.append((dk_ref[head, rows, :] + dot(vd_ref[head, rows, :], back, NT),
-                        dv_ref[head, rows, :] + dot(kd_ref[head, rows, :], back, NN)))
-        for h in range(half):
-            old = (mine_key_ref[h, rows, :], mine_value_ref[h, rows, :])
-            for n, target in enumerate((key_ref, value_ref)):
-                low = jnp.where(core == 0, old[n], new[h][n])
-                high = jnp.where(core == 0, new[h][n], old[n])
-                target[pl.ds(i * block * heads + h, block, stride=heads), :] = low
-                target[pl.ds(i * block * heads + half + h, block, stride=heads), :] = high
-        chunk = pl.ds(i * block * heads, block * heads)
-        for n, (source, target) in enumerate(((key_ref, key_hbm), (value_ref, value_hbm))):
-            copy = pltpu.make_async_copy(source.at[chunk], target.at[chunk], sems.at[n, i])
-            copy.start()
-            copies.append(copy)
+        copies.append(pltpu.make_async_copy(value_ref.at[h], value_hbm.at[:, head, :], sems.at[1, h]))
+        copies[-1].start()
     for copy in copies:
         copy.wait()
+
+
+def final_mine(sizes, position_ref, *refs):
+    final_heads(sizes, (position_ref[0] & 1) * (sizes[0] // 2), position_ref, *refs[:6], *refs[8:10], *refs[6:8], refs[10])
+
+
+def final_other(sizes, position_ref, *refs):
+    start = (1 - (position_ref[0] & 1)) * (sizes[0] // 2)
+    final_heads(sizes, start, position_ref, *refs[:6], *refs[10:12], *refs[8:10], refs[12])
 
 
 def shards(query_rows, key_rows, value_rows, level_pick, level_table, norm_gain, out_grad):
@@ -408,6 +385,17 @@
 
     own = jnp.einsum("shd,she->hde", key_rows, value_rows, preferred_element_type=F32)
     near = swapped(own, "seq", 0)
+    sizes = (heads, length, levels, block, bits)
+    rows = length * heads
+    flat = lambda a: a.reshape(rows, width)
+    local_flops = heads * length * length * width
+    weights = call(
+        functools.partial(level_rows, sizes, scale),
+        shape((heads, length, levels), F32),
+        (place_arg, level_pick.reshape(1, length), level_table),
+        [SMEM, VMEM, VMEM],
+        name="level_rows",
+    )
     pair = own + near
 
     block_sum = lax.dynamic_slice(
@@ -417,12 +405,8 @@
     group = 1 << far
     received = turned([block_sum] * (group - 1), "seq", group)
 
-    rows = length * heads
-    flat = lambda a: a.reshape(rows, width)
-    local_flops = heads * length * length * width
-    sizes = (heads, length, levels, block, bits)
-    inner, probs, diag, qd, kd, vd, gg, weights = call(
-        functools.partial(local_forward, sizes, scale),
+    inner, probs, diag, qd, kd, vd = call(
+        functools.partial(local_forward, sizes),
         (
             shape((heads, length, width), F32),
             shape((heads, length, length), BF16),
@@ -430,30 +414,22 @@
             shape((heads, length, width), BF16),
             shape((heads, length, width), BF16),
             shape((heads, length, width), BF16),
-            shape((heads, length, width), F32),
-            shape((heads, length, levels), F32),
         ),
-        (
-            place_arg,
-            flat(query_rows),
-            flat(key_rows),
-            flat(value_rows),
-            flat(out_grad),
-            norm_gain,
-            level_pick.reshape(1, length),
-            level_table,
-        ),
-        [SMEM, HBM, HBM, HBM, HBM, HBM, VMEM, VMEM],
-        [
-            pltpu.VMEM((rows, width), F32),
-            pltpu.VMEM((4, rows, width), BF16),
-            pltpu.VMEM((heads, width), F32),
-            pltpu.SemaphoreType.DMA((5,)),
-        ],
+        (flat(query_rows), flat(key_rows), flat(value_rows), weights),
+        [VMEM] * 4,
+        [pltpu.VMEM((rows, width), F32)],
         flops=4 * local_flops,
         name="local_forward",
     )
-    inner, received = lax.optimization_barrier((inner, received))
+    gg = call(
+        functools.partial(gain_rows, (heads, length)),
+        shape((heads, length, width), F32),
+        (flat(out_grad), norm_gain),
+        [VMEM] * 2,
+        [pltpu.VMEM((rows, width), F32)],
+        name="gain_rows",
+    )
+    inner, gg, received = lax.optimization_barrier((inner, gg, received))
     state = shape((half, width, width), F32)
     mine = call(
         functools.partial(combine_kernel, group),
@@ -558,28 +534,32 @@
 
     final_sizes = (heads, length, block)
     final_flops = 2 * heads * length * width * width
-    key_mine, value_mine = call(
+    whole = (shape((length, heads, width), F32), shape((length, heads, width), F32))
+    scratch = [
+        pltpu.VMEM((half, length, width), F32),
+        pltpu.VMEM((half, length, width), F32),
+        pltpu.SemaphoreType.DMA((2, half)),
+    ]
+    started = call(
         functools.partial(final_mine, final_sizes),
-        (shape((half, length, width), F32), shape((half, length, width), F32)),
+        whole,
         (place_arg, near_mine, total, kd, vd, key_part, value_part),
         [SMEM] + [VMEM] * 6,
+        scratch,
         flops=final_flops,
         name="key_value_mine",
+        outs=HBM,
     )
     key_grad, value_grad = call(
         functools.partial(final_other, final_sizes),
-        (shape((rows, width), F32), shape((rows, width), F32)),
-        (place_arg, near_other, other, kd, vd, key_part, value_part, key_mine, value_mine),
-        [SMEM] + [VMEM] * 8,
-        [
-            pltpu.VMEM((half, width, width), BF16),
-            pltpu.VMEM((rows, width), F32),
-            pltpu.VMEM((rows, width), F32),
-            pltpu.SemaphoreType.DMA((2, length // block)),
-        ],
+        whole,
+        (place_arg, near_other, other, kd, vd, key_part, value_part, *started),
+        [SMEM] + [VMEM] * 6 + [HBM] * 2,
+        scratch,
         flops=final_flops,
         name="key_value_other",
         outs=HBM,
+        aliases={7: 0, 8: 1},
     )
     return tuple(a.reshape(length, heads, width) for a in (normed, query_grad, key_grad, value_grad))
 

time: 37.1 us -> 36.9 us (level)
  local copies, waits for them, and re-layouts: 1.64 us -> 1.13 us
  Pallas kernels: 9.38 us -> 9.86 us
    ppermute x7, waiting for transfers between devices: 3.09 us -> 2.28 us  [swapped(): return lax.ppermute(block, axis, route)]
    ppermute x6, waiting for transfers between devices: 2.2 us -> 2.85 us  [turned(): result.append(lax.ppermute(block, axis, route))]
    unnamed x14, local copies, waits for them, and re-layouts: 1.63 us -> 1.12 us
    pallas_call x10 -> x12, Pallas kernels: 9.38 us -> 9.86 us  [call(): pl.pallas_call(kernel, out_shape=out_shape, in_specs=specs, out_specs=jax...]
  transfers between devices with their start and end apart: 16 -> 16, of which waited for: 10 -> 10; matrix products, arithmetic and copies ran while one was open for 0% -> 0% of each run, Pallas kernels for 19% -> 20%
where the time goes in v6:
time: 36.9 us; the launch traced here: 36.7 us
  starting transfers between devices  16.4 us (44%)
  Pallas kernels  9.86 us (27%)
  waiting for transfers between devices  7.22 us (20%)
  matrix products  1.35 us (4%)
  local copies, waits for them, and re-layouts  1.13 us (3%)
  between operations  0.78 us (2%)
    ppermute x6, starting transfers between devices, turned(): result.append(lax.ppermute(block, axis, route))  10.1 us
    pallas_call x12, Pallas kernels, call(): pl.pallas_call(kernel, out_shape=out_shape, in_specs=specs, out_specs=jax...  9.86 us
    ppermute x3, starting transfers between devices, summands(): lax.ppermute(block, axis, [(i, (i + step) % count) for i in range(count)])  4.49 us
    ppermute x6, waiting for transfers between devices, turned(): result.append(lax.ppermute(block, axis, route))  2.85 us
    ppermute x7, waiting for transfers between devices, swapped(): return lax.ppermute(block, axis, route)  2.28 us
    ppermute x3, waiting for transfers between devices, summands(): lax.ppermute(block, axis, [(i, (i + step) % count) for i in range(count)])  2.09 us
    ppermute x7, starting transfers between devices, swapped(): return lax.ppermute(block, axis, route)  1.74 us
    dot_general x1, matrix products, shards(): jnp.einsum('shd,she->hde', key_rows, value_rows, preferred_element_type=F32)  1.35 us
  transfers between devices with their start and end apart: 16, of which 10 were waited for; matrix products, arithmetic and copies ran while one was open for 0% of the time, Pallas kernels for 20%

profile of v6, /device:TPU:0, one launch (start us, length us, event | category | flops | bytes accessed | tf_op | source)
XLA Modules:
  0.0 36.7 jit_solution(2769446736811350995)
XLA Ops:
  0.6 1.3 %fusion = f32[2,128,128]{2,1,0:T(8,128)S(1)} fusion(bf16[512,2,128]{2,1,0:T(2,128)(2,1)} %param.9, bf16[512,2,128]{2,1,0:T(2,128)(2,1)} %param.8), kind=kOutput, calls=%fused_computation | convolution fusion | flops 33554432 | bytes 655360 | tf_op jit(solution)/shard_map/shd,she->hde/dot_general | solution.py:386
  2.0 0.5 %collective-permute-start = (f32[2,128,128]{2,1,0:T(8,128)S(1)}, f32[2,128,128]{2,1,0:T(8,128)S(1)}, u32[]{:S(2)}, u32[]{:S(2)}) collective-permute-start(f32[2,128,128]{2,1,0:T(8,128)S(1)} %fusion), channel_id=1, source_target_pairs={{0,1},{1,0},{2,3},{3,2},{4,5},{5,4},{6,7},{7,6},{8,9},{9,8},{10,11... | collective-permute-start | bytes 393224 | tf_op jit(solution)/shard_map/ppermute | solution.py:33
  2.5 1.0 %collective-permute-done.refs_5_ = f32[2,128,128]{2,1,0:T(8,128)S(1)} collective-permute-done((f32[2,128,128]{2,1,0:T(8,128)S(1)}, f32[2,128,128]{2,1,0:T(8,128)S(1)}, u32[]{:S(2)}, u32[]{:S(2)}) %collective-permute-start) | collective-permute-done | bytes 131104 | tf_op jit(solution)/shard_map/ppermute | solution.py:33
  3.5 0.0 copy-start.5
  3.5 5.0 %collective-permute-start.1 = (f32[1,128,128]{2,1,0:T(8,128)S(1)}, f32[1,128,128]{2,1,0:T(8,128)S(1)}, u32[]{:S(2)}, u32[]{:S(2)}) collective-permute-start(f32[1,128,128]{2,1,0:T(8,128)S(1)} %dynamic-slice_add_fusion), channel_id=1, source_target_pairs={{0,6},{1,7},{2,4},{3,5},{4,2},{5,3},{6,0},{7,1},{8,14},{9,15},{10,... | collective-permute-start | bytes 196616 | tf_op jit(solution)/shard_map/ppermute | solution.py:64
  8.5 0.0 collective-permute-start.2
  8.5 0.6 %collective-permute-start.3 = (f32[1,128,128]{2,1,0:T(8,128)S(1)}, f32[1,128,128]{2,1,0:T(8,128)S(1)}, u32[]{:S(2)}, u32[]{:S(2)}) collective-permute-start(f32[1,128,128]{2,1,0:T(8,128)S(1)} %dynamic-slice_add_fusion), channel_id=1, source_target_pairs={{0,2},{1,3},{2,0},{3,1},{4,6},{5,7},{6,4},{7,5},{8,10},{9,11},{10,... | collective-permute-start | bytes 196616 | tf_op jit(solution)/shard_map/ppermute | solution.py:64
  9.2 0.1 gain_rows.1.refs_3_.refs_2_.gg_ref
  9.3 0.0 copy-start.6
  9.3 0.6 %copy-done.4 = f32[8,2,13]{2,1,0:T(2,128)S(1)} copy-done((f32[8,2,13]{2,1,0:T(2,128)S(1)}, f32[8,2,13]{2,1,0:T(2,128)}, u32[]{:S(2)}) %copy-start.4) | copy-done | bytes 856
  9.9 0.1 copy-done.6
  10.0 0.6 %level_rows.1.tw_ref.refs_4_ = f32[2,512,13]{2,1,0:T(8,128)S(1)} custom-call(s32[1]{0:T(128)} %bitcast.position_ref.refs_0_, s32[1,512]{1,0:T(1,128)S(1)} %bitcast.12, f32[8,2,13]{2,1,0:T(2,128)S(1)} %copy-done.4), custom_call_target="tpu_custom_call" | custom-call | bytes 2884 | tf_op jit(solution)/shard_map/level_rows/pallas_call | solution.py:69
  10.6 0.3 copy-done
  11.0 0.1 copy-done.1
  11.0 1.9 %local_forward.1 = (f32[2,512,128]{2,1,0:T(8,128)S(1)}, bf16[2,512,512]{2,1,0:T(8,128)(2,1)S(1)}, f32[8,128,128]{2,1,0:T(8,128)S(1)}, bf16[2,512,128]{2,1,0:T(8,...) custom-call(bf16[1024,128]{1,0:T(8,128)(2,1)S(1)} %bitcast.10, ...), custom_call_target="tpu_custom_call" | custom-call | flops 268435456 | bytes 839680 | tf_op jit(solution)/shard_map/local_forward/pallas_call | solution.py:69
  12.9 0.0 collective-permute-done.1.refs_0_
  13.0 1.5 %collective-permute-done.2.refs_1_ = f32[1,128,128]{2,1,0:T(8,128)S(1)} collective-permute-done((f32[1,128,128]{2,1,0:T(8,128)S(1)}, f32[1,128,128]{2,1,0:T(8,128)S(1)}, u32[]{:S(2)}, u32[]{:S(2)}) %collective-permute-start.2) | collective-permute-done | bytes 65568 | tf_op jit(solution)/shard_map/ppermute | solution.py:64
  14.4 0.0 collective-permute-done.3.refs_2_
  14.5 0.1 collective-permute-start.4
  14.5 0.5 %collective-permute-start.5 = (f32[1,128,128]{2,1,0:T(8,128)S(1)}, f32[1,128,128]{2,1,0:T(8,128)S(1)}, u32[]{:S(2)}, u32[]{:S(2)}) collective-permute-start(f32[1,128,128]{2,1,0:T(8,128)S(1)} %get-tuple-element.57.refs_7_), channel_id=1, source_target_pairs={{0,1},{1,0},{2,3},{3,2},{4,5},{5,4},{6,7},{7,6},{8,9},{9,8},{10,11... | collective-permute-start | bytes 196616 | tf_op jit(solution)/shard_map/ppermute | solution.py:33
  15.0 0.5 %cross_mine.1 = (f32[1,512,128]{2,1,0:T(8,128)S(1)}, f32[2,512]{1,0:T(2,128)S(1)}, bf16[3,1,128,128]{3,2,1,0:T(8,128)(2,1)S(1)}) custom-call(s32[1]{0:T(128)} %bitcast.position_ref.refs_0_, f32[2,512,128]{2,1,0:T(8,128)S(1)} %get-tuple-element.50.refs_1_, bf16[2,512,128]{2,1,0:T(8,128)(2,1)S(1)} %get-tuple-element.51.refs_2_.refs_3_.qd_ref, ...), custom_call_target="tpu_custom_call" | custom-call | flops 50331648 | bytes 1626116 | tf_op jit(solution)/shard_map/cross_mine/pallas_call | solution.py:69
  15.5 0.2 collective-permute-done.4.refs_7_
  15.8 0.2 collective-permute-done.5.refs_8_
  15.9 0.5 %cross_other.1 = (f32[1,512,128]{2,1,0:T(8,128)S(1)}, f32[2,512]{1,0:T(2,128)S(1)}, bf16[3,1,128,128]{3,2,1,0:T(8,128)(2,1)S(1)}) custom-call(s32[1]{0:T(128)} %bitcast.position_ref.refs_0_, f32[2,512,128]{2,1,0:T(8,128)S(1)} %get-tuple-element.50.refs_1_, bf16[2,512,128]{2,1,0:T(8,128)(2,1)S(1)} %get-tuple-element.51.refs_2_.refs_3_.qd_ref, ...), custom_call_target="tpu_custom_call" | custom-call | flops 50331648 | bytes 1630212 | tf_op jit(solution)/shard_map/cross_other/pallas_call | solution.py:69
  16.4 1.5 %collective-permute-start.6 = (f32[2,512]{1,0:T(2,128)S(1)}, f32[2,512]{1,0:T(2,128)S(1)}, u32[]{:S(2)}, u32[]{:S(2)}) collective-permute-start(f32[2,512]{1,0:T(2,128)S(1)} %get-tuple-element.61.refs_5_), channel_id=1, source_target_pairs={{0,8},{8,16},{16,24},{24,0},{1,9},{9,17},{17,25},{25,1},{2,10},{10... | collective-permute-start | bytes 12296 | tf_op jit(solution)/shard_map/ppermute | solution.py:51
  18.0 1.4 %collective-permute-start.7 = (f32[2,512]{1,0:T(2,128)S(1)}, f32[2,512]{1,0:T(2,128)S(1)}, u32[]{:S(2)}, u32[]{:S(2)}) collective-permute-start(f32[2,512]{1,0:T(2,128)S(1)} %get-tuple-element.61.refs_5_), channel_id=1, source_target_pairs={{0,24},{8,0},{16,8},{24,16},{1,25},{9,1},{17,9},{25,17},{2,26},{10... | collective-permute-start | bytes 12296 | tf_op jit(solution)/shard_map/ppermute | solution.py:51
  19.4 1.5 %collective-permute-start.8 = (f32[2,512]{1,0:T(2,128)S(1)}, f32[2,512]{1,0:T(2,128)S(1)}, u32[]{:S(2)}, u32[]{:S(2)}) collective-permute-start(f32[2,512]{1,0:T(2,128)S(1)} %get-tuple-element.61.refs_5_), channel_id=1, source_target_pairs={{0,16},{8,24},{16,0},{24,8},{1,17},{9,25},{17,1},{25,9},{2,18},{10... | collective-permute-start | bytes 12296 | tf_op jit(solution)/shard_map/ppermute | solution.py:51
  20.9 0.1 collective-permute-done.6.refs_6_
  21.0 0.6 %collective-permute-done.7.refs_7_ = f32[2,512]{1,0:T(2,128)S(1)} collective-permute-done((f32[2,512]{1,0:T(2,128)S(1)}, f32[2,512]{1,0:T(2,128)S(1)}, u32[]{:S(2)}, u32[]{:S(2)}) %collective-permute-start.7) | collective-permute-done | bytes 4128 | tf_op jit(solution)/shard_map/ppermute | solution.py:51
  21.6 1.4 %collective-permute-done.8.refs_8_ = f32[2,512]{1,0:T(2,128)S(1)} collective-permute-done((f32[2,512]{1,0:T(2,128)S(1)}, f32[2,512]{1,0:T(2,128)S(1)}, u32[]{:S(2)}, u32[]{:S(2)}) %collective-permute-start.8) | collective-permute-done | bytes 4128 | tf_op jit(solution)/shard_map/ppermute | solution.py:51
  23.0 0.8 %state_grads_other.1 = (bf16[1,512,128]{2,1,0:T(8,128)(2,1)S(1)}, f32[1,512]{1,0:T(1,128)S(1)}, f32[512,128]{1,0:T(8,128)S(1)}, f32[512,128]{1,0:T(8,128)S(1)}, ...) custom-call(s32[1]{0:T(128)} %bitcast.position_ref.refs_0_, ...), custom_call_target="tpu_custom_call" | custom-call | flops 50331648 | bytes 1118212 | tf_op jit(solution)/shard_map/state_grads_other/pallas_call | solution.py:69
  23.8 0.1 collective-permute-start.10
  23.9 0.6 %state_grads_mine.1 = (bf16[2,512,128]{2,1,0:T(8,128)(2,1)S(1)}, f32[1,128,128]{2,1,0:T(8,128)S(1)}, f32[2,1,128,128]{3,2,1,0:T(8,128)S(1)}, f32[2,512,128]{2,1,0:T(8,128)S(1)}, bf16[3,2,128,128]{3,2,1,0:T(8,128)(2,1)S(1)}) custom-call(s32[1]{0:T(128)} %bitcast.position_ref.refs_0_, f32[1,512,128]{2,1,0:T(8,128)S(1)} %get-tuple-element.58.attn_ref, ...), custom_call_target="tpu_custom_call" | custom-call | flops 50331648 | bytes 2215940 | tf_op jit(solution)/shard_map/state_grads_mine/pallas_call | solution.py:69
  24.5 0.7 %collective-permute-done.10.came_ref = f32[2,1,128,128]{3,2,1,0:T(8,128)S(1)} collective-permute-done((f32[2,1,128,128]{3,2,1,0:T(8,128)S(1)}, f32[2,1,128,128]{3,2,1,0:T(8,128)S(1)}, u32[]{:S(2)}, u32[]{:S(2)}) %collective-permute-start.10) | collective-permute-done | bytes 131104 | tf_op jit(solution)/shard_map/ppermute | solution.py:33
  25.3 2.5 %collective-permute-start.11 = (f32[1,128,128]{2,1,0:T(8,128)S(1)}, f32[1,128,128]{2,1,0:T(8,128)S(1)}, u32[]{:S(2)}, u32[]{:S(2)}) collective-permute-start(f32[1,128,128]{2,1,0:T(8,128)S(1)} %get-tuple-element.80), channel_id=1, source_target_pairs={{0,6},{1,7},{2,4},{3,5},{4,2},{5,3},{6,0},{7,1},{8,14},{9,15},{10,... | collective-permute-start | bytes 196616 | tf_op jit(solution)/shard_map/ppermute | solution.py:64
  27.8 0.1 collective-permute-start.12
  27.9 1.8 %collective-permute-start.13 = (f32[1,128,128]{2,1,0:T(8,128)S(1)}, f32[1,128,128]{2,1,0:T(8,128)S(1)}, u32[]{:S(2)}, u32[]{:S(2)}) collective-permute-start(f32[1,128,128]{2,1,0:T(8,128)S(1)} %get-tuple-element.82), channel_id=1, source_target_pairs={{0,2},{1,3},{2,0},{3,1},{4,6},{5,7},{6,4},{7,5},{8,10},{9,11},{10,... | collective-permute-start | bytes 196616 | tf_op jit(solution)/shard_map/ppermute | solution.py:64
  29.7 0.0 collective-permute-start.15
  29.7 0.5 %collective-permute-start.9 = (f32[1,128,128]{2,1,0:T(8,128)S(1)}, f32[1,128,128]{2,1,0:T(8,128)S(1)}, u32[]{:S(2)}, u32[]{:S(2)}) collective-permute-start(f32[1,128,128]{2,1,0:T(8,128)S(1)} %get-tuple-element.77), channel_id=1, source_target_pairs={{0,1},{1,0},{2,3},{3,2},{4,5},{5,4},{6,7},{7,6},{8,9},{9,8},{10,11... | collective-permute-start | bytes 196616 | tf_op jit(solution)/shard_map/ppermute | solution.py:33
  30.2 2.8 %local_backward.1 = (f32[1024,128]{1,0:T(8,128)}, f32[1024,128]{1,0:T(8,128)}, f32[2,512,128]{2,1,0:T(8,128)S(1)}, f32[2,512,128]{2,1,0:T(8,128)S(1)}) custom-call(bf16[2,512,128]{2,1,0:T(8,128)(2,1)S(1)} %get-tuple-element.67.ag_ref, bf16[2,512,128]{2,1,0:T(8,128)(2,1)S(1)} %get-tuple-element.51.refs_2_.refs_3_.qd_ref, ...), custom_call_target="tpu_custom_call" | custom-call | flops 536870912 | bytes 3398656 | tf_op jit(solution)/shard_map/local_backward/pallas_call | solution.py:69
  33.0 0.0 collective-permute-done.11
  33.0 1.4 %collective-permute-done.12 = f32[1,128,128]{2,1,0:T(8,128)S(1)} collective-permute-done((f32[1,128,128]{2,1,0:T(8,128)S(1)}, f32[1,128,128]{2,1,0:T(8,128)S(1)}, u32[]{:S(2)}, u32[]{:S(2)}) %collective-permute-start.12) | collective-permute-done | bytes 65568 | tf_op jit(solution)/shard_map/ppermute | solution.py:64
  34.3 0.0 collective-permute-done.13
  34.4 0.1 collective-permute-start.14
  34.4 0.0 collective-permute-done.15.refs_0_
  34.5 1.0 %key_value_mine.1 = (f32[512,2,128]{2,1,0:T(2,128)}, f32[512,2,128]{2,1,0:T(2,128)}) custom-call(s32[1]{0:T(128)} %bitcast.position_ref.refs_0_, f32[1,128,128]{2,1,0:T(8,128)S(1)} %collective-permute-done.15.refs_0_, f32[1,128,128]{2,1,0:T(8,128)S(1)} %add_add_fusion.refs_1_, bf16[2,512,128]{2,1,0:T(8,128)(2,1)S(1)} %get-tuple-element.68.kd_ref.refs_2_, ...), custom_call_target="tpu_custom_call" | custom-call | flops 33554432 | bytes 1703940 | tf_op jit(solution)/shard_map/key_value_mine/pallas_call | solution.py:69
  35.5 0.2 collective-permute-done.14.refs_1_
  35.7 1.0 %key_value_other.1 = (f32[512,2,128]{2,1,0:T(2,128)}, f32[512,2,128]{2,1,0:T(2,128)}) custom-call(s32[1]{0:T(128)} %bitcast.position_ref.refs_0_, f32[1,128,128]{2,1,0:T(8,128)S(1)} %collective-permute-done.9.refs_0_, f32[1,128,128]{2,1,0:T(8,128)S(1)} %collective-permute-done.14.refs_1_, ...), custom_call_target="tpu_custom_call", output_to_operand_aliasing={{0}: (7, {}), {1}: (8, {})} | custom-call | flops 33554432 | bytes 2752516 | tf_op jit(solution)/shard_map/key_value_other/pallas_call | solution.py:69
  (14 shorter events, 0.1 us)
Async XLA Ops:
  0.6 8.6 %copy-start.3 = (bf16[512,2,128]{2,1,0:T(2,128)(2,1)S(1)}, bf16[512,2,128]{2,1,0:T(2,128)(2,1)}, u32[]{:S(2)}) copy-start(bf16[512,2,128]{2,1,0:T(2,128)(2,1)} %param.13) | copy-start | bytes 786436
  2.0 1.5 %collective-permute-start = (f32[2,128,128]{2,1,0:T(8,128)S(1)}, f32[2,128,128]{2,1,0:T(8,128)S(1)}, u32[]{:S(2)}, u32[]{:S(2)}) collective-permute-start(f32[2,128,128]{2,1,0:T(8,128)S(1)} %fusion), channel_id=1, source_target_pairs={{0,1},{1,0},{2,3},{3,2},{4,5},{5,4},{6,7},{7,6},{8,9},{9,8},{10,11... | collective-permute-start | bytes 393224 | tf_op jit(solution)/shard_map/ppermute | solution.py:33
  3.5 5.7 %copy-start.5 = (f32[2,128]{1,0:T(2,128)S(1)}, f32[2,128]{1,0:T(2,128)}, u32[]{:S(2)}) copy-start(f32[2,128]{1,0:T(2,128)} %gain_ref.3) | copy-start | bytes 3076
  3.5 9.4 %collective-permute-start.1 = (f32[1,128,128]{2,1,0:T(8,128)S(1)}, f32[1,128,128]{2,1,0:T(8,128)S(1)}, u32[]{:S(2)}, u32[]{:S(2)}) collective-permute-start(f32[1,128,128]{2,1,0:T(8,128)S(1)} %dynamic-slice_add_fusion), channel_id=1, source_target_pairs={{0,6},{1,7},{2,4},{3,5},{4,2},{5,3},{6,0},{7,1},{8,14},{9,15},{10,... | collective-permute-start | bytes 196616 | tf_op jit(solution)/shard_map/ppermute | solution.py:64
  8.5 5.9 %collective-permute-start.2 = (f32[1,128,128]{2,1,0:T(8,128)S(1)}, f32[1,128,128]{2,1,0:T(8,128)S(1)}, u32[]{:S(2)}, u32[]{:S(2)}) collective-permute-start(f32[1,128,128]{2,1,0:T(8,128)S(1)} %dynamic-slice_add_fusion), channel_id=1, source_target_pairs={{0,4},{1,5},{2,6},{3,7},{4,0},{5,1},{6,2},{7,3},{8,12},{9,13},{10,... | collective-permute-start | bytes 196616 | tf_op jit(solution)/shard_map/ppermute | solution.py:64
  8.5 5.9 %collective-permute-start.3 = (f32[1,128,128]{2,1,0:T(8,128)S(1)}, f32[1,128,128]{2,1,0:T(8,128)S(1)}, u32[]{:S(2)}, u32[]{:S(2)}) collective-permute-start(f32[1,128,128]{2,1,0:T(8,128)S(1)} %dynamic-slice_add_fusion), channel_id=1, source_target_pairs={{0,2},{1,3},{2,0},{3,1},{4,6},{5,7},{6,4},{7,5},{8,10},{9,11},{10,... | collective-permute-start | bytes 196616 | tf_op jit(solution)/shard_map/ppermute | solution.py:64
  9.2 0.7 %copy-start.4 = (f32[8,2,13]{2,1,0:T(2,128)S(1)}, f32[8,2,13]{2,1,0:T(2,128)}, u32[]{:S(2)}) copy-start(f32[8,2,13]{2,1,0:T(2,128)} %table_ref.1) | copy-start | bytes 2500
  9.2 1.4 %copy-start.2 = (bf16[512,2,128]{2,1,0:T(2,128)(2,1)S(1)}, bf16[512,2,128]{2,1,0:T(2,128)(2,1)}, u32[]{:S(2)}) copy-start(bf16[512,2,128]{2,1,0:T(2,128)(2,1)} %param.7) | copy-start | bytes 786436
  9.3 0.7 %copy-start.6 = (s32[512]{0:T(512)S(1)}, s32[512]{0:T(512)}, u32[]{:S(2)}) copy-start(s32[512]{0:T(512)} %param.10) | copy-start | bytes 6148
  10.0 1.0 %copy-start = (bf16[512,2,128]{2,1,0:T(2,128)(2,1)S(1)}, bf16[512,2,128]{2,1,0:T(2,128)(2,1)}, u32[]{:S(2)}) copy-start(bf16[512,2,128]{2,1,0:T(2,128)(2,1)} %param.8) | copy-start | bytes 786436
  10.0 1.0 %copy-start.1 = (bf16[512,2,128]{2,1,0:T(2,128)(2,1)S(1)}, bf16[512,2,128]{2,1,0:T(2,128)(2,1)}, u32[]{:S(2)}) copy-start(bf16[512,2,128]{2,1,0:T(2,128)(2,1)} %param.9) | copy-start | bytes 786436
  14.5 1.3 %collective-permute-start.4 = (f32[1,128,128]{2,1,0:T(8,128)S(1)}, f32[1,128,128]{2,1,0:T(8,128)S(1)}, u32[]{:S(2)}, u32[]{:S(2)}) collective-permute-start(f32[1,128,128]{2,1,0:T(8,128)S(1)} %get-tuple-element.56.refs_6_), channel_id=1, source_target_pairs={{0,1},{1,0},{2,3},{3,2},{4,5},{5,4},{6,7},{7,6},{8,9},{9,8},{10,11... | collective-permute-start | bytes 196616 | tf_op jit(solution)/shard_map/ppermute | solution.py:33
  14.5 1.4 %collective-permute-start.5 = (f32[1,128,128]{2,1,0:T(8,128)S(1)}, f32[1,128,128]{2,1,0:T(8,128)S(1)}, u32[]{:S(2)}, u32[]{:S(2)}) collective-permute-start(f32[1,128,128]{2,1,0:T(8,128)S(1)} %get-tuple-element.57.refs_7_), channel_id=1, source_target_pairs={{0,1},{1,0},{2,3},{3,2},{4,5},{5,4},{6,7},{7,6},{8,9},{9,8},{10,11... | collective-permute-start | bytes 196616 | tf_op jit(solution)/shard_map/ppermute | solution.py:33
  16.4 4.6 %collective-permute-start.6 = (f32[2,512]{1,0:T(2,128)S(1)}, f32[2,512]{1,0:T(2,128)S(1)}, u32[]{:S(2)}, u32[]{:S(2)}) collective-permute-start(f32[2,512]{1,0:T(2,128)S(1)} %get-tuple-element.61.refs_5_), channel_id=1, source_target_pairs={{0,8},{8,16},{16,24},{24,0},{1,9},{9,17},{17,25},{25,1},{2,10},{10... | collective-permute-start | bytes 12296 | tf_op jit(solution)/shard_map/ppermute | solution.py:51
  18.0 3.6 %collective-permute-start.7 = (f32[2,512]{1,0:T(2,128)S(1)}, f32[2,512]{1,0:T(2,128)S(1)}, u32[]{:S(2)}, u32[]{:S(2)}) collective-permute-start(f32[2,512]{1,0:T(2,128)S(1)} %get-tuple-element.61.refs_5_), channel_id=1, source_target_pairs={{0,24},{8,0},{16,8},{24,16},{1,25},{9,1},{17,9},{25,17},{2,26},{10... | collective-permute-start | bytes 12296 | tf_op jit(solution)/shard_map/ppermute | solution.py:51
  19.4 3.6 %collective-permute-start.8 = (f32[2,512]{1,0:T(2,128)S(1)}, f32[2,512]{1,0:T(2,128)S(1)}, u32[]{:S(2)}, u32[]{:S(2)}) collective-permute-start(f32[2,512]{1,0:T(2,128)S(1)} %get-tuple-element.61.refs_5_), channel_id=1, source_target_pairs={{0,16},{8,24},{16,0},{24,8},{1,17},{9,25},{17,1},{25,9},{2,18},{10... | collective-permute-start | bytes 12296 | tf_op jit(solution)/shard_map/ppermute | solution.py:51
  23.8 1.4 %collective-permute-start.10 = (f32[2,1,128,128]{3,2,1,0:T(8,128)S(1)}, f32[2,1,128,128]{3,2,1,0:T(8,128)S(1)}, u32[]{:S(2)}, u32[]{:S(2)}) collective-permute-start(f32[2,1,128,128]{3,2,1,0:T(8,128)S(1)} %get-tuple-element.79), channel_id=1, source_target_pairs={{0,1},{1,0},{2,3},{3,2},{4,5},{5,4},{6,7},{7,6},{8,9},{9,8},{10,11... | collective-permute-start | bytes 393224 | tf_op jit(solution)/shard_map/ppermute | solution.py:33
  25.3 7.7 %collective-permute-start.11 = (f32[1,128,128]{2,1,0:T(8,128)S(1)}, f32[1,128,128]{2,1,0:T(8,128)S(1)}, u32[]{:S(2)}, u32[]{:S(2)}) collective-permute-start(f32[1,128,128]{2,1,0:T(8,128)S(1)} %get-tuple-element.80), channel_id=1, source_target_pairs={{0,6},{1,7},{2,4},{3,5},{4,2},{5,3},{6,0},{7,1},{8,14},{9,15},{10,... | collective-permute-start | bytes 196616 | tf_op jit(solution)/shard_map/ppermute | solution.py:64
  27.8 6.5 %collective-permute-start.12 = (f32[1,128,128]{2,1,0:T(8,128)S(1)}, f32[1,128,128]{2,1,0:T(8,128)S(1)}, u32[]{:S(2)}, u32[]{:S(2)}) collective-permute-start(f32[1,128,128]{2,1,0:T(8,128)S(1)} %get-tuple-element.81), channel_id=1, source_target_pairs={{0,4},{1,5},{2,6},{3,7},{4,0},{5,1},{6,2},{7,3},{8,12},{9,13},{10,... | collective-permute-start | bytes 196616 | tf_op jit(solution)/shard_map/ppermute | solution.py:64
  27.9 6.5 %collective-permute-start.13 = (f32[1,128,128]{2,1,0:T(8,128)S(1)}, f32[1,128,128]{2,1,0:T(8,128)S(1)}, u32[]{:S(2)}, u32[]{:S(2)}) collective-permute-start(f32[1,128,128]{2,1,0:T(8,128)S(1)} %get-tuple-element.82), channel_id=1, source_target_pairs={{0,2},{1,3},{2,0},{3,1},{4,6},{5,7},{6,4},{7,5},{8,10},{9,11},{10,... | collective-permute-start | bytes 196616 | tf_op jit(solution)/shard_map/ppermute | solution.py:64
  29.7 4.7 %collective-permute-start.15 = (f32[1,128,128]{2,1,0:T(8,128)S(1)}, f32[1,128,128]{2,1,0:T(8,128)S(1)}, u32[]{:S(2)}, u32[]{:S(2)}) collective-permute-start(f32[1,128,128]{2,1,0:T(8,128)S(1)} %get-tuple-element.89), channel_id=1, source_target_pairs={{0,1},{1,0},{2,3},{3,2},{4,5},{5,4},{6,7},{7,6},{8,9},{9,8},{10,11... | collective-permute-start | bytes 196616 | tf_op jit(solution)/shard_map/ppermute | solution.py:33
  29.7 5.8 %collective-permute-start.9 = (f32[1,128,128]{2,1,0:T(8,128)S(1)}, f32[1,128,128]{2,1,0:T(8,128)S(1)}, u32[]{:S(2)}, u32[]{:S(2)}) collective-permute-start(f32[1,128,128]{2,1,0:T(8,128)S(1)} %get-tuple-element.77), channel_id=1, source_target_pairs={{0,1},{1,0},{2,3},{3,2},{4,5},{5,4},{6,7},{7,6},{8,9},{9,8},{10,11... | collective-permute-start | bytes 196616 | tf_op jit(solution)/shard_map/ppermute | solution.py:33
  34.4 1.3 %collective-permute-start.14 = (f32[1,128,128]{2,1,0:T(8,128)S(1)}, f32[1,128,128]{2,1,0:T(8,128)S(1)}, u32[]{:S(2)}, u32[]{:S(2)}) collective-permute-start(f32[1,128,128]{2,1,0:T(8,128)S(1)} %add_add_fusion.refs_1_), channel_id=1, source_target_pairs={{0,1},{1,0},{2,3},{3,2},{4,5},{5,4},{6,7},{7,6},{8,9},{9,8},{10,11... | collective-permute-start | bytes 196616 | tf_op jit(solution)/shard_map/ppermute | solution.py:33

commit v7 on v6

--- a/solution.py
+++ b/solution.py
@@ -236,7 +236,7 @@
     return inverse, inverse * inverse * inverse * (total[1:2] / features)
 
 
-def grad_heads(sizes, heads_at, left_at, right_at, attn_ref, gg_ref, qd_ref, tw_ref, put_grad, scaled_ref, put_state):
+def grad_heads(sizes, heads_at, left_at, right_at, attn_ref, gg_ref, qd_ref, tw_ref, put_grad, scaled_ref, put_state, lowest=0):
     _, length, levels, block, bits = sizes
     width = attn_ref.shape[-1]
     for h, head in enumerate(heads_at):
@@ -245,19 +245,19 @@
             grad = (left_at(rows) * gg_ref[head, rows, :] - attn_ref[h, rows, :] * right_at(rows)).astype(BF16)
             put_grad(h, rows, grad)
             wide = grad.astype(F32)
-            for j in range(bits):
+            for j in range(lowest, bits):
                 at = levels - bits + j
-                scaled_ref[rows, j * width:(j + 1) * width] = (tw_ref[head, rows, at:at + 1] * wide).astype(BF16)
-        product = dot(qd_ref[head], scaled_ref[...], TN)
-        for j in range(bits):
-            put_state(j, h, product[:, j * width:(j + 1) * width])
+                scaled_ref[rows, (j - lowest) * width:(j - lowest + 1) * width] = (tw_ref[head, rows, at:at + 1] * wide).astype(BF16)
+        product = dot(qd_ref[head], scaled_ref[:, :(bits - lowest) * width], TN)
+        for j in range(lowest, bits):
+            put_state(j, h, product[:, (j - lowest) * width:(j - lowest + 1) * width])
 
 
 def grad_other(sizes, features, *refs):
     heads, length, levels, block, bits = sizes
     position_ref, attn_ref, gg_ref, qd_ref, tw_ref = refs[:5]
-    sums = refs[5:-7]
-    ag_ref, inverse_ref, left_ref, right_ref, first_ref, send_ref, scaled_ref = refs[-7:]
+    sums = refs[5:-6]
+    ag_ref, inverse_ref, left_ref, right_ref, send_ref, scaled_ref = refs[-6:]
     half = heads // 2
     start = (1 - (position_ref[0] & 1)) * half
     width = attn_ref.shape[-1]
@@ -272,16 +272,13 @@
         ag_ref[h, rows, :] = grad
 
     def put_state(j, h, value):
-        if j == 0:
-            first_ref[h] = value
-        else:
-            send_ref[j - 1, h] = value
+        send_ref[j - 1, h] = value
     grad_heads(sizes, [start + h for h in range(half)], lambda rows: left_ref[rows, :], lambda rows: right_ref[rows, :],
-               attn_ref, gg_ref, qd_ref, tw_ref, put_grad, scaled_ref, put_state)
+               attn_ref, gg_ref, qd_ref, tw_ref, put_grad, scaled_ref, put_state, 1)
 
 
 def grad_mine(sizes, position_ref, attn_ref, far_ref, gg_ref, qd_ref, tw_ref, other_ref, left_ref, right_ref,
-              held_mine_ref, held_other_ref, ag_ref, first_ref, keep_ref, attn_full_ref, held_ref, scaled_ref):
+              held_mine_ref, held_other_ref, ag_ref, first_ref, first_far_ref, keep_ref, attn_full_ref, held_ref, scaled_ref):
     heads, length, levels, block, bits = sizes
     half = heads // 2
     core = position_ref[0] & 1
@@ -300,6 +297,10 @@
                attn_ref, gg_ref, qd_ref, tw_ref, put_grad, scaled_ref, put_state)
     for h in range(half):
         ag_ref[away + h] = other_ref[h]
+        at = levels - bits
+        width = other_ref.shape[-1]
+        scaled_ref[:, :width] = (tw_ref[away + h, :, at:at + 1] * other_ref[h].astype(F32)).astype(BF16)
+        first_far_ref[h] = dot(qd_ref[away + h], scaled_ref[:, :width], TN)
         attn_full_ref[start + h] = attn_ref[h]
         attn_full_ref[away + h] = far_ref[h]
         for j in range(bits):
@@ -468,14 +469,13 @@
     )
     features = heads * width * lax.axis_size("heads")
     parts = summands(sums, "heads")
-    grad_far, inverse, left, right, first_other, send = call(
+    grad_far, inverse, left, right, send = call(
         functools.partial(grad_other, sizes, features),
         (
             shape((half, length, width), BF16),
             shape((1, length), F32),
             shape((length, width), F32),
             shape((length, width), F32),
-            shape((half, width, width), F32),
             shape((bits - 1, half, width, width), F32),
         ),
         (place_arg, attn_other, gg, qd, weights, *parts),
@@ -484,10 +484,11 @@
         flops=cross_flops,
         name="state_grads_other",
     )
-    attn_grad, first_mine, keep, attn, held = call(
+    attn_grad, first_mine, first_other, keep, attn, held = call(
         functools.partial(grad_mine, sizes),
         (
             shape((heads, length, width), BF16),
+            shape((half, width, width), F32),
             shape((half, width, width), F32),
             shape((bits - 1, half, width, width), F32),
             shape((heads, length, width), F32),

time: 36.9 us -> 36.8 us (level)
  transfers between devices with their start and end apart: 16 -> 16, of which waited for: 10 -> 10; matrix products, arithmetic and copies ran while one was open for 0% -> 0% of each run, Pallas kernels for 20% -> 21%
where the time goes in v7:
time: 36.8 us; the launch traced here: 36.6 us
  starting transfers between devices  16.4 us (45%)
  Pallas kernels  9.79 us (27%)
  waiting for transfers between devices  7.16 us (19%)
  matrix products  1.35 us (4%)
  local copies, waits for them, and re-layouts  1.13 us (3%)
  between operations  0.78 us (2%)
    ppermute x6, starting transfers between devices, turned(): result.append(lax.ppermute(block, axis, route))  10.1 us
    pallas_call x12, Pallas kernels, call(): pl.pallas_call(kernel, out_shape=out_shape, in_specs=specs, out_specs=jax...  9.79 us
    ppermute x3, starting transfers between devices, summands(): lax.ppermute(block, axis, [(i, (i + step) % count) for i in range(count)])  4.49 us
    ppermute x6, waiting for transfers between devices, turned(): result.append(lax.ppermute(block, axis, route))  2.85 us
    ppermute x7, waiting for transfers between devices, swapped(): return lax.ppermute(block, axis, route)  2.22 us
    ppermute x3, waiting for transfers between devices, summands(): lax.ppermute(block, axis, [(i, (i + step) % count) for i in range(count)])  2.09 us
    ppermute x7, starting transfers between devices, swapped(): return lax.ppermute(block, axis, route)  1.74 us
    dot_general x1, matrix products, shards(): jnp.einsum('shd,she->hde', key_rows, value_rows, preferred_element_type=F32)  1.35 us
  transfers between devices with their start and end apart: 16, of which 10 were waited for; matrix products, arithmetic and copies ran while one was open for 0% of the time, Pallas kernels for 21%

profile of v7, /device:TPU:0, one launch (start us, length us, event | category | flops | bytes accessed | tf_op | source)
XLA Modules:
  0.0 36.6 jit_solution(12051177744216841931)
XLA Ops:
  0.6 1.3 %fusion = f32[2,128,128]{2,1,0:T(8,128)S(1)} fusion(bf16[512,2,128]{2,1,0:T(2,128)(2,1)} %param.9, bf16[512,2,128]{2,1,0:T(2,128)(2,1)} %param.8), kind=kOutput, calls=%fused_computation | convolution fusion | flops 33554432 | bytes 655360 | tf_op jit(solution)/shard_map/shd,she->hde/dot_general | solution.py:387
  2.0 0.5 %collective-permute-start = (f32[2,128,128]{2,1,0:T(8,128)S(1)}, f32[2,128,128]{2,1,0:T(8,128)S(1)}, u32[]{:S(2)}, u32[]{:S(2)}) collective-permute-start(f32[2,128,128]{2,1,0:T(8,128)S(1)} %fusion), channel_id=1, source_target_pairs={{0,1},{1,0},{2,3},{3,2},{4,5},{5,4},{6,7},{7,6},{8,9},{9,8},{10,11... | collective-permute-start | bytes 393224 | tf_op jit(solution)/shard_map/ppermute | solution.py:33
  2.5 1.0 %collective-permute-done.refs_5_ = f32[2,128,128]{2,1,0:T(8,128)S(1)} collective-permute-done((f32[2,128,128]{2,1,0:T(8,128)S(1)}, f32[2,128,128]{2,1,0:T(8,128)S(1)}, u32[]{:S(2)}, u32[]{:S(2)}) %collective-permute-start) | collective-permute-done | bytes 131104 | tf_op jit(solution)/shard_map/ppermute | solution.py:33
  3.5 0.0 copy-start.5
  3.5 5.0 %collective-permute-start.1 = (f32[1,128,128]{2,1,0:T(8,128)S(1)}, f32[1,128,128]{2,1,0:T(8,128)S(1)}, u32[]{:S(2)}, u32[]{:S(2)}) collective-permute-start(f32[1,128,128]{2,1,0:T(8,128)S(1)} %dynamic-slice_add_fusion), channel_id=1, source_target_pairs={{0,6},{1,7},{2,4},{3,5},{4,2},{5,3},{6,0},{7,1},{8,14},{9,15},{10,... | collective-permute-start | bytes 196616 | tf_op jit(solution)/shard_map/ppermute | solution.py:64
  8.5 0.0 collective-permute-start.2
  8.5 0.6 %collective-permute-start.3 = (f32[1,128,128]{2,1,0:T(8,128)S(1)}, f32[1,128,128]{2,1,0:T(8,128)S(1)}, u32[]{:S(2)}, u32[]{:S(2)}) collective-permute-start(f32[1,128,128]{2,1,0:T(8,128)S(1)} %dynamic-slice_add_fusion), channel_id=1, source_target_pairs={{0,2},{1,3},{2,0},{3,1},{4,6},{5,7},{6,4},{7,5},{8,10},{9,11},{10,... | collective-permute-start | bytes 196616 | tf_op jit(solution)/shard_map/ppermute | solution.py:64
  9.2 0.1 gain_rows.1.refs_3_.refs_2_.gg_ref
  9.3 0.0 copy-start.6
  9.3 0.6 %copy-done.4 = f32[8,2,13]{2,1,0:T(2,128)S(1)} copy-done((f32[8,2,13]{2,1,0:T(2,128)S(1)}, f32[8,2,13]{2,1,0:T(2,128)}, u32[]{:S(2)}) %copy-start.4) | copy-done | bytes 856
  9.9 0.1 copy-done.6
  10.0 0.6 %level_rows.1.tw_ref.refs_4_ = f32[2,512,13]{2,1,0:T(8,128)S(1)} custom-call(s32[1]{0:T(128)} %bitcast.position_ref.refs_0_, s32[1,512]{1,0:T(1,128)S(1)} %bitcast.12, f32[8,2,13]{2,1,0:T(2,128)S(1)} %copy-done.4), custom_call_target="tpu_custom_call" | custom-call | bytes 2884 | tf_op jit(solution)/shard_map/level_rows/pallas_call | solution.py:69
  10.6 0.3 copy-done
  11.0 0.1 copy-done.1
  11.0 1.9 %local_forward.1 = (f32[2,512,128]{2,1,0:T(8,128)S(1)}, bf16[2,512,512]{2,1,0:T(8,128)(2,1)S(1)}, f32[8,128,128]{2,1,0:T(8,128)S(1)}, bf16[2,512,128]{2,1,0:T(8,...) custom-call(bf16[1024,128]{1,0:T(8,128)(2,1)S(1)} %bitcast.10, ...), custom_call_target="tpu_custom_call" | custom-call | flops 268435456 | bytes 839680 | tf_op jit(solution)/shard_map/local_forward/pallas_call | solution.py:69
  12.9 0.0 collective-permute-done.1.refs_0_
  13.0 1.5 %collective-permute-done.2.refs_1_ = f32[1,128,128]{2,1,0:T(8,128)S(1)} collective-permute-done((f32[1,128,128]{2,1,0:T(8,128)S(1)}, f32[1,128,128]{2,1,0:T(8,128)S(1)}, u32[]{:S(2)}, u32[]{:S(2)}) %collective-permute-start.2) | collective-permute-done | bytes 65568 | tf_op jit(solution)/shard_map/ppermute | solution.py:64
  14.4 0.0 collective-permute-done.3.refs_2_
  14.5 0.1 collective-permute-start.4
  14.5 0.5 %collective-permute-start.5 = (f32[1,128,128]{2,1,0:T(8,128)S(1)}, f32[1,128,128]{2,1,0:T(8,128)S(1)}, u32[]{:S(2)}, u32[]{:S(2)}) collective-permute-start(f32[1,128,128]{2,1,0:T(8,128)S(1)} %get-tuple-element.57.refs_7_), channel_id=1, source_target_pairs={{0,1},{1,0},{2,3},{3,2},{4,5},{5,4},{6,7},{7,6},{8,9},{9,8},{10,11... | collective-permute-start | bytes 196616 | tf_op jit(solution)/shard_map/ppermute | solution.py:33
  15.0 0.5 %cross_mine.1 = (f32[1,512,128]{2,1,0:T(8,128)S(1)}, f32[2,512]{1,0:T(2,128)S(1)}, bf16[3,1,128,128]{3,2,1,0:T(8,128)(2,1)S(1)}) custom-call(s32[1]{0:T(128)} %bitcast.position_ref.refs_0_, f32[2,512,128]{2,1,0:T(8,128)S(1)} %get-tuple-element.50.refs_1_, bf16[2,512,128]{2,1,0:T(8,128)(2,1)S(1)} %get-tuple-element.51.refs_2_.refs_3_.qd_ref, ...), custom_call_target="tpu_custom_call" | custom-call | flops 50331648 | bytes 1626116 | tf_op jit(solution)/shard_map/cross_mine/pallas_call | solution.py:69
  15.5 0.3 collective-permute-done.4.refs_7_
  15.8 0.2 collective-permute-done.5.refs_8_
  15.9 0.5 %cross_other.1 = (f32[1,512,128]{2,1,0:T(8,128)S(1)}, f32[2,512]{1,0:T(2,128)S(1)}, bf16[3,1,128,128]{3,2,1,0:T(8,128)(2,1)S(1)}) custom-call(s32[1]{0:T(128)} %bitcast.position_ref.refs_0_, f32[2,512,128]{2,1,0:T(8,128)S(1)} %get-tuple-element.50.refs_1_, bf16[2,512,128]{2,1,0:T(8,128)(2,1)S(1)} %get-tuple-element.51.refs_2_.refs_3_.qd_ref, ...), custom_call_target="tpu_custom_call" | custom-call | flops 50331648 | bytes 1630212 | tf_op jit(solution)/shard_map/cross_other/pallas_call | solution.py:69
  16.4 1.5 %collective-permute-start.6 = (f32[2,512]{1,0:T(2,128)S(1)}, f32[2,512]{1,0:T(2,128)S(1)}, u32[]{:S(2)}, u32[]{:S(2)}) collective-permute-start(f32[2,512]{1,0:T(2,128)S(1)} %get-tuple-element.61.refs_5_), channel_id=1, source_target_pairs={{0,8},{8,16},{16,24},{24,0},{1,9},{9,17},{17,25},{25,1},{2,10},{10... | collective-permute-start | bytes 12296 | tf_op jit(solution)/shard_map/ppermute | solution.py:51
  18.0 1.4 %collective-permute-start.7 = (f32[2,512]{1,0:T(2,128)S(1)}, f32[2,512]{1,0:T(2,128)S(1)}, u32[]{:S(2)}, u32[]{:S(2)}) collective-permute-start(f32[2,512]{1,0:T(2,128)S(1)} %get-tuple-element.61.refs_5_), channel_id=1, source_target_pairs={{0,24},{8,0},{16,8},{24,16},{1,25},{9,1},{17,9},{25,17},{2,26},{10... | collective-permute-start | bytes 12296 | tf_op jit(solution)/shard_map/ppermute | solution.py:51
  19.4 1.5 %collective-permute-start.8 = (f32[2,512]{1,0:T(2,128)S(1)}, f32[2,512]{1,0:T(2,128)S(1)}, u32[]{:S(2)}, u32[]{:S(2)}) collective-permute-start(f32[2,512]{1,0:T(2,128)S(1)} %get-tuple-element.61.refs_5_), channel_id=1, source_target_pairs={{0,16},{8,24},{16,0},{24,8},{1,17},{9,25},{17,1},{25,9},{2,18},{10... | collective-permute-start | bytes 12296 | tf_op jit(solution)/shard_map/ppermute | solution.py:51
  20.9 0.1 collective-permute-done.6.refs_6_
  21.0 0.6 %collective-permute-done.7.refs_7_ = f32[2,512]{1,0:T(2,128)S(1)} collective-permute-done((f32[2,512]{1,0:T(2,128)S(1)}, f32[2,512]{1,0:T(2,128)S(1)}, u32[]{:S(2)}, u32[]{:S(2)}) %collective-permute-start.7) | collective-permute-done | bytes 4128 | tf_op jit(solution)/shard_map/ppermute | solution.py:51
  21.6 1.4 %collective-permute-done.8.refs_8_ = f32[2,512]{1,0:T(2,128)S(1)} collective-permute-done((f32[2,512]{1,0:T(2,128)S(1)}, f32[2,512]{1,0:T(2,128)S(1)}, u32[]{:S(2)}, u32[]{:S(2)}) %collective-permute-start.8) | collective-permute-done | bytes 4128 | tf_op jit(solution)/shard_map/ppermute | solution.py:51
  23.0 0.6 %state_grads_other.1 = (bf16[1,512,128]{2,1,0:T(8,128)(2,1)S(1)}, f32[1,512]{1,0:T(1,128)S(1)}, f32[512,128]{1,0:T(8,128)S(1)}, f32[512,128]{1,0:T(8,128)S(1)}, f32[2,1,128,128]{3,2,1,0:T(8,128)S(1)}) custom-call(s32[1]{0:T(128)} %bitcast.position_ref.refs_0_, f32[1,512,128]{2,1,0:T(8,128)S(1)} %get-tuple-element.60.refs_1_.far_ref, ...), custom_call_target="tpu_custom_call" | custom-call | flops 50331648 | bytes 1118212 | tf_op jit(solution)/shard_map/state_grads_other/pallas_call | solution.py:69
  23.7 0.1 collective-permute-start.10
  23.7 0.7 %state_grads_mine.1 = (bf16[2,512,128]{2,1,0:T(8,128)(2,1)S(1)}, f32[1,128,128]{2,1,0:T(8,128)S(1)}, f32[1,128,128]{2,1,0:T(8,128)S(1)}, f32[2,1,128,128]{3,2,1,...) custom-call(s32[1]{0:T(128)} %bitcast.position_ref.refs_0_, ...), custom_call_target="tpu_custom_call" | custom-call | flops 50331648 | bytes 2215940 | tf_op jit(solution)/shard_map/state_grads_mine/pallas_call | solution.py:69
  24.4 0.7 %collective-permute-done.10.came_ref = f32[2,1,128,128]{3,2,1,0:T(8,128)S(1)} collective-permute-done((f32[2,1,128,128]{3,2,1,0:T(8,128)S(1)}, f32[2,1,128,128]{3,2,1,0:T(8,128)S(1)}, u32[]{:S(2)}, u32[]{:S(2)}) %collective-permute-start.10) | collective-permute-done | bytes 131104 | tf_op jit(solution)/shard_map/ppermute | solution.py:33
  25.1 2.5 %collective-permute-start.11 = (f32[1,128,128]{2,1,0:T(8,128)S(1)}, f32[1,128,128]{2,1,0:T(8,128)S(1)}, u32[]{:S(2)}, u32[]{:S(2)}) collective-permute-start(f32[1,128,128]{2,1,0:T(8,128)S(1)} %get-tuple-element.80), channel_id=1, source_target_pairs={{0,6},{1,7},{2,4},{3,5},{4,2},{5,3},{6,0},{7,1},{8,14},{9,15},{10,... | collective-permute-start | bytes 196616 | tf_op jit(solution)/shard_map/ppermute | solution.py:64
  27.7 0.1 collective-permute-start.12
  27.8 1.8 %collective-permute-start.13 = (f32[1,128,128]{2,1,0:T(8,128)S(1)}, f32[1,128,128]{2,1,0:T(8,128)S(1)}, u32[]{:S(2)}, u32[]{:S(2)}) collective-permute-start(f32[1,128,128]{2,1,0:T(8,128)S(1)} %get-tuple-element.82), channel_id=1, source_target_pairs={{0,2},{1,3},{2,0},{3,1},{4,6},{5,7},{6,4},{7,5},{8,10},{9,11},{10,... | collective-permute-start | bytes 196616 | tf_op jit(solution)/shard_map/ppermute | solution.py:64
  29.6 0.0 collective-permute-start.15
  29.6 0.5 %collective-permute-start.9 = (f32[1,128,128]{2,1,0:T(8,128)S(1)}, f32[1,128,128]{2,1,0:T(8,128)S(1)}, u32[]{:S(2)}, u32[]{:S(2)}) collective-permute-start(f32[1,128,128]{2,1,0:T(8,128)S(1)} %get-tuple-element.77), channel_id=1, source_target_pairs={{0,1},{1,0},{2,3},{3,2},{4,5},{5,4},{6,7},{7,6},{8,9},{9,8},{10,11... | collective-permute-start | bytes 196616 | tf_op jit(solution)/shard_map/ppermute | solution.py:33
  30.1 2.8 %local_backward.1 = (f32[1024,128]{1,0:T(8,128)}, f32[1024,128]{1,0:T(8,128)}, f32[2,512,128]{2,1,0:T(8,128)S(1)}, f32[2,512,128]{2,1,0:T(8,128)S(1)}) custom-call(bf16[2,512,128]{2,1,0:T(8,128)(2,1)S(1)} %get-tuple-element.67.ag_ref, bf16[2,512,128]{2,1,0:T(8,128)(2,1)S(1)} %get-tuple-element.51.refs_2_.refs_3_.qd_ref, ...), custom_call_target="tpu_custom_call" | custom-call | flops 536870912 | bytes 3398656 | tf_op jit(solution)/shard_map/local_backward/pallas_call | solution.py:69
  32.9 0.0 collective-permute-done.11
  32.9 1.4 %collective-permute-done.12 = f32[1,128,128]{2,1,0:T(8,128)S(1)} collective-permute-done((f32[1,128,128]{2,1,0:T(8,128)S(1)}, f32[1,128,128]{2,1,0:T(8,128)S(1)}, u32[]{:S(2)}, u32[]{:S(2)}) %collective-permute-start.12) | collective-permute-done | bytes 65568 | tf_op jit(solution)/shard_map/ppermute | solution.py:64
  34.2 0.0 collective-permute-done.13
  34.2 0.1 collective-permute-start.14
  34.3 1.0 %key_value_mine.1 = (f32[512,2,128]{2,1,0:T(2,128)}, f32[512,2,128]{2,1,0:T(2,128)}) custom-call(s32[1]{0:T(128)} %bitcast.position_ref.refs_0_, f32[1,128,128]{2,1,0:T(8,128)S(1)} %collective-permute-done.15.refs_0_, f32[1,128,128]{2,1,0:T(8,128)S(1)} %add_add_fusion.refs_1_, bf16[2,512,128]{2,1,0:T(8,128)(2,1)S(1)} %get-tuple-element.68.kd_ref.refs_2_, ...), custom_call_target="tpu_custom_call" | custom-call | flops 33554432 | bytes 1703940 | tf_op jit(solution)/shard_map/key_value_mine/pallas_call | solution.py:69
  35.4 0.0 collective-permute-done.9.refs_0_
  35.4 0.2 collective-permute-done.14.refs_1_
  35.6 1.0 %key_value_other.1 = (f32[512,2,128]{2,1,0:T(2,128)}, f32[512,2,128]{2,1,0:T(2,128)}) custom-call(s32[1]{0:T(128)} %bitcast.position_ref.refs_0_, f32[1,128,128]{2,1,0:T(8,128)S(1)} %collective-permute-done.9.refs_0_, f32[1,128,128]{2,1,0:T(8,128)S(1)} %collective-permute-done.14.refs_1_, ...), custom_call_target="tpu_custom_call", output_to_operand_aliasing={{0}: (7, {}), {1}: (8, {})} | custom-call | flops 33554432 | bytes 2752516 | tf_op jit(solution)/shard_map/key_value_other/pallas_call | solution.py:69
  (14 shorter events, 0.1 us)
Async XLA Ops:
  0.6 8.6 %copy-start.3 = (bf16[512,2,128]{2,1,0:T(2,128)(2,1)S(1)}, bf16[512,2,128]{2,1,0:T(2,128)(2,1)}, u32[]{:S(2)}) copy-start(bf16[512,2,128]{2,1,0:T(2,128)(2,1)} %param.13) | copy-start | bytes 786436
  2.0 1.5 %collective-permute-start = (f32[2,128,128]{2,1,0:T(8,128)S(1)}, f32[2,128,128]{2,1,0:T(8,128)S(1)}, u32[]{:S(2)}, u32[]{:S(2)}) collective-permute-start(f32[2,128,128]{2,1,0:T(8,128)S(1)} %fusion), channel_id=1, source_target_pairs={{0,1},{1,0},{2,3},{3,2},{4,5},{5,4},{6,7},{7,6},{8,9},{9,8},{10,11... | collective-permute-start | bytes 393224 | tf_op jit(solution)/shard_map/ppermute | solution.py:33
  3.5 5.7 %copy-start.5 = (f32[2,128]{1,0:T(2,128)S(1)}, f32[2,128]{1,0:T(2,128)}, u32[]{:S(2)}) copy-start(f32[2,128]{1,0:T(2,128)} %gain_ref.3) | copy-start | bytes 3076
  3.5 9.4 %collective-permute-start.1 = (f32[1,128,128]{2,1,0:T(8,128)S(1)}, f32[1,128,128]{2,1,0:T(8,128)S(1)}, u32[]{:S(2)}, u32[]{:S(2)}) collective-permute-start(f32[1,128,128]{2,1,0:T(8,128)S(1)} %dynamic-slice_add_fusion), channel_id=1, source_target_pairs={{0,6},{1,7},{2,4},{3,5},{4,2},{5,3},{6,0},{7,1},{8,14},{9,15},{10,... | collective-permute-start | bytes 196616 | tf_op jit(solution)/shard_map/ppermute | solution.py:64
  8.5 5.9 %collective-permute-start.2 = (f32[1,128,128]{2,1,0:T(8,128)S(1)}, f32[1,128,128]{2,1,0:T(8,128)S(1)}, u32[]{:S(2)}, u32[]{:S(2)}) collective-permute-start(f32[1,128,128]{2,1,0:T(8,128)S(1)} %dynamic-slice_add_fusion), channel_id=1, source_target_pairs={{0,4},{1,5},{2,6},{3,7},{4,0},{5,1},{6,2},{7,3},{8,12},{9,13},{10,... | collective-permute-start | bytes 196616 | tf_op jit(solution)/shard_map/ppermute | solution.py:64
  8.5 5.9 %collective-permute-start.3 = (f32[1,128,128]{2,1,0:T(8,128)S(1)}, f32[1,128,128]{2,1,0:T(8,128)S(1)}, u32[]{:S(2)}, u32[]{:S(2)}) collective-permute-start(f32[1,128,128]{2,1,0:T(8,128)S(1)} %dynamic-slice_add_fusion), channel_id=1, source_target_pairs={{0,2},{1,3},{2,0},{3,1},{4,6},{5,7},{6,4},{7,5},{8,10},{9,11},{10,... | collective-permute-start | bytes 196616 | tf_op jit(solution)/shard_map/ppermute | solution.py:64
  9.2 0.7 %copy-start.4 = (f32[8,2,13]{2,1,0:T(2,128)S(1)}, f32[8,2,13]{2,1,0:T(2,128)}, u32[]{:S(2)}) copy-start(f32[8,2,13]{2,1,0:T(2,128)} %table_ref.1) | copy-start | bytes 2500
  9.2 1.4 %copy-start.2 = (bf16[512,2,128]{2,1,0:T(2,128)(2,1)S(1)}, bf16[512,2,128]{2,1,0:T(2,128)(2,1)}, u32[]{:S(2)}) copy-start(bf16[512,2,128]{2,1,0:T(2,128)(2,1)} %param.7) | copy-start | bytes 786436
  9.3 0.7 %copy-start.6 = (s32[512]{0:T(512)S(1)}, s32[512]{0:T(512)}, u32[]{:S(2)}) copy-start(s32[512]{0:T(512)} %param.10) | copy-start | bytes 6148
  10.0 1.0 %copy-start = (bf16[512,2,128]{2,1,0:T(2,128)(2,1)S(1)}, bf16[512,2,128]{2,1,0:T(2,128)(2,1)}, u32[]{:S(2)}) copy-start(bf16[512,2,128]{2,1,0:T(2,128)(2,1)} %param.8) | copy-start | bytes 786436
  10.0 1.0 %copy-start.1 = (bf16[512,2,128]{2,1,0:T(2,128)(2,1)S(1)}, bf16[512,2,128]{2,1,0:T(2,128)(2,1)}, u32[]{:S(2)}) copy-start(bf16[512,2,128]{2,1,0:T(2,128)(2,1)} %param.9) | copy-start | bytes 786436
  14.5 1.3 %collective-permute-start.4 = (f32[1,128,128]{2,1,0:T(8,128)S(1)}, f32[1,128,128]{2,1,0:T(8,128)S(1)}, u32[]{:S(2)}, u32[]{:S(2)}) collective-permute-start(f32[1,128,128]{2,1,0:T(8,128)S(1)} %get-tuple-element.56.refs_6_), channel_id=1, source_target_pairs={{0,1},{1,0},{2,3},{3,2},{4,5},{5,4},{6,7},{7,6},{8,9},{9,8},{10,11... | collective-permute-start | bytes 196616 | tf_op jit(solution)/shard_map/ppermute | solution.py:33
  14.5 1.4 %collective-permute-start.5 = (f32[1,128,128]{2,1,0:T(8,128)S(1)}, f32[1,128,128]{2,1,0:T(8,128)S(1)}, u32[]{:S(2)}, u32[]{:S(2)}) collective-permute-start(f32[1,128,128]{2,1,0:T(8,128)S(1)} %get-tuple-element.57.refs_7_), channel_id=1, source_target_pairs={{0,1},{1,0},{2,3},{3,2},{4,5},{5,4},{6,7},{7,6},{8,9},{9,8},{10,11... | collective-permute-start | bytes 196616 | tf_op jit(solution)/shard_map/ppermute | solution.py:33
  16.4 4.6 %collective-permute-start.6 = (f32[2,512]{1,0:T(2,128)S(1)}, f32[2,512]{1,0:T(2,128)S(1)}, u32[]{:S(2)}, u32[]{:S(2)}) collective-permute-start(f32[2,512]{1,0:T(2,128)S(1)} %get-tuple-element.61.refs_5_), channel_id=1, source_target_pairs={{0,8},{8,16},{16,24},{24,0},{1,9},{9,17},{17,25},{25,1},{2,10},{10... | collective-permute-start | bytes 12296 | tf_op jit(solution)/shard_map/ppermute | solution.py:51
  18.0 3.6 %collective-permute-start.7 = (f32[2,512]{1,0:T(2,128)S(1)}, f32[2,512]{1,0:T(2,128)S(1)}, u32[]{:S(2)}, u32[]{:S(2)}) collective-permute-start(f32[2,512]{1,0:T(2,128)S(1)} %get-tuple-element.61.refs_5_), channel_id=1, source_target_pairs={{0,24},{8,0},{16,8},{24,16},{1,25},{9,1},{17,9},{25,17},{2,26},{10... | collective-permute-start | bytes 12296 | tf_op jit(solution)/shard_map/ppermute | solution.py:51
  19.4 3.6 %collective-permute-start.8 = (f32[2,512]{1,0:T(2,128)S(1)}, f32[2,512]{1,0:T(2,128)S(1)}, u32[]{:S(2)}, u32[]{:S(2)}) collective-permute-start(f32[2,512]{1,0:T(2,128)S(1)} %get-tuple-element.61.refs_5_), channel_id=1, source_target_pairs={{0,16},{8,24},{16,0},{24,8},{1,17},{9,25},{17,1},{25,9},{2,18},{10... | collective-permute-start | bytes 12296 | tf_op jit(solution)/shard_map/ppermute | solution.py:51
  23.7 1.4 %collective-permute-start.10 = (f32[2,1,128,128]{3,2,1,0:T(8,128)S(1)}, f32[2,1,128,128]{3,2,1,0:T(8,128)S(1)}, u32[]{:S(2)}, u32[]{:S(2)}) collective-permute-start(f32[2,1,128,128]{3,2,1,0:T(8,128)S(1)} %get-tuple-element.79), channel_id=1, source_target_pairs={{0,1},{1,0},{2,3},{3,2},{4,5},{5,4},{6,7},{7,6},{8,9},{9,8},{10,11... | collective-permute-start | bytes 393224 | tf_op jit(solution)/shard_map/ppermute | solution.py:33
  25.1 7.7 %collective-permute-start.11 = (f32[1,128,128]{2,1,0:T(8,128)S(1)}, f32[1,128,128]{2,1,0:T(8,128)S(1)}, u32[]{:S(2)}, u32[]{:S(2)}) collective-permute-start(f32[1,128,128]{2,1,0:T(8,128)S(1)} %get-tuple-element.80), channel_id=1, source_target_pairs={{0,6},{1,7},{2,4},{3,5},{4,2},{5,3},{6,0},{7,1},{8,14},{9,15},{10,... | collective-permute-start | bytes 196616 | tf_op jit(solution)/shard_map/ppermute | solution.py:64
  27.7 6.5 %collective-permute-start.12 = (f32[1,128,128]{2,1,0:T(8,128)S(1)}, f32[1,128,128]{2,1,0:T(8,128)S(1)}, u32[]{:S(2)}, u32[]{:S(2)}) collective-permute-start(f32[1,128,128]{2,1,0:T(8,128)S(1)} %get-tuple-element.81), channel_id=1, source_target_pairs={{0,4},{1,5},{2,6},{3,7},{4,0},{5,1},{6,2},{7,3},{8,12},{9,13},{10,... | collective-permute-start | bytes 196616 | tf_op jit(solution)/shard_map/ppermute | solution.py:64
  27.8 6.5 %collective-permute-start.13 = (f32[1,128,128]{2,1,0:T(8,128)S(1)}, f32[1,128,128]{2,1,0:T(8,128)S(1)}, u32[]{:S(2)}, u32[]{:S(2)}) collective-permute-start(f32[1,128,128]{2,1,0:T(8,128)S(1)} %get-tuple-element.82), channel_id=1, source_target_pairs={{0,2},{1,3},{2,0},{3,1},{4,6},{5,7},{6,4},{7,5},{8,10},{9,11},{10,... | collective-permute-start | bytes 196616 | tf_op jit(solution)/shard_map/ppermute | solution.py:64
  29.6 4.7 %collective-permute-start.15 = (f32[1,128,128]{2,1,0:T(8,128)S(1)}, f32[1,128,128]{2,1,0:T(8,128)S(1)}, u32[]{:S(2)}, u32[]{:S(2)}) collective-permute-start(f32[1,128,128]{2,1,0:T(8,128)S(1)} %get-tuple-element.89), channel_id=1, source_target_pairs={{0,1},{1,0},{2,3},{3,2},{4,5},{5,4},{6,7},{7,6},{8,9},{9,8},{10,11... | collective-permute-start | bytes 196616 | tf_op jit(solution)/shard_map/ppermute | solution.py:33
  29.6 5.8 %collective-permute-start.9 = (f32[1,128,128]{2,1,0:T(8,128)S(1)}, f32[1,128,128]{2,1,0:T(8,128)S(1)}, u32[]{:S(2)}, u32[]{:S(2)}) collective-permute-start(f32[1,128,128]{2,1,0:T(8,128)S(1)} %get-tuple-element.77), channel_id=1, source_target_pairs={{0,1},{1,0},{2,3},{3,2},{4,5},{5,4},{6,7},{7,6},{8,9},{9,8},{10,11... | collective-permute-start | bytes 196616 | tf_op jit(solution)/shard_map/ppermute | solution.py:33
  34.2 1.3 %collective-permute-start.14 = (f32[1,128,128]{2,1,0:T(8,128)S(1)}, f32[1,128,128]{2,1,0:T(8,128)S(1)}, u32[]{:S(2)}, u32[]{:S(2)}) collective-permute-start(f32[1,128,128]{2,1,0:T(8,128)S(1)} %add_add_fusion.refs_1_), channel_id=1, source_target_pairs={{0,1},{1,0},{2,3},{3,2},{4,5},{5,4},{6,7},{7,6},{8,9},{9,8},{10,11... | collective-permute-start | bytes 196616 | tf_op jit(solution)/shard_map/ppermute | solution.py:33

commit v8 on v7

--- a/solution.py
+++ b/solution.py
@@ -44,6 +44,10 @@
     return list(range(group - 1, 0, -1))
 
 
+def back_swaps(group):
+    return [group - 1, *range(1, group - 1)]
+
+
 def summands(block, axis):
     count = lax.axis_size(axis)
     result = [block]
@@ -52,10 +56,10 @@
     return result
 
 
-def turned(blocks, axis, group):
+def turned(blocks, axis, group, order):
     count = lax.axis_size(axis)
     result = []
-    for step, block in zip(swaps(group), blocks):
+    for step, block in zip(order, blocks):
         route = []
         for i in range(count):
             chip = i >> 1
@@ -216,7 +220,7 @@
 def message_kernel(group, position_ref, above_ref, keep_ref, came_ref, *targets):
     far = group.bit_length() - 1
     chip = (position_ref[0] >> 1) & (group - 1)
-    for step, message in zip(swaps(group), targets):
+    for step, message in zip(back_swaps(group), targets):
         target = chip ^ step
         total = above_ref[...]
         for place in range(far):
@@ -404,7 +408,7 @@
     )
     far = min(bits - 1, 2)
     group = 1 << far
-    received = turned([block_sum] * (group - 1), "seq", group)
+    received = turned([block_sum] * (group - 1), "seq", group, swaps(group))
 
     inner, probs, diag, qd, kd, vd = call(
         functools.partial(local_forward, sizes),
@@ -511,7 +515,7 @@
         [SMEM] + [VMEM] * 3,
         name="far_messages",
     )
-    landed = turned(messages, "seq", group)
+    landed = turned(messages, "seq", group, back_swaps(group))
     near_other = swapped(first_mine, "seq", 0)
     near_mine = swapped(first_other, "seq", 0)
 

time: 36.8 us -> 36.7 us (level)
  no operation moved by 1% of the time
where the time goes in v8:
time: 36.7 us; the launch traced here: 36.4 us
  starting transfers between devices  16.4 us (45%)
  Pallas kernels  9.79 us (27%)
  waiting for transfers between devices  7 us (19%)
  matrix products  1.35 us (4%)
  local copies, waits for them, and re-layouts  1.13 us (3%)
  between operations  0.79 us (2%)
    ppermute x6, starting transfers between devices, turned(): result.append(lax.ppermute(block, axis, route))  10.1 us
    pallas_call x12, Pallas kernels, call(): pl.pallas_call(kernel, out_shape=out_shape, in_specs=specs, out_specs=jax...  9.79 us
    ppermute x3, starting transfers between devices, summands(): lax.ppermute(block, axis, [(i, (i + step) % count) for i in range(count)])  4.49 us
    ppermute x6, waiting for transfers between devices, turned(): result.append(lax.ppermute(block, axis, route))  2.69 us
    ppermute x7, waiting for transfers between devices, swapped(): return lax.ppermute(block, axis, route)  2.23 us
    ppermute x3, waiting for transfers between devices, summands(): lax.ppermute(block, axis, [(i, (i + step) % count) for i in range(count)])  2.09 us
    ppermute x7, starting transfers between devices, swapped(): return lax.ppermute(block, axis, route)  1.74 us
    dot_general x1, matrix products, shards(): jnp.einsum('shd,she->hde', key_rows, value_rows, preferred_element_type=F32)  1.35 us
  transfers between devices with their start and end apart: 16, of which 10 were waited for; matrix products, arithmetic and copies ran while one was open for 0% of the time, Pallas kernels for 21%

profile of v8, /device:TPU:0, one launch (start us, length us, event | category | flops | bytes accessed | tf_op | source)
XLA Modules:
  0.0 36.4 jit_solution(11876111161094060320)
XLA Ops:
  0.6 1.3 %fusion = f32[2,128,128]{2,1,0:T(8,128)S(1)} fusion(bf16[512,2,128]{2,1,0:T(2,128)(2,1)} %param.9, bf16[512,2,128]{2,1,0:T(2,128)(2,1)} %param.8), kind=kOutput, calls=%fused_computation | convolution fusion | flops 33554432 | bytes 655360 | tf_op jit(solution)/shard_map/shd,she->hde/dot_general | solution.py:391
  2.0 0.5 %collective-permute-start = (f32[2,128,128]{2,1,0:T(8,128)S(1)}, f32[2,128,128]{2,1,0:T(8,128)S(1)}, u32[]{:S(2)}, u32[]{:S(2)}) collective-permute-start(f32[2,128,128]{2,1,0:T(8,128)S(1)} %fusion), channel_id=1, source_target_pairs={{0,1},{1,0},{2,3},{3,2},{4,5},{5,4},{6,7},{7,6},{8,9},{9,8},{10,11... | collective-permute-start | bytes 393224 | tf_op jit(solution)/shard_map/ppermute | solution.py:33
  2.5 1.0 %collective-permute-done.refs_5_ = f32[2,128,128]{2,1,0:T(8,128)S(1)} collective-permute-done((f32[2,128,128]{2,1,0:T(8,128)S(1)}, f32[2,128,128]{2,1,0:T(8,128)S(1)}, u32[]{:S(2)}, u32[]{:S(2)}) %collective-permute-start) | collective-permute-done | bytes 131104 | tf_op jit(solution)/shard_map/ppermute | solution.py:33
  3.5 0.0 copy-start.5
  3.5 5.0 %collective-permute-start.1 = (f32[1,128,128]{2,1,0:T(8,128)S(1)}, f32[1,128,128]{2,1,0:T(8,128)S(1)}, u32[]{:S(2)}, u32[]{:S(2)}) collective-permute-start(f32[1,128,128]{2,1,0:T(8,128)S(1)} %dynamic-slice_add_fusion), channel_id=1, source_target_pairs={{0,6},{1,7},{2,4},{3,5},{4,2},{5,3},{6,0},{7,1},{8,14},{9,15},{10,... | collective-permute-start | bytes 196616 | tf_op jit(solution)/shard_map/ppermute | solution.py:68
  8.5 0.0 collective-permute-start.2
  8.5 0.6 %collective-permute-start.3 = (f32[1,128,128]{2,1,0:T(8,128)S(1)}, f32[1,128,128]{2,1,0:T(8,128)S(1)}, u32[]{:S(2)}, u32[]{:S(2)}) collective-permute-start(f32[1,128,128]{2,1,0:T(8,128)S(1)} %dynamic-slice_add_fusion), channel_id=1, source_target_pairs={{0,2},{1,3},{2,0},{3,1},{4,6},{5,7},{6,4},{7,5},{8,10},{9,11},{10,... | collective-permute-start | bytes 196616 | tf_op jit(solution)/shard_map/ppermute | solution.py:68
  9.2 0.1 gain_rows.1.refs_3_.refs_2_.gg_ref
  9.3 0.0 copy-start.6
  9.3 0.6 %copy-done.4 = f32[8,2,13]{2,1,0:T(2,128)S(1)} copy-done((f32[8,2,13]{2,1,0:T(2,128)S(1)}, f32[8,2,13]{2,1,0:T(2,128)}, u32[]{:S(2)}) %copy-start.4) | copy-done | bytes 856
  9.9 0.1 copy-done.6
  10.0 0.6 %level_rows.1.tw_ref.refs_4_ = f32[2,512,13]{2,1,0:T(8,128)S(1)} custom-call(s32[1]{0:T(128)} %bitcast.position_ref.refs_0_, s32[1,512]{1,0:T(1,128)S(1)} %bitcast.12, f32[8,2,13]{2,1,0:T(2,128)S(1)} %copy-done.4), custom_call_target="tpu_custom_call" | custom-call | bytes 2884 | tf_op jit(solution)/shard_map/level_rows/pallas_call | solution.py:73
  10.6 0.3 copy-done
  11.0 0.1 copy-done.1
  11.0 1.9 %local_forward.1 = (f32[2,512,128]{2,1,0:T(8,128)S(1)}, bf16[2,512,512]{2,1,0:T(8,128)(2,1)S(1)}, f32[8,128,128]{2,1,0:T(8,128)S(1)}, bf16[2,512,128]{2,1,0:T(8,...) custom-call(bf16[1024,128]{1,0:T(8,128)(2,1)S(1)} %bitcast.10, ...), custom_call_target="tpu_custom_call" | custom-call | flops 268435456 | bytes 839680 | tf_op jit(solution)/shard_map/local_forward/pallas_call | solution.py:73
  12.9 0.0 collective-permute-done.1.refs_0_
  13.0 1.5 %collective-permute-done.2.refs_1_ = f32[1,128,128]{2,1,0:T(8,128)S(1)} collective-permute-done((f32[1,128,128]{2,1,0:T(8,128)S(1)}, f32[1,128,128]{2,1,0:T(8,128)S(1)}, u32[]{:S(2)}, u32[]{:S(2)}) %collective-permute-start.2) | collective-permute-done | bytes 65568 | tf_op jit(solution)/shard_map/ppermute | solution.py:68
  14.4 0.0 collective-permute-done.3.refs_2_
  14.5 0.1 collective-permute-start.4
  14.5 0.5 %collective-permute-start.5 = (f32[1,128,128]{2,1,0:T(8,128)S(1)}, f32[1,128,128]{2,1,0:T(8,128)S(1)}, u32[]{:S(2)}, u32[]{:S(2)}) collective-permute-start(f32[1,128,128]{2,1,0:T(8,128)S(1)} %get-tuple-element.57.refs_7_), channel_id=1, source_target_pairs={{0,1},{1,0},{2,3},{3,2},{4,5},{5,4},{6,7},{7,6},{8,9},{9,8},{10,11... | collective-permute-start | bytes 196616 | tf_op jit(solution)/shard_map/ppermute | solution.py:33
  15.0 0.5 %cross_mine.1 = (f32[1,512,128]{2,1,0:T(8,128)S(1)}, f32[2,512]{1,0:T(2,128)S(1)}, bf16[3,1,128,128]{3,2,1,0:T(8,128)(2,1)S(1)}) custom-call(s32[1]{0:T(128)} %bitcast.position_ref.refs_0_, f32[2,512,128]{2,1,0:T(8,128)S(1)} %get-tuple-element.50.refs_1_, bf16[2,512,128]{2,1,0:T(8,128)(2,1)S(1)} %get-tuple-element.51.refs_2_.refs_3_.qd_ref, ...), custom_call_target="tpu_custom_call" | custom-call | flops 50331648 | bytes 1626116 | tf_op jit(solution)/shard_map/cross_mine/pallas_call | solution.py:73
  15.5 0.3 collective-permute-done.4.refs_7_
  15.8 0.2 collective-permute-done.5.refs_8_
  15.9 0.5 %cross_other.1 = (f32[1,512,128]{2,1,0:T(8,128)S(1)}, f32[2,512]{1,0:T(2,128)S(1)}, bf16[3,1,128,128]{3,2,1,0:T(8,128)(2,1)S(1)}) custom-call(s32[1]{0:T(128)} %bitcast.position_ref.refs_0_, f32[2,512,128]{2,1,0:T(8,128)S(1)} %get-tuple-element.50.refs_1_, bf16[2,512,128]{2,1,0:T(8,128)(2,1)S(1)} %get-tuple-element.51.refs_2_.refs_3_.qd_ref, ...), custom_call_target="tpu_custom_call" | custom-call | flops 50331648 | bytes 1630212 | tf_op jit(solution)/shard_map/cross_other/pallas_call | solution.py:73
  16.4 1.5 %collective-permute-start.6 = (f32[2,512]{1,0:T(2,128)S(1)}, f32[2,512]{1,0:T(2,128)S(1)}, u32[]{:S(2)}, u32[]{:S(2)}) collective-permute-start(f32[2,512]{1,0:T(2,128)S(1)} %get-tuple-element.61.refs_5_), channel_id=1, source_target_pairs={{0,8},{8,16},{16,24},{24,0},{1,9},{9,17},{17,25},{25,1},{2,10},{10... | collective-permute-start | bytes 12296 | tf_op jit(solution)/shard_map/ppermute | solution.py:55
  18.0 1.4 %collective-permute-start.7 = (f32[2,512]{1,0:T(2,128)S(1)}, f32[2,512]{1,0:T(2,128)S(1)}, u32[]{:S(2)}, u32[]{:S(2)}) collective-permute-start(f32[2,512]{1,0:T(2,128)S(1)} %get-tuple-element.61.refs_5_), channel_id=1, source_target_pairs={{0,24},{8,0},{16,8},{24,16},{1,25},{9,1},{17,9},{25,17},{2,26},{10... | collective-permute-start | bytes 12296 | tf_op jit(solution)/shard_map/ppermute | solution.py:55
  19.4 1.5 %collective-permute-start.8 = (f32[2,512]{1,0:T(2,128)S(1)}, f32[2,512]{1,0:T(2,128)S(1)}, u32[]{:S(2)}, u32[]{:S(2)}) collective-permute-start(f32[2,512]{1,0:T(2,128)S(1)} %get-tuple-element.61.refs_5_), channel_id=1, source_target_pairs={{0,16},{8,24},{16,0},{24,8},{1,17},{9,25},{17,1},{25,9},{2,18},{10... | collective-permute-start | bytes 12296 | tf_op jit(solution)/shard_map/ppermute | solution.py:55
  20.9 0.1 collective-permute-done.6.refs_6_
  21.0 0.6 %collective-permute-done.7.refs_7_ = f32[2,512]{1,0:T(2,128)S(1)} collective-permute-done((f32[2,512]{1,0:T(2,128)S(1)}, f32[2,512]{1,0:T(2,128)S(1)}, u32[]{:S(2)}, u32[]{:S(2)}) %collective-permute-start.7) | collective-permute-done | bytes 4128 | tf_op jit(solution)/shard_map/ppermute | solution.py:55
  21.6 1.4 %collective-permute-done.8.refs_8_ = f32[2,512]{1,0:T(2,128)S(1)} collective-permute-done((f32[2,512]{1,0:T(2,128)S(1)}, f32[2,512]{1,0:T(2,128)S(1)}, u32[]{:S(2)}, u32[]{:S(2)}) %collective-permute-start.8) | collective-permute-done | bytes 4128 | tf_op jit(solution)/shard_map/ppermute | solution.py:55
  23.0 0.6 %state_grads_other.1 = (bf16[1,512,128]{2,1,0:T(8,128)(2,1)S(1)}, f32[1,512]{1,0:T(1,128)S(1)}, f32[512,128]{1,0:T(8,128)S(1)}, f32[512,128]{1,0:T(8,128)S(1)}, f32[2,1,128,128]{3,2,1,0:T(8,128)S(1)}) custom-call(s32[1]{0:T(128)} %bitcast.position_ref.refs_0_, f32[1,512,128]{2,1,0:T(8,128)S(1)} %get-tuple-element.60.refs_1_.far_ref, ...), custom_call_target="tpu_custom_call" | custom-call | flops 50331648 | bytes 1118212 | tf_op jit(solution)/shard_map/state_grads_other/pallas_call | solution.py:73
  23.7 0.1 collective-permute-start.10
  23.7 0.7 %state_grads_mine.1 = (bf16[2,512,128]{2,1,0:T(8,128)(2,1)S(1)}, f32[1,128,128]{2,1,0:T(8,128)S(1)}, f32[1,128,128]{2,1,0:T(8,128)S(1)}, f32[2,1,128,128]{3,2,1,...) custom-call(s32[1]{0:T(128)} %bitcast.position_ref.refs_0_, ...), custom_call_target="tpu_custom_call" | custom-call | flops 50331648 | bytes 2215940 | tf_op jit(solution)/shard_map/state_grads_mine/pallas_call | solution.py:73
  24.4 0.7 %collective-permute-done.10.came_ref = f32[2,1,128,128]{3,2,1,0:T(8,128)S(1)} collective-permute-done((f32[2,1,128,128]{3,2,1,0:T(8,128)S(1)}, f32[2,1,128,128]{3,2,1,0:T(8,128)S(1)}, u32[]{:S(2)}, u32[]{:S(2)}) %collective-permute-start.10) | collective-permute-done | bytes 131104 | tf_op jit(solution)/shard_map/ppermute | solution.py:33
  25.1 2.5 %collective-permute-start.11 = (f32[1,128,128]{2,1,0:T(8,128)S(1)}, f32[1,128,128]{2,1,0:T(8,128)S(1)}, u32[]{:S(2)}, u32[]{:S(2)}) collective-permute-start(f32[1,128,128]{2,1,0:T(8,128)S(1)} %get-tuple-element.80), channel_id=1, source_target_pairs={{0,6},{1,7},{2,4},{3,5},{4,2},{5,3},{6,0},{7,1},{8,14},{9,15},{10,... | collective-permute-start | bytes 196616 | tf_op jit(solution)/shard_map/ppermute | solution.py:68
  27.7 0.0 collective-permute-start.12
  27.7 1.9 %collective-permute-start.13 = (f32[1,128,128]{2,1,0:T(8,128)S(1)}, f32[1,128,128]{2,1,0:T(8,128)S(1)}, u32[]{:S(2)}, u32[]{:S(2)}) collective-permute-start(f32[1,128,128]{2,1,0:T(8,128)S(1)} %get-tuple-element.82), channel_id=1, source_target_pairs={{0,4},{1,5},{2,6},{3,7},{4,0},{5,1},{6,2},{7,3},{8,12},{9,13},{10,... | collective-permute-start | bytes 196616 | tf_op jit(solution)/shard_map/ppermute | solution.py:68
  29.6 0.0 collective-permute-start.15
  29.6 0.5 %collective-permute-start.9 = (f32[1,128,128]{2,1,0:T(8,128)S(1)}, f32[1,128,128]{2,1,0:T(8,128)S(1)}, u32[]{:S(2)}, u32[]{:S(2)}) collective-permute-start(f32[1,128,128]{2,1,0:T(8,128)S(1)} %get-tuple-element.77), channel_id=1, source_target_pairs={{0,1},{1,0},{2,3},{3,2},{4,5},{5,4},{6,7},{7,6},{8,9},{9,8},{10,11... | collective-permute-start | bytes 196616 | tf_op jit(solution)/shard_map/ppermute | solution.py:33
  30.1 2.8 %local_backward.1 = (f32[1024,128]{1,0:T(8,128)}, f32[1024,128]{1,0:T(8,128)}, f32[2,512,128]{2,1,0:T(8,128)S(1)}, f32[2,512,128]{2,1,0:T(8,128)S(1)}) custom-call(bf16[2,512,128]{2,1,0:T(8,128)(2,1)S(1)} %get-tuple-element.67.ag_ref, bf16[2,512,128]{2,1,0:T(8,128)(2,1)S(1)} %get-tuple-element.51.refs_2_.refs_3_.qd_ref, ...), custom_call_target="tpu_custom_call" | custom-call | flops 536870912 | bytes 3398656 | tf_op jit(solution)/shard_map/local_backward/pallas_call | solution.py:73
  32.9 0.0 collective-permute-done.11
  32.9 1.2 %collective-permute-done.12 = f32[1,128,128]{2,1,0:T(8,128)S(1)} collective-permute-done((f32[1,128,128]{2,1,0:T(8,128)S(1)}, f32[1,128,128]{2,1,0:T(8,128)S(1)}, u32[]{:S(2)}, u32[]{:S(2)}) %collective-permute-start.12) | collective-permute-done | bytes 65568 | tf_op jit(solution)/shard_map/ppermute | solution.py:68
  34.1 0.0 collective-permute-done.13
  34.1 0.1 collective-permute-start.14
  34.2 0.0 collective-permute-done.15.refs_0_
  34.2 1.0 %key_value_mine.1 = (f32[512,2,128]{2,1,0:T(2,128)}, f32[512,2,128]{2,1,0:T(2,128)}) custom-call(s32[1]{0:T(128)} %bitcast.position_ref.refs_0_, f32[1,128,128]{2,1,0:T(8,128)S(1)} %collective-permute-done.15.refs_0_, f32[1,128,128]{2,1,0:T(8,128)S(1)} %add_add_fusion.refs_1_, bf16[2,512,128]{2,1,0:T(8,128)(2,1)S(1)} %get-tuple-element.68.kd_ref.refs_2_, ...), custom_call_target="tpu_custom_call" | custom-call | flops 33554432 | bytes 1703940 | tf_op jit(solution)/shard_map/key_value_mine/pallas_call | solution.py:73
  35.2 0.2 collective-permute-done.14.refs_1_
  35.4 1.0 %key_value_other.1 = (f32[512,2,128]{2,1,0:T(2,128)}, f32[512,2,128]{2,1,0:T(2,128)}) custom-call(s32[1]{0:T(128)} %bitcast.position_ref.refs_0_, f32[1,128,128]{2,1,0:T(8,128)S(1)} %collective-permute-done.9.refs_0_, f32[1,128,128]{2,1,0:T(8,128)S(1)} %collective-permute-done.14.refs_1_, ...), custom_call_target="tpu_custom_call", output_to_operand_aliasing={{0}: (7, {}), {1}: (8, {})} | custom-call | flops 33554432 | bytes 2752516 | tf_op jit(solution)/shard_map/key_value_other/pallas_call | solution.py:73
  (14 shorter events, 0.1 us)
Async XLA Ops:
  0.6 8.6 %copy-start.3 = (bf16[512,2,128]{2,1,0:T(2,128)(2,1)S(1)}, bf16[512,2,128]{2,1,0:T(2,128)(2,1)}, u32[]{:S(2)}) copy-start(bf16[512,2,128]{2,1,0:T(2,128)(2,1)} %param.13) | copy-start | bytes 786436
  2.0 1.5 %collective-permute-start = (f32[2,128,128]{2,1,0:T(8,128)S(1)}, f32[2,128,128]{2,1,0:T(8,128)S(1)}, u32[]{:S(2)}, u32[]{:S(2)}) collective-permute-start(f32[2,128,128]{2,1,0:T(8,128)S(1)} %fusion), channel_id=1, source_target_pairs={{0,1},{1,0},{2,3},{3,2},{4,5},{5,4},{6,7},{7,6},{8,9},{9,8},{10,11... | collective-permute-start | bytes 393224 | tf_op jit(solution)/shard_map/ppermute | solution.py:33
  3.5 5.7 %copy-start.5 = (f32[2,128]{1,0:T(2,128)S(1)}, f32[2,128]{1,0:T(2,128)}, u32[]{:S(2)}) copy-start(f32[2,128]{1,0:T(2,128)} %gain_ref.3) | copy-start | bytes 3076
  3.5 9.4 %collective-permute-start.1 = (f32[1,128,128]{2,1,0:T(8,128)S(1)}, f32[1,128,128]{2,1,0:T(8,128)S(1)}, u32[]{:S(2)}, u32[]{:S(2)}) collective-permute-start(f32[1,128,128]{2,1,0:T(8,128)S(1)} %dynamic-slice_add_fusion), channel_id=1, source_target_pairs={{0,6},{1,7},{2,4},{3,5},{4,2},{5,3},{6,0},{7,1},{8,14},{9,15},{10,... | collective-permute-start | bytes 196616 | tf_op jit(solution)/shard_map/ppermute | solution.py:68
  8.5 5.9 %collective-permute-start.2 = (f32[1,128,128]{2,1,0:T(8,128)S(1)}, f32[1,128,128]{2,1,0:T(8,128)S(1)}, u32[]{:S(2)}, u32[]{:S(2)}) collective-permute-start(f32[1,128,128]{2,1,0:T(8,128)S(1)} %dynamic-slice_add_fusion), channel_id=1, source_target_pairs={{0,4},{1,5},{2,6},{3,7},{4,0},{5,1},{6,2},{7,3},{8,12},{9,13},{10,... | collective-permute-start | bytes 196616 | tf_op jit(solution)/shard_map/ppermute | solution.py:68
  8.5 5.9 %collective-permute-start.3 = (f32[1,128,128]{2,1,0:T(8,128)S(1)}, f32[1,128,128]{2,1,0:T(8,128)S(1)}, u32[]{:S(2)}, u32[]{:S(2)}) collective-permute-start(f32[1,128,128]{2,1,0:T(8,128)S(1)} %dynamic-slice_add_fusion), channel_id=1, source_target_pairs={{0,2},{1,3},{2,0},{3,1},{4,6},{5,7},{6,4},{7,5},{8,10},{9,11},{10,... | collective-permute-start | bytes 196616 | tf_op jit(solution)/shard_map/ppermute | solution.py:68
  9.2 0.7 %copy-start.4 = (f32[8,2,13]{2,1,0:T(2,128)S(1)}, f32[8,2,13]{2,1,0:T(2,128)}, u32[]{:S(2)}) copy-start(f32[8,2,13]{2,1,0:T(2,128)} %table_ref.1) | copy-start | bytes 2500
  9.2 1.4 %copy-start.2 = (bf16[512,2,128]{2,1,0:T(2,128)(2,1)S(1)}, bf16[512,2,128]{2,1,0:T(2,128)(2,1)}, u32[]{:S(2)}) copy-start(bf16[512,2,128]{2,1,0:T(2,128)(2,1)} %param.7) | copy-start | bytes 786436
  9.3 0.7 %copy-start.6 = (s32[512]{0:T(512)S(1)}, s32[512]{0:T(512)}, u32[]{:S(2)}) copy-start(s32[512]{0:T(512)} %param.10) | copy-start | bytes 6148
  10.0 1.0 %copy-start = (bf16[512,2,128]{2,1,0:T(2,128)(2,1)S(1)}, bf16[512,2,128]{2,1,0:T(2,128)(2,1)}, u32[]{:S(2)}) copy-start(bf16[512,2,128]{2,1,0:T(2,128)(2,1)} %param.8) | copy-start | bytes 786436
  10.0 1.0 %copy-start.1 = (bf16[512,2,128]{2,1,0:T(2,128)(2,1)S(1)}, bf16[512,2,128]{2,1,0:T(2,128)(2,1)}, u32[]{:S(2)}) copy-start(bf16[512,2,128]{2,1,0:T(2,128)(2,1)} %param.9) | copy-start | bytes 786436
  14.5 1.3 %collective-permute-start.4 = (f32[1,128,128]{2,1,0:T(8,128)S(1)}, f32[1,128,128]{2,1,0:T(8,128)S(1)}, u32[]{:S(2)}, u32[]{:S(2)}) collective-permute-start(f32[1,128,128]{2,1,0:T(8,128)S(1)} %get-tuple-element.56.refs_6_), channel_id=1, source_target_pairs={{0,1},{1,0},{2,3},{3,2},{4,5},{5,4},{6,7},{7,6},{8,9},{9,8},{10,11... | collective-permute-start | bytes 196616 | tf_op jit(solution)/shard_map/ppermute | solution.py:33
  14.5 1.4 %collective-permute-start.5 = (f32[1,128,128]{2,1,0:T(8,128)S(1)}, f32[1,128,128]{2,1,0:T(8,128)S(1)}, u32[]{:S(2)}, u32[]{:S(2)}) collective-permute-start(f32[1,128,128]{2,1,0:T(8,128)S(1)} %get-tuple-element.57.refs_7_), channel_id=1, source_target_pairs={{0,1},{1,0},{2,3},{3,2},{4,5},{5,4},{6,7},{7,6},{8,9},{9,8},{10,11... | collective-permute-start | bytes 196616 | tf_op jit(solution)/shard_map/ppermute | solution.py:33
  16.4 4.6 %collective-permute-start.6 = (f32[2,512]{1,0:T(2,128)S(1)}, f32[2,512]{1,0:T(2,128)S(1)}, u32[]{:S(2)}, u32[]{:S(2)}) collective-permute-start(f32[2,512]{1,0:T(2,128)S(1)} %get-tuple-element.61.refs_5_), channel_id=1, source_target_pairs={{0,8},{8,16},{16,24},{24,0},{1,9},{9,17},{17,25},{25,1},{2,10},{10... | collective-permute-start | bytes 12296 | tf_op jit(solution)/shard_map/ppermute | solution.py:55
  18.0 3.6 %collective-permute-start.7 = (f32[2,512]{1,0:T(2,128)S(1)}, f32[2,512]{1,0:T(2,128)S(1)}, u32[]{:S(2)}, u32[]{:S(2)}) collective-permute-start(f32[2,512]{1,0:T(2,128)S(1)} %get-tuple-element.61.refs_5_), channel_id=1, source_target_pairs={{0,24},{8,0},{16,8},{24,16},{1,25},{9,1},{17,9},{25,17},{2,26},{10... | collective-permute-start | bytes 12296 | tf_op jit(solution)/shard_map/ppermute | solution.py:55
  19.4 3.6 %collective-permute-start.8 = (f32[2,512]{1,0:T(2,128)S(1)}, f32[2,512]{1,0:T(2,128)S(1)}, u32[]{:S(2)}, u32[]{:S(2)}) collective-permute-start(f32[2,512]{1,0:T(2,128)S(1)} %get-tuple-element.61.refs_5_), channel_id=1, source_target_pairs={{0,16},{8,24},{16,0},{24,8},{1,17},{9,25},{17,1},{25,9},{2,18},{10... | collective-permute-start | bytes 12296 | tf_op jit(solution)/shard_map/ppermute | solution.py:55
  23.7 1.4 %collective-permute-start.10 = (f32[2,1,128,128]{3,2,1,0:T(8,128)S(1)}, f32[2,1,128,128]{3,2,1,0:T(8,128)S(1)}, u32[]{:S(2)}, u32[]{:S(2)}) collective-permute-start(f32[2,1,128,128]{3,2,1,0:T(8,128)S(1)} %get-tuple-element.79), channel_id=1, source_target_pairs={{0,1},{1,0},{2,3},{3,2},{4,5},{5,4},{6,7},{7,6},{8,9},{9,8},{10,11... | collective-permute-start | bytes 393224 | tf_op jit(solution)/shard_map/ppermute | solution.py:33
  25.1 7.7 %collective-permute-start.11 = (f32[1,128,128]{2,1,0:T(8,128)S(1)}, f32[1,128,128]{2,1,0:T(8,128)S(1)}, u32[]{:S(2)}, u32[]{:S(2)}) collective-permute-start(f32[1,128,128]{2,1,0:T(8,128)S(1)} %get-tuple-element.80), channel_id=1, source_target_pairs={{0,6},{1,7},{2,4},{3,5},{4,2},{5,3},{6,0},{7,1},{8,14},{9,15},{10,... | collective-permute-start | bytes 196616 | tf_op jit(solution)/shard_map/ppermute | solution.py:68
  27.7 6.4 %collective-permute-start.12 = (f32[1,128,128]{2,1,0:T(8,128)S(1)}, f32[1,128,128]{2,1,0:T(8,128)S(1)}, u32[]{:S(2)}, u32[]{:S(2)}) collective-permute-start(f32[1,128,128]{2,1,0:T(8,128)S(1)} %get-tuple-element.81), channel_id=1, source_target_pairs={{0,2},{1,3},{2,0},{3,1},{4,6},{5,7},{6,4},{7,5},{8,10},{9,11},{10,... | collective-permute-start | bytes 196616 | tf_op jit(solution)/shard_map/ppermute | solution.py:68
  27.7 6.4 %collective-permute-start.13 = (f32[1,128,128]{2,1,0:T(8,128)S(1)}, f32[1,128,128]{2,1,0:T(8,128)S(1)}, u32[]{:S(2)}, u32[]{:S(2)}) collective-permute-start(f32[1,128,128]{2,1,0:T(8,128)S(1)} %get-tuple-element.82), channel_id=1, source_target_pairs={{0,4},{1,5},{2,6},{3,7},{4,0},{5,1},{6,2},{7,3},{8,12},{9,13},{10,... | collective-permute-start | bytes 196616 | tf_op jit(solution)/shard_map/ppermute | solution.py:68
  29.6 4.6 %collective-permute-start.15 = (f32[1,128,128]{2,1,0:T(8,128)S(1)}, f32[1,128,128]{2,1,0:T(8,128)S(1)}, u32[]{:S(2)}, u32[]{:S(2)}) collective-permute-start(f32[1,128,128]{2,1,0:T(8,128)S(1)} %get-tuple-element.89), channel_id=1, source_target_pairs={{0,1},{1,0},{2,3},{3,2},{4,5},{5,4},{6,7},{7,6},{8,9},{9,8},{10,11... | collective-permute-start | bytes 196616 | tf_op jit(solution)/shard_map/ppermute | solution.py:33
  29.6 5.6 %collective-permute-start.9 = (f32[1,128,128]{2,1,0:T(8,128)S(1)}, f32[1,128,128]{2,1,0:T(8,128)S(1)}, u32[]{:S(2)}, u32[]{:S(2)}) collective-permute-start(f32[1,128,128]{2,1,0:T(8,128)S(1)} %get-tuple-element.77), channel_id=1, source_target_pairs={{0,1},{1,0},{2,3},{3,2},{4,5},{5,4},{6,7},{7,6},{8,9},{9,8},{10,11... | collective-permute-start | bytes 196616 | tf_op jit(solution)/shard_map/ppermute | solution.py:33
  34.1 1.3 %collective-permute-start.14 = (f32[1,128,128]{2,1,0:T(8,128)S(1)}, f32[1,128,128]{2,1,0:T(8,128)S(1)}, u32[]{:S(2)}, u32[]{:S(2)}) collective-permute-start(f32[1,128,128]{2,1,0:T(8,128)S(1)} %add_add_fusion.refs_1_), channel_id=1, source_target_pairs={{0,1},{1,0},{2,3},{3,2},{4,5},{5,4},{6,7},{7,6},{8,9},{9,8},{10,11... | collective-permute-start | bytes 196616 | tf_op jit(solution)/shard_map/ppermute | solution.py:33
